TPU v7x, 128 devices: a whole 4x4x4 slice. The times are simulated.
128 devices in a mesh: expert: 16 (over x, y_hi, core), dp: 8 (over z, y_lo).
Axes of the slice: x: 4, y: 4 (y_hi: 2, y_lo: 2; y = y_hi * 2 + y_lo), z: 4, core: 2. Of those that a mesh axis runs over, the one named last changes fastest.
Arguments:
- tokens: bfloat16 [16384, 4096], P(('expert', 'dp')), may hold values from -6 to 6
- cotangent: bfloat16 [16384, 4096], P(('expert', 'dp')), may hold values from -6 to 6
- expert_ids: int32 [16384, 2], P(('expert', 'dp')), may hold values from 0 to 15, all different within a row; in each aligned block of 128 rows (0 to 127, 128 to 255, ...) at most 32 rows name the same one
- router_w: bfloat16 [4096, 16], replicated, may hold values from -0.09375 to 0.09375
- w_gate: bfloat16 [16, 4096, 768], P('expert'), may hold values from -0.09375 to 0.09375
- w_up: bfloat16 [16, 4096, 768], P('expert'), may hold values from -0.09375 to 0.09375
- w_down: bfloat16 [16, 4096, 768], P('expert'), may hold values from -0.21875 to 0.21875
Outputs:
- output: bfloat16 [16384, 4096], P(('expert', 'dp'))
- d_tokens: bfloat16 [16384, 4096], P(('expert', 'dp'))
- router_grad: float32 [4096, 16], replicated
- gate_grad: bfloat16 [16, 4096, 768], P('expert', 'dp')
- up_grad: bfloat16 [16, 4096, 768], P('expert', 'dp')
- down_grad: bfloat16 [16, 4096, 768], P('expert', 'dp')
Inputs may be any that keep to these rules, and one draw needn't show every extreme that they name: `expert_ids`: each row names 2 different experts. Within each aligned block of 128 rows (the tokens of one device) no expert is named more than 32 times, a bound that some block reaches.
All inputs are finite; a program needn't handle non-finite values.
Results may differ from a plain program's by a relative error of at most 0.014.
Values may be sent and summed in bfloat16 or wider, within the bound.
A program may use at most 192 MiB of HBM per device.

v0:
```python
import jax
import jax.numpy as jnp
from jax import lax
from jax.sharding import PartitionSpec as P


def slot_positions(expert_ids, expert_count, capacity):
    row_count, top_count = expert_ids.shape
    flat_ids = expert_ids.reshape(row_count * top_count)
    onehot = (flat_ids[:, None] == jnp.arange(expert_count, dtype=jnp.int32)[None, :]).astype(
        jnp.int32
    )
    before = jnp.cumsum(onehot, axis=0) - onehot
    rank_in = jnp.sum(before * onehot, axis=1)
    return flat_ids * capacity + rank_in


def owner_table(flat_slots, slot_count):
    entry_count = flat_slots.shape[0]
    owners = jnp.full((slot_count,), entry_count, dtype=jnp.int32)
    return owners.at[flat_slots].set(jnp.arange(entry_count, dtype=jnp.int32))


def padded_rows(values, row_index):
    zero_row = jnp.zeros((1, values.shape[1]), values.dtype)
    return jnp.concatenate([values, zero_row], axis=0)[row_index]


def expert_forward(source_rows, expert_weights):
    gate_w, up_w, down_w = expert_weights
    gate_pre = jnp.einsum("...d,dh->...h", source_rows, gate_w, preferred_element_type=jnp.float32)
    up_pre = jnp.einsum("...d,dh->...h", source_rows, up_w, preferred_element_type=jnp.float32)
    hidden = (jax.nn.silu(gate_pre) * up_pre).astype(jnp.bfloat16)
    expert_out = jnp.einsum(
        "...h,dh->...d", hidden, down_w, preferred_element_type=jnp.float32
    ).astype(jnp.bfloat16)
    return (expert_out, hidden, gate_pre, up_pre)


def expert_backward(grad_rows, gate_pre, up_pre, expert_weights):
    gate_w, up_w, down_w = expert_weights
    grad_hidden = jnp.einsum("...d,dh->...h", grad_rows, down_w, preferred_element_type=jnp.float32)
    sigmoid_gate = jax.nn.sigmoid(gate_pre)
    grad_gate = (
        grad_hidden * up_pre * sigmoid_gate * (1.0 + gate_pre * (1.0 - sigmoid_gate))
    ).astype(jnp.bfloat16)
    grad_up = (grad_hidden * jax.nn.silu(gate_pre)).astype(jnp.bfloat16)
    grad_in = jnp.einsum("...h,dh->...d", grad_gate, gate_w, preferred_element_type=jnp.float32)
    grad_in = grad_in + jnp.einsum(
        "...h,dh->...d", grad_up, up_w, preferred_element_type=jnp.float32
    )
    return (grad_in.astype(jnp.bfloat16), grad_gate, grad_up)


def on_device(tokens, cotangent, expert_ids, router_w, w_gate, w_up, w_down):
    row_count, top_count = expert_ids.shape
    feature_count = tokens.shape[1]
    expert_count = lax.axis_size("expert")
    replica_count = lax.axis_size("dp")
    capacity = 2 * row_count * top_count // expert_count
    slot_count = expert_count * capacity
    expert_weights = (w_gate[0], w_up[0], w_down[0])
    logits = jnp.dot(tokens, router_w, preferred_element_type=jnp.float32)
    chosen = jnp.take_along_axis(logits, expert_ids, axis=1)
    route_probs = jax.nn.sigmoid(2.0 * chosen - jnp.sum(chosen, axis=1, keepdims=True))
    flat_slots = slot_positions(expert_ids, expert_count, capacity)
    owners = owner_table(flat_slots, slot_count)
    outbound = padded_rows(tokens, owners // top_count).reshape(
        expert_count, capacity, feature_count
    )
    received = lax.all_to_all(outbound, "expert", split_axis=0, concat_axis=0, tiled=True)
    expert_out, hidden, gate_pre, up_pre = expert_forward(received, expert_weights)
    received, expert_out, hidden, gate_pre, up_pre = (
        received,
        expert_out,
        hidden,
        gate_pre,
        up_pre,
    )
    returned = lax.all_to_all(
        expert_out, "expert", split_axis=0, concat_axis=0, tiled=True
    ).reshape(slot_count, feature_count)
    routed = returned[flat_slots].reshape(row_count, top_count, feature_count)
    output = jnp.sum(route_probs[:, :, None] * routed.astype(jnp.float32), axis=1).astype(
        jnp.bfloat16
    )
    grad_prob = jnp.einsum("td,tkd->tk", cotangent, routed, preferred_element_type=jnp.float32)
    mixed = jnp.sum(route_probs * grad_prob, axis=1, keepdims=True)
    grad_chosen = route_probs * (grad_prob - mixed)
    columns = jnp.arange(router_w.shape[1], dtype=jnp.int32)
    match = (expert_ids[:, :, None] == columns[None, None, :]).astype(jnp.float32)
    grad_logits = jnp.sum(grad_chosen[:, :, None] * match, axis=1).astype(jnp.bfloat16)
    router_part = jnp.dot(tokens.T, grad_logits, preferred_element_type=jnp.float32)
    router_grad = lax.psum(router_part, ("expert", "dp")) / replica_count
    weighted = (route_probs[:, :, None] * cotangent[:, None, :].astype(jnp.float32)).astype(
        jnp.bfloat16
    )
    weighted = weighted.reshape(row_count * top_count, feature_count)
    grad_out = padded_rows(weighted, owners).reshape(expert_count, capacity, feature_count)
    grad_recv = lax.all_to_all(grad_out, "expert", split_axis=0, concat_axis=0, tiled=True)
    grad_in, grad_gate, grad_up = expert_backward(grad_recv, gate_pre, up_pre, expert_weights)
    grad_back = lax.all_to_all(grad_in, "expert", split_axis=0, concat_axis=0, tiled=True).reshape(
        slot_count, feature_count
    )
    grad_tokens = jnp.sum(
        grad_back[flat_slots].reshape(row_count, top_count, feature_count).astype(jnp.float32),
        axis=1,
    )
    grad_tokens = grad_tokens + jnp.dot(grad_logits, router_w.T, preferred_element_type=jnp.float32)
    d_tokens = grad_tokens.astype(jnp.bfloat16)
    gate_part = jnp.einsum("nkd,nkh->dh", received, grad_gate, preferred_element_type=jnp.float32)
    up_part = jnp.einsum("nkd,nkh->dh", received, grad_up, preferred_element_type=jnp.float32)
    down_part = jnp.einsum("nkd,nkh->dh", grad_recv, hidden, preferred_element_type=jnp.float32)
    gate_total, up_total, down_total = (
        lax.psum_scatter(
            gate_part.astype(jnp.bfloat16), "dp", scatter_dimension=0, tiled=True
        ).astype(jnp.float32),
        lax.psum_scatter(
            up_part.astype(jnp.bfloat16), "dp", scatter_dimension=0, tiled=True
        ).astype(jnp.float32),
        lax.psum_scatter(
            down_part.astype(jnp.bfloat16), "dp", scatter_dimension=0, tiled=True
        ).astype(jnp.float32),
    )
    gate_grad = (gate_total / replica_count).astype(jnp.bfloat16)[None]
    up_grad = (up_total / replica_count).astype(jnp.bfloat16)[None]
    down_grad = (down_total / replica_count).astype(jnp.bfloat16)[None]
    return (output, d_tokens, router_grad, gate_grad, up_grad, down_grad)


def solution(mesh):
    placed = (
        P(("expert", "dp"), None),
        P(("expert", "dp"), None),
        P(("expert", "dp"), None),
        P(),
        P("expert", None, None),
        P("expert", None, None),
        P("expert", None, None),
    )
    return jax.shard_map(
        on_device,
        mesh=mesh,
        in_specs=placed,
        out_specs=(
            P(("expert", "dp"), None),
            P(("expert", "dp"), None),
            P(),
            P("expert", "dp", None),
            P("expert", "dp", None),
            P("expert", "dp", None),
        ),
        check_vma=False,
    )
```

profile of v0, /device:TPU:4, one launch (start us, length us, event | category | flops | bytes accessed | tf_op | source)
XLA Modules:
  0.0 724.9 jit_solution(3862800200507733260)
XLA Ops:
  8.0 0.7 broadcast_multiply_fusion.1
  8.7 0.8 copy.40
  9.5 0.1 eq.42
  9.7 0.1 eq.38
  9.8 0.1 copy.39
  9.9 0.1 mul.95
  10.1 0.6 reduce-window.6
  10.7 0.2 slice_reduce_fusion
  10.9 0.1 fusion.26
  11.0 1.4 scatter_custom_fusion
  12.4 1.3 concatenate.6
  13.8 4.4 gather_fusion
  18.1 56.9 %all_to_all.20 = bf16[16,32,4096]{2,1,0:T(8,128)(2,1)S(1)} all-to-all(bf16[16,32,4096]{2,1,0:T(8,128)(2,1)} %bitcast.98), channel_id=1, replica_groups=mesh['expert'=16,'dp'=8] {'expert'}, dimensions={0} | all-to-all | bytes 8388608 | tf_op jit(solution)/shard_map/all_to_all | solution.py:71
  75.0 7.1 fusion.10
  82.2 4.6 multiply_convert_fusion.6
  86.8 0.9 copy-done.9
  87.6 5.1 fusion.12
  92.8 7.4 %all-to-all-start.1 = ((bf16[16,32,4096]{2,1,0:T(8,128)(2,1)}), bf16[16,32,4096]{2,1,0:T(8,128)(2,1)}, u32[]{:S(2)}, u32[]{:S(2)}) async-start(bf16[16,32,4096]{2,1,0:T(8,128)(2,1)} %fusion.12), calls=%async_computation.1 | async-start | bytes 8388608 | tf_op jit(solution)/shard_map/all_to_all | solution.py:80
  100.2 0.1 copy.36
  100.4 0.1 reshape.151
  100.5 0.4 fusion.37
  100.9 2.0 gather_fusion.4
  102.9 0.1 reshape.154
  103.0 0.1 copy.37
  103.1 4.1 mul.102
  107.2 6.1 mul.103
  113.3 41.2 %all-to-all-done.1 = bf16[16,32,4096]{2,1,0:T(8,128)(2,1)} async-done(((bf16[16,32,4096]{2,1,0:T(8,128)(2,1)}), bf16[16,32,4096]{2,1,0:T(8,128)(2,1)}, u32[]{:S(2)}, u32[]{:S(2)}) %all-to-all-start.1) | async-done | bytes 4194336 | tf_op jit(solution)/shard_map/all_to_all | solution.py:80
  154.4 6.6 gather_fusion.1
  161.0 2.7 reshape.115
  163.7 7.3 %fusion.18 = f32[128,1,2]{2,1,0:T(1,128)S(1)} fusion(bf16[128,2,4096]{2,1,0:T(2,128)(2,1)} %reshape.115, bf16[128,4096,1]{1,0,2:T(8,128)(2,1)} %bitcast.99), kind=kOutput, calls=%fused_computation.28 | convolution fusion | flops 2097152 | bytes 3146752 | tf_op jit(solution)/shard_map/td,tkd->tk/dot_general | solution.py:87
  171.0 0.1 copy.45
  171.2 0.1 copy.38
  171.3 0.1 mul.100
  171.4 2.6 multiply_convert_fusion
  174.1 0.3 concatenate.7
  174.3 16.0 %gather_fusion.2 = bf16[512,4096]{1,0:T(8,128)(2,1)} fusion(bf16[257,4096]{1,0:T(8,128)(2,1)S(1)} %concatenate.7, s32[1024]{0:T(1024)S(1)} %get-tuple-element.16), kind=kCustom, calls=%fused_computation.2 | custom fusion | bytes 8390656 | tf_op jit(solution)/shard_map/gather | solution.py:26
  190.4 10.8 %all-to-all-start.2 = ((bf16[16,32,4096]{2,1,0:T(8,128)(2,1)}), bf16[16,32,4096]{2,1,0:T(8,128)(2,1)}, u32[]{:S(2)}, u32[]{:S(2)}) async-start(bf16[16,32,4096]{2,1,0:T(8,128)(2,1)} %bitcast.97), calls=%async_computation.2 | async-start | bytes 8388608 | tf_op jit(solution)/shard_map/all_to_all | solution.py:100
  201.2 0.0 all-reduce.4.cloned.1.call-start
  201.3 1.0 convolution_bitcast_fusion
  202.3 0.0 reduce-scatter.8.cloned.1.call-start
  202.3 53.7 %all-to-all-done.2 = bf16[16,32,4096]{2,1,0:T(8,128)(2,1)} async-done(((bf16[16,32,4096]{2,1,0:T(8,128)(2,1)}), bf16[16,32,4096]{2,1,0:T(8,128)(2,1)}, u32[]{:S(2)}, u32[]{:S(2)}) %all-to-all-start.2) | async-done | bytes 4194336 | tf_op jit(solution)/shard_map/all_to_all | solution.py:100
  256.0 8.4 %bitcast_convert_fusion = bf16[4096,768]{1,0:T(8,128)(2,1)} fusion(bf16[16,32,4096]{2,1,0:T(8,128)(2,1)} %all-to-all-done.2, bf16[16,32,768]{2,1,0:T(8,128)(2,1)S(1)} %copy-done.10), kind=kOutput, calls=%fused_computation.6 | convolution fusion | flops 3224371200 | bytes 11272192 | tf_op jit(solution)/shard_map/nkd,nkh->dh/dot_general | solution.py:113
  264.4 0.0 reduce-scatter.8.cloned.1.call-update
  264.4 0.0 reduce-scatter.4.cloned.1.call-start
  264.5 8.8 %multiply_convert_fusion.5 = (bf16[16,32,768]{2,1,0:T(8,128)(2,1)S(1)}, bf16[16,32,768]{2,1,0:T(8,128)(2,1)S(1)}) fusion(f32[16,32,768]{2,1,0:T(8,128)} %copy-done.8, f32[16,32,768]{2,1,0:T(8,128)} %get-tuple-element.15, bf16[16,32,4096]{2,1,0:T(8,128)(2,1)} %all-to-all-done.2, bf16[1,4096,768]{2,1,0:T(8,128)(2,1)} %param.13), kind=kOutput, calls=%fused_computation.34 | convolution fusion | flops 3226337280 | bytes 15204352 | tf_op jit(solution)/shard_map/...d,dh->...h/dot_general | solution.py:42
  273.3 5.4 bitcast_convert_fusion.2
  278.7 0.0 reduce-scatter.4.cloned.1.call-update
  278.7 0.0 reduce-scatter.6.cloned.1.call-start
  278.8 8.3 %bitcast_convert_fusion.1 = bf16[4096,768]{1,0:T(8,128)(2,1)} fusion(bf16[16,32,4096]{2,1,0:T(8,128)(2,1)} %copy-done.3, bf16[16,32,768]{2,1,0:T(8,128)(2,1)S(1)} %get-tuple-element.11), kind=kOutput, calls=%fused_computation.7 | convolution fusion | flops 3224371200 | bytes 11272192 | tf_op jit(solution)/shard_map/nkd,nkh->dh/dot_general | solution.py:112
  287.1 0.0 reduce-scatter.6.cloned.1.call-update
  287.1 5.9 fusion.4
  293.1 5.2 add_convert_fusion
  298.2 12.8 %all-to-all-start.3 = ((bf16[16,32,4096]{2,1,0:T(8,128)(2,1)}), bf16[16,32,4096]{2,1,0:T(8,128)(2,1)}, u32[]{:S(2)}, u32[]{:S(2)}) async-start(bf16[16,32,4096]{2,1,0:T(8,128)(2,1)} %add_convert_fusion), calls=%async_computation.3 | async-start | bytes 8388608 | tf_op jit(solution)/shard_map/all_to_all | solution.py:102
  311.0 7.5 %multiply_reduce_fusion = bf16[128,4096]{1,0:T(8,128)(2,1)} fusion(bf16[128,2,4096]{2,1,0:T(2,128)(2,1)S(1)} %copy-done.2, f32[128,2]{1,0:T(8,128)S(1)} %copy.38), kind=kLoop, calls=%fused_computation.27 | loop fusion | flops 2621440 | bytes 3146752 | tf_op jit(solution)/shard_map/reduce_sum | solution.py:84
  318.5 258.5 %all-reduce.4.cloned.1.call-done = f32[4096,16]{0,1:T(8,128)} async-done(((f32[4096,16]{0,1:T(8,128)}), f32[4096,16]{0,1:T(8,128)}) %all-reduce.4.cloned.1.call-update) | async-done | bytes 262160 | tf_op jit(solution)/shard_map/psum | solution.py:94
  577.0 1.7 broadcast_multiply_fusion
  578.7 6.6 gather_fusion.3
  585.3 4.2 reshape.118
  589.5 7.5 %reduce_sum.60 = f32[128,4096]{1,0:T(8,128)S(1)} reduce(f32[128,2,4096]{2,1,0:T(2,128)} %reshape.118, f32[]{:T(128)} %constant.56.clone.1), dimensions={1}, to_apply=%region_6.7 | reduce | flops 524288 | bytes 6291460 | tf_op jit(solution)/shard_map/reduce_sum | solution.py:105
  597.0 1.4 fusion.17
  598.4 2.1 fusion.23
  600.6 2.2 fusion.21
  602.7 112.0 %reduce-scatter.6.cloned.1.call-done = bf16[512,768]{1,0:T(8,128)(2,1)} async-done(((bf16[4096,768]{1,0:T(8,128)(2,1)}), bf16[512,768]{1,0:T(8,128)(2,1)}) %reduce-scatter.6.cloned.1.call-update) | async-done | bytes 786448 | tf_op jit(solution)/shard_map/reduce_scatter | solution.py:118
  714.8 2.1 fusion.22
  (53 shorter events, 0.3 us)
Async XLA Ops:
  8.0 92.5 %copy-start = (bf16[4096,16]{0,1:T(8,128)(2,1)S(1)}, bf16[4096,16]{0,1:T(8,128)(2,1)}, u32[]{:S(2)}) copy-start(bf16[4096,16]{0,1:T(8,128)(2,1)} %param.10) | copy-start | bytes 393220
  18.1 64.0 %slice-start.2 = ((s8[6291456]{0:T(1024)(128)(4,1)}), s8[4194304]{0:T(1024)(128)(4,1)S(1)}, s32[]{:S(2)}) async-start(s8[6291456]{0:T(1024)(128)(4,1)} %bitcast.105), calls=%async_computation.13 | async-start | bytes 8388608
  75.0 7.1 copy-start.3
  75.0 7.1 slice-start.3
  75.0 12.6 %slice-start = ((s8[6291456]{0:T(1024)(128)(4,1)}), s8[4194304]{0:T(1024)(128)(4,1)S(1)}, s32[]{:S(2)}) async-start(s8[6291456]{0:T(1024)(128)(4,1)} %bitcast.103), calls=%async_computation.11 | async-start | bytes 8388608
  82.1 4.6 copy-start.8
  82.2 5.5 slice-start.1
  86.8 0.9 copy-start.9
  92.8 7.4 %copy-start.6 = (s32[128,2]{0,1:T(2,128)S(1)}, s32[128,2]{0,1:T(2,128)}, u32[]{:S(2)}) copy-start(s32[128,2]{0,1:T(2,128)} %param.9) | copy-start | bytes 3076
  92.8 7.7 %copy-start.1 = (bf16[128,4096]{1,0:T(8,128)(2,1)S(1)}, bf16[128,4096]{1,0:T(8,128)(2,1)}, u32[]{:S(2)}) copy-start(bf16[128,4096]{1,0:T(8,128)(2,1)} %param.7) | copy-start | bytes 3145732
  92.8 61.6 %all-to-all-start.1 = ((bf16[16,32,4096]{2,1,0:T(8,128)(2,1)}), bf16[16,32,4096]{2,1,0:T(8,128)(2,1)}, u32[]{:S(2)}, u32[]{:S(2)}) async-start(bf16[16,32,4096]{2,1,0:T(8,128)(2,1)} %fusion.12), calls=%async_computation.1 | async-start | bytes 8388608 | tf_op jit(solution)/shard_map/all_to_all | solution.py:80
  100.9 2.2 copy-start.5
  190.4 65.7 %copy-start.10 = (bf16[16,32,768]{2,1,0:T(8,128)(2,1)S(1)}, bf16[16,32,768]{2,1,0:T(8,128)(2,1)}, u32[]{:S(2)}) copy-start(bf16[16,32,768]{2,1,0:T(8,128)(2,1)} %copy-done.9) | copy-start | bytes 2359300
  190.4 65.7 %all-to-all-start.2 = ((bf16[16,32,4096]{2,1,0:T(8,128)(2,1)}), bf16[16,32,4096]{2,1,0:T(8,128)(2,1)}, u32[]{:S(2)}, u32[]{:S(2)}) async-start(bf16[16,32,4096]{2,1,0:T(8,128)(2,1)} %bitcast.97), calls=%async_computation.2 | async-start | bytes 8388608 | tf_op jit(solution)/shard_map/all_to_all | solution.py:100
  201.2 375.8 %all-reduce.4.cloned.1.call-start = ((), (), s32[]{:S(2)}) async-start(), calls=%async_computation.7 | async-start | bytes 524288 | tf_op jit(solution)/shard_map/psum | solution.py:94
  202.3 396.2 %reduce-scatter.8.cloned.1.call-start = ((), (), s32[]{:S(2)}) async-start(), calls=%async_computation.10 | async-start | bytes 7077888 | tf_op jit(solution)/shard_map/reduce_scatter | solution.py:121
  264.4 336.1 %reduce-scatter.4.cloned.1.call-start = ((), (), s32[]{:S(2)}) async-start(), calls=%async_computation.8 | async-start | bytes 7077888 | tf_op jit(solution)/shard_map/reduce_scatter | solution.py:115
  264.5 8.8 %copy-start.4 = (bf16[16,32,4096]{2,1,0:T(8,128)(2,1)S(1)}, bf16[16,32,4096]{2,1,0:T(8,128)(2,1)}, u32[]{:S(2)}) copy-start(bf16[16,32,4096]{2,1,0:T(8,128)(2,1)} %copy-done.3) | copy-start | bytes 12582916
  273.2 5.5 copy-start.7
  278.7 436.0 %reduce-scatter.6.cloned.1.call-start = ((), (), s32[]{:S(2)}) async-start(), calls=%async_computation.9 | async-start | bytes 7077888 | tf_op jit(solution)/shard_map/reduce_scatter | solution.py:118
  287.1 6.0 slice-start.4
  287.1 6.0 slice-start.5
  298.2 12.8 %copy-start.2 = (bf16[128,2,4096]{2,1,0:T(2,128)(2,1)S(1)}, bf16[128,2,4096]{2,1,0:T(2,128)(2,1)}, u32[]{:S(2)}) copy-start(bf16[128,2,4096]{2,1,0:T(2,128)(2,1)} %reshape.115) | copy-start | bytes 6291460
  298.2 280.4 %all-to-all-start.3 = ((bf16[16,32,4096]{2,1,0:T(8,128)(2,1)}), bf16[16,32,4096]{2,1,0:T(8,128)(2,1)}, u32[]{:S(2)}, u32[]{:S(2)}) async-start(bf16[16,32,4096]{2,1,0:T(8,128)(2,1)} %add_convert_fusion), calls=%async_computation.3 | async-start | bytes 8388608 | tf_op jit(solution)/shard_map/all_to_all | solution.py:102
Sparse Core Ops, SparseCore 0:
  207.3 369.5 all-reduce.3
Sparse Core Ops, SparseCore 1:
  264.5 183.5 reduce-scatter.7
  450.3 131.4 reduce-scatter.3
  584.1 130.6 reduce-scatter.5
where the time goes:
time: 733 us; the launch traced here: 725 us
  waiting for transfers between devices  465 us (63%)
  matrix products  68.8 us (9%)
  local copies, waits for them, and re-layouts  58.9 us (8%)
  blocking collectives  56.9 us (8%)
  starting transfers between devices  31.2 us (4%)
  other arithmetic  27.3 us (4%)
  between operations  16.5 us (2%)
    psum x1, waiting for transfers between devices, on_device(): router_grad = lax.psum(router_part, ('expert', 'dp')) / replica_count  258 us
    reduce_scatter x1, waiting for transfers between devices, on_device(): lax.psum_scatter(up_part.astype(jnp.bfloat16), 'dp', scatter_dimension=0,...  112 us
    all_to_all x1, blocking collectives, on_device(): lax.all_to_all(outbound, 'expert', split_axis=0, concat_axis=0, tiled=True)  56.9 us
    all_to_all x1, waiting for transfers between devices, on_device(): lax.all_to_all(grad_out, 'expert', split_axis=0, concat_axis=0, tiled=True)  53.7 us
    all_to_all x1, waiting for transfers between devices, on_device(): lax.all_to_all(expert_out, 'expert', split_axis=0, concat_axis=0, tiled=T...  41.2 us
    gather x2, local copies, waits for them, and re-layouts, padded_rows(): return jnp.concatenate([values, zero_row], axis=0)[row_index]  20.4 us
  transfers between devices with their start and end apart: 7, of which 4 were waited for; matrix products, arithmetic and copies ran while one was open for 12% of the time, Pallas kernels for 0%

commit v1 on v0

--- a/solution.py
+++ b/solution.py
@@ -68,18 +68,22 @@
     outbound = padded_rows(tokens, owners // top_count).reshape(
         expert_count, capacity, feature_count
     )
-    received = lax.all_to_all(outbound, "expert", split_axis=0, concat_axis=0, tiled=True)
+    weighted = (route_probs[:, :, None] * cotangent[:, None, :].astype(jnp.float32)).astype(
+        jnp.bfloat16
+    )
+    weighted = weighted.reshape(row_count * top_count, feature_count)
+    grad_out = padded_rows(weighted, owners).reshape(expert_count, capacity, feature_count)
+    sent = jnp.stack([outbound, grad_out], axis=1)
+    arrived = lax.all_to_all(sent, "expert", split_axis=0, concat_axis=0, tiled=True)
+    received = arrived[:, 0]
+    grad_recv = arrived[:, 1]
     expert_out, hidden, gate_pre, up_pre = expert_forward(received, expert_weights)
-    received, expert_out, hidden, gate_pre, up_pre = (
-        received,
-        expert_out,
-        hidden,
-        gate_pre,
-        up_pre,
+    grad_in, grad_gate, grad_up = expert_backward(grad_recv, gate_pre, up_pre, expert_weights)
+    back = lax.all_to_all(
+        jnp.stack([expert_out, grad_in], axis=1), "expert", split_axis=0, concat_axis=0, tiled=True
     )
-    returned = lax.all_to_all(
-        expert_out, "expert", split_axis=0, concat_axis=0, tiled=True
-    ).reshape(slot_count, feature_count)
+    returned = back[:, 0].reshape(slot_count, feature_count)
+    grad_back = back[:, 1].reshape(slot_count, feature_count)
     routed = returned[flat_slots].reshape(row_count, top_count, feature_count)
     output = jnp.sum(route_probs[:, :, None] * routed.astype(jnp.float32), axis=1).astype(
         jnp.bfloat16
@@ -92,16 +96,6 @@
     grad_logits = jnp.sum(grad_chosen[:, :, None] * match, axis=1).astype(jnp.bfloat16)
     router_part = jnp.dot(tokens.T, grad_logits, preferred_element_type=jnp.float32)
     router_grad = lax.psum(router_part, ("expert", "dp")) / replica_count
-    weighted = (route_probs[:, :, None] * cotangent[:, None, :].astype(jnp.float32)).astype(
-        jnp.bfloat16
-    )
-    weighted = weighted.reshape(row_count * top_count, feature_count)
-    grad_out = padded_rows(weighted, owners).reshape(expert_count, capacity, feature_count)
-    grad_recv = lax.all_to_all(grad_out, "expert", split_axis=0, concat_axis=0, tiled=True)
-    grad_in, grad_gate, grad_up = expert_backward(grad_recv, gate_pre, up_pre, expert_weights)
-    grad_back = lax.all_to_all(grad_in, "expert", split_axis=0, concat_axis=0, tiled=True).reshape(
-        slot_count, feature_count
-    )
     grad_tokens = jnp.sum(
         grad_back[flat_slots].reshape(row_count, top_count, feature_count).astype(jnp.float32),
         axis=1,

time: 733 us -> 783 us (1.068)
  blocking collectives: 56.9 us -> 102 us
  starting transfers between devices: 31.2 us -> 7.69 us
  waiting for transfers between devices: 465 us -> 480 us
  other arithmetic: 27.3 us -> 42 us
    reduce_scatter x1, waiting for transfers between devices: 112 us -> 0.01 us  [on_device(): lax.psum_scatter(up_part.astype(jnp.bfloat16), 'dp', scatter_dimension=0,...]
    psum x1, waiting for transfers between devices: 258 us -> 319 us  [on_device(): router_grad = lax.psum(router_part, ('expert', 'dp')) / replica_count]
    all_to_all x1, blocking collectives: 56.9 us -> 102 us  [on_device(): lax.all_to_all(sent, 'expert', split_axis=0, concat_axis=0, tiled=True)]
    reduce_scatter x1, waiting for transfers between devices: 0.01 us -> 41.3 us  [on_device(): lax.psum_scatter(gate_part.astype(jnp.bfloat16), 'dp', scatter_dimension=...]
    all_to_all x3 -> x1, waiting for transfers between devices: 94.9 us -> 120 us  [on_device(): lax.all_to_all(jnp.stack([expert_out, grad_in], axis=1), 'expert', split_...]
    all_to_all x3 -> x1, starting transfers between devices: 31 us -> 7.14 us  [on_device(): lax.all_to_all(jnp.stack([expert_out, grad_in], axis=1), 'expert', split_...]
    another operation x2 -> x4, other arithmetic: 0.63 us -> 14.4 us  [the longest x1 7.59 us: on_device(): sent = jnp.stack([outbound, grad_out], axis=1)]
    gather x2, local copies, waits for them, and re-layouts: 20.4 us -> 8.76 us  [padded_rows(): return jnp.concatenate([values, zero_row], axis=0)[row_index]]
  transfers between devices with their start and end apart: 7 -> 5, of which waited for: 4 -> 3; matrix products, arithmetic and copies ran while one was open for 12% -> 8% of each run, Pallas kernels for 0% -> 0%
where the time goes in v1:
time: 783 us; the launch traced here: 776 us
  waiting for transfers between devices  480 us (61%)
  blocking collectives  102 us (13%)
  matrix products  66 us (8%)
  local copies, waits for them, and re-layouts  61.3 us (8%)
  other arithmetic  42 us (5%)
  between operations  16.5 us (2%)
    psum x1, waiting for transfers between devices, on_device(): router_grad = lax.psum(router_part, ('expert', 'dp')) / replica_count  319 us
    all_to_all x1, waiting for transfers between devices, on_device(): lax.all_to_all(jnp.stack([expert_out, grad_in], axis=1), 'expert', split_...  120 us
    all_to_all x1, blocking collectives, on_device(): lax.all_to_all(sent, 'expert', split_axis=0, concat_axis=0, tiled=True)  102 us
    reduce_scatter x1, waiting for transfers between devices, on_device(): lax.psum_scatter(gate_part.astype(jnp.bfloat16), 'dp', scatter_dimension=...  41.3 us
  transfers between devices with their start and end apart: 5, of which 3 were waited for; matrix products, arithmetic and copies ran while one was open for 8% of the time, Pallas kernels for 0%

profile of v1, /device:TPU:4, one launch (start us, length us, event | category | flops | bytes accessed | tf_op | source)
XLA Modules:
  0.0 775.7 jit_solution(6980482226678451178)
XLA Ops:
  8.0 0.7 bitcast_or_fusion
  8.7 0.7 broadcast_multiply_fusion.1
  9.4 0.8 copy.60
  10.2 0.1 eq.42
  10.3 0.1 eq.38
  10.5 0.1 copy.59
  10.6 0.1 mul.95
  10.7 0.1 copy.56
  10.9 0.1 reshape.135
  11.0 1.6 fusion.44
  12.6 2.0 gather_fusion.4
  14.6 0.1 reshape.138
  14.7 0.1 copy.57
  14.9 0.1 copy.58
  15.0 0.1 mul.97
  15.1 0.6 reduce-window.6
  15.7 0.2 slice_reduce_fusion
  16.0 0.1 fusion.32
  16.1 1.4 scatter_custom_fusion
  17.5 0.1 concatenate.6
  17.6 4.1 mul.99
  21.7 6.1 mul.100
  27.8 2.6 multiply_convert_fusion
  30.4 0.3 concatenate.7
  30.7 4.4 gather_fusion
  35.1 4.4 gather_fusion.1
  39.5 7.6 pad_maximum_fusion
  47.1 102.0 %all_to_all.10 = bf16[16,2,32,4096]{3,2,1,0:T(8,128)(2,1)S(1)} all-to-all(bf16[16,2,32,4096]{3,2,1,0:T(8,128)(2,1)} %pad_maximum_fusion), channel_id=1, replica_groups=mesh['expert'=16,'dp'=8] {'expert'}, dimensions={0} | all-to-all | bytes 16777216 | tf_op jit(solution)/shard_map/all_to_all | solution.py:77
  149.1 3.5 fusion.10
  152.6 3.4 fusion
  156.1 3.9 multiply_convert_fusion.6
  160.1 3.7 fusion.17
  163.8 5.7 fusion.4
  169.5 9.6 %fusion.20 = bf16[16,1,32,4096]{3,2,0,1:T(8,128)(2,1)} fusion(f32[16,32,4096]{2,1,0:T(8,128)} %fusion.4, bf16[16,32,768]{2,1,0:T(8,128)(2,1)S(1)} %get-tuple-element.11, bf16[1,4096,768]{2,1,0:T(8,128)(2,1)} %param.11), kind=kOutput, calls=%fused_computation.26 | convolution fusion | flops 3225419776 | bytes 19660800 | tf_op jit(solution)/shard_map/...h,dh->...d/dot_general | solution.py:48
  179.1 6.2 pad_maximum_fusion.1
  185.3 7.7 copy.68
  193.0 7.1 all-to-all-start.1
  200.2 119.6 %all-to-all-done.1 = bf16[16,2,32,4096]{3,2,1,0:T(8,128)(2,1)} async-done(((bf16[16,2,32,4096]{3,2,1,0:T(8,128)(2,1)}), bf16[16,2,32,4096]{3,2,1,0:T(8,128)(2,1)}, u32[]{:S(2)}, u32[]{:S(2)}) %all-to-all-start.1) | async-done | bytes 8388640 | tf_op jit(solution)/shard_map/all_to_all | solution.py:82
  319.8 6.0 fusion.43
  325.8 6.6 gather_fusion.2
  332.4 2.7 reshape.101
  335.1 7.2 fusion.24
  342.3 0.1 copy.70
  342.5 1.0 convolution_bitcast_fusion
  343.4 0.2 reduce-scatter.8.cloned.1.call-start
  343.7 8.3 %bitcast_convert_fusion = bf16[4096,768]{1,0:T(8,128)(2,1)} fusion(bf16[16,32,768]{2,1,0:T(8,128)(2,1)S(1)} %copy-done.15, bf16[16,2,32,4096]{3,2,1,0:T(8,128)(2,1)} %copy-done.3), kind=kOutput, calls=%fused_computation.6 | convolution fusion | flops 3224371200 | bytes 11272192 | tf_op jit(solution)/shard_map/nkd,nkh->dh/dot_general | solution.py:107
  352.0 0.0 reduce-scatter.6.cloned.1.call-start
  352.1 1.1 copy-done.13
  353.1 8.2 %bitcast_convert_fusion.1 = bf16[4096,768]{1,0:T(8,128)(2,1)} fusion(bf16[16,32,768]{2,1,0:T(8,128)(2,1)S(1)} %copy-done.13, bf16[16,2,32,4096]{3,2,1,0:T(8,128)(2,1)} %copy-done.3), kind=kOutput, calls=%fused_computation.7 | convolution fusion | flops 3224371200 | bytes 11272192 | tf_op jit(solution)/shard_map/nkd,nkh->dh/dot_general | solution.py:106
  361.4 0.3 reduce-scatter.4.cloned.1.call-start
  361.7 0.8 copy-done.11
  362.5 8.4 %bitcast_convert_fusion.2 = bf16[4096,768]{1,0:T(8,128)(2,1)} fusion(bf16[16,32,768]{2,1,0:T(8,128)(2,1)S(1)} %copy-done.11, bf16[16,2,32,4096]{3,2,1,0:T(8,128)(2,1)} %copy-done.3), kind=kOutput, calls=%fused_computation.8 | convolution fusion | flops 3224371200 | bytes 11272192 | tf_op jit(solution)/shard_map/nkd,nkh->dh/dot_general | solution.py:105
  370.9 6.6 gather_fusion.3
  377.5 4.2 reshape.102
  381.8 7.5 reduce_sum.60
  389.3 1.4 fusion.23
  390.7 0.5 copy-done.4
  391.3 7.8 %multiply_reduce_fusion = bf16[128,4096]{1,0:T(8,128)(2,1)} fusion(bf16[128,2,4096]{2,1,0:T(2,128)(2,1)S(1)} %copy-done.4, f32[128,2]{1,0:T(8,128)S(1)} %copy-done.8), kind=kLoop, calls=%fused_computation.32 | loop fusion | flops 2621440 | bytes 3146752 | tf_op jit(solution)/shard_map/reduce_sum | solution.py:88
  399.0 319.2 %all-reduce.4.cloned.1.call-done = f32[4096,16]{0,1:T(8,128)} async-done(((f32[4096,16]{0,1:T(8,128)}), f32[4096,16]{0,1:T(8,128)}) %all-reduce.4.cloned.1.call-update) | async-done | bytes 262160 | tf_op jit(solution)/shard_map/psum | solution.py:98
  718.3 1.7 broadcast_multiply_fusion
  720.0 2.1 fusion.29
  722.1 2.1 fusion.28
  724.2 41.3 %reduce-scatter.4.cloned.1.call-done = bf16[512,768]{1,0:T(8,128)(2,1)} async-done(((bf16[4096,768]{1,0:T(8,128)(2,1)}), bf16[512,768]{1,0:T(8,128)(2,1)}) %reduce-scatter.4.cloned.1.call-update) | async-done | bytes 786448 | tf_op jit(solution)/shard_map/reduce_scatter | solution.py:109
  765.5 2.1 fusion.27
  (64 shorter events, 0.4 us)
Async XLA Ops:
  8.0 3.0 copy-start
  12.6 2.2 copy-start.9
  12.6 4.9 copy-start.1
  12.6 5.0 copy-start.5
  15.0 2.5 copy-start.7
  39.5 109.6 %slice-start.4 = ((s8[6291456]{0:T(1024)(128)(4,1)}), s8[2097152]{0:T(1024)(128)(4,1)S(1)}, s32[]{:S(2)}) async-start(s8[6291456]{0:T(1024)(128)(4,1)} %bitcast.129), calls=%async_computation.13 | async-start | bytes 4194304
  47.1 102.0 %slice-start.5 = ((s8[6291456]{0:T(1024)(128)(4,1)}), s8[4194304]{0:T(1024)(128)(4,1)S(1)}, s32[]{:S(2)}) async-start(s8[6291456]{0:T(1024)(128)(4,1)} %bitcast.129), calls=%async_computation.14 | async-start | bytes 8388608
  47.1 105.5 %slice-start = ((s8[6291456]{0:T(1024)(128)(4,1)}), s8[4194304]{0:T(1024)(128)(4,1)S(1)}, s32[]{:S(2)}) async-start(s8[6291456]{0:T(1024)(128)(4,1)} %bitcast.125), calls=%async_computation.9 | async-start | bytes 8388608
  47.1 109.0 %slice-start.2 = ((s8[6291456]{0:T(1024)(128)(4,1)}), s8[4194304]{0:T(1024)(128)(4,1)S(1)}, s32[]{:S(2)}) async-start(s8[6291456]{0:T(1024)(128)(4,1)} %bitcast.127), calls=%async_computation.11 | async-start | bytes 8388608
  149.1 7.0 copy-start.3
  149.1 3.5 slice-start.1
  149.1 7.0 slice-start.3
  160.0 3.7 copy-start.14
  160.1 3.7 copy-start.12
  160.1 9.5 %copy-start.10 = (bf16[16,32,768]{2,1,0:T(8,128)(2,1)}, bf16[16,32,768]{2,1,0:T(8,128)(2,1)S(1)}, u32[]{:S(2)}) copy-start(bf16[16,32,768]{2,1,0:T(8,128)(2,1)S(1)} %get-tuple-element.11) | copy-start | bytes 2359300
  193.0 126.8 %all-to-all-start.1 = ((bf16[16,2,32,4096]{3,2,1,0:T(8,128)(2,1)}), bf16[16,2,32,4096]{3,2,1,0:T(8,128)(2,1)}, u32[]{:S(2)}, u32[]{:S(2)}) async-start(bf16[16,2,32,4096]{3,2,1,0:T(8,128)(2,1)} %copy.68), calls=%async_computation.1 | async-start | bytes 16777216 | tf_op jit(solution)/shard_map/all_to_all | solution.py:82
  200.1 518.1 %all-reduce.4.cloned.1.call-start = ((), (), s32[]{:S(2)}) async-start(), calls=%async_computation.5 | async-start | bytes 524288 | tf_op jit(solution)/shard_map/psum | solution.py:98
  332.4 2.7 copy-start.6
  335.1 7.4 copy-start.2
  335.1 8.6 %copy-start.15 = (bf16[16,32,768]{2,1,0:T(8,128)(2,1)S(1)}, bf16[16,32,768]{2,1,0:T(8,128)(2,1)}, u32[]{:S(2)}) copy-start(bf16[16,32,768]{2,1,0:T(8,128)(2,1)} %copy-done.14) | copy-start | bytes 2359300
  343.4 376.5 %reduce-scatter.8.cloned.1.call-start = ((), (), s32[]{:S(2)}) async-start(), calls=%async_computation.8 | async-start | bytes 7077888 | tf_op jit(solution)/shard_map/reduce_scatter | solution.py:115
  352.0 1.1 copy-start.13
  352.0 370.1 %reduce-scatter.6.cloned.1.call-start = ((), (), s32[]{:S(2)}) async-start(), calls=%async_computation.7 | async-start | bytes 7077888 | tf_op jit(solution)/shard_map/reduce_scatter | solution.py:112
  361.4 1.1 copy-start.11
  361.4 404.1 %reduce-scatter.4.cloned.1.call-start = ((), (), s32[]{:S(2)}) async-start(), calls=%async_computation.6 | async-start | bytes 7077888 | tf_op jit(solution)/shard_map/reduce_scatter | solution.py:109
  381.8 9.0 %copy-start.8 = (f32[128,2]{1,0:T(8,128)S(1)}, f32[128,2]{1,0:T(8,128)}, u32[]{:S(2)}) copy-start(f32[128,2]{1,0:T(8,128)} %copy-done.7) | copy-start | bytes 3076
  389.3 2.0 copy-start.4
Sparse Core Ops, SparseCore 0:
  343.6 374.6 all-reduce.3
Sparse Core Ops, SparseCore 1:
  352.1 146.3 reduce-scatter.7
  500.8 130.8 reduce-scatter.5
  633.9 131.5 reduce-scatter.3

commit v2 on v0

--- a/solution.py
+++ b/solution.py
@@ -52,6 +52,25 @@
     return (grad_in.astype(jnp.bfloat16), grad_gate, grad_up)
 
 
+def all_reduce_by_exchange(part, axes):
+    device_count = lax.axis_size(axes)
+    chunks = part.reshape(device_count, part.size // device_count)
+    mine = jnp.sum(lax.all_to_all(chunks, axes, 0, 0, tiled=True), axis=0, keepdims=True)
+    spread = jnp.broadcast_to(mine, chunks.shape)
+    return lax.all_to_all(spread, axes, 0, 0, tiled=True).reshape(part.shape)
+
+
+def reduce_scatter_by_exchange(parts, axis):
+    replica_count = lax.axis_size(axis)
+    rows = parts[0].shape[0] // replica_count
+    blocks = jnp.stack([p.astype(jnp.bfloat16) for p in parts], axis=1)
+    blocks = blocks.reshape((replica_count, rows) + blocks.shape[1:])
+    blocks = blocks.reshape(replica_count, rows, len(parts), parts[0].shape[1])
+    arrived = lax.all_to_all(blocks, axis, 0, 0, tiled=True)
+    total = jnp.sum(arrived.astype(jnp.float32), axis=0)
+    return tuple(total[:, i] for i in range(len(parts)))
+
+
 def on_device(tokens, cotangent, expert_ids, router_w, w_gate, w_up, w_down):
     row_count, top_count = expert_ids.shape
     feature_count = tokens.shape[1]
@@ -91,7 +110,7 @@
     match = (expert_ids[:, :, None] == columns[None, None, :]).astype(jnp.float32)
     grad_logits = jnp.sum(grad_chosen[:, :, None] * match, axis=1).astype(jnp.bfloat16)
     router_part = jnp.dot(tokens.T, grad_logits, preferred_element_type=jnp.float32)
-    router_grad = lax.psum(router_part, ("expert", "dp")) / replica_count
+    router_grad = all_reduce_by_exchange(router_part, ("expert", "dp")) / replica_count
     weighted = (route_probs[:, :, None] * cotangent[:, None, :].astype(jnp.float32)).astype(
         jnp.bfloat16
     )
@@ -111,16 +130,8 @@
     gate_part = jnp.einsum("nkd,nkh->dh", received, grad_gate, preferred_element_type=jnp.float32)
     up_part = jnp.einsum("nkd,nkh->dh", received, grad_up, preferred_element_type=jnp.float32)
     down_part = jnp.einsum("nkd,nkh->dh", grad_recv, hidden, preferred_element_type=jnp.float32)
-    gate_total, up_total, down_total = (
-        lax.psum_scatter(
-            gate_part.astype(jnp.bfloat16), "dp", scatter_dimension=0, tiled=True
-        ).astype(jnp.float32),
-        lax.psum_scatter(
-            up_part.astype(jnp.bfloat16), "dp", scatter_dimension=0, tiled=True
-        ).astype(jnp.float32),
-        lax.psum_scatter(
-            down_part.astype(jnp.bfloat16), "dp", scatter_dimension=0, tiled=True
-        ).astype(jnp.float32),
+    gate_total, up_total, down_total = reduce_scatter_by_exchange(
+        (gate_part, up_part, down_part), "dp"
     )
     gate_grad = (gate_total / replica_count).astype(jnp.bfloat16)[None]
     up_grad = (up_total / replica_count).astype(jnp.bfloat16)[None]

time: 733 us -> 603 us (0.82)
  the two profiles are of different devices: /device:TPU:4 before, /device:TPU:20 now
where the time goes in v2:
time: 603 us; the launch traced here: 595 us
  waiting for transfers between devices  321 us (53%)
  matrix products  66 us (11%)
  starting transfers between devices  59.8 us (10%)
  blocking collectives  54.5 us (9%)
  local copies, waits for them, and re-layouts  52.3 us (9%)
  other arithmetic  40.6 us (7%)
    all_to_all x1, waiting for transfers between devices, reduce_scatter_by_exchange(): arrived = lax.all_to_all(blocks, axis, 0, 0, tiled=True)  178 us
    all_to_all x1, waiting for transfers between devices, on_device(): lax.all_to_all(grad_out, 'expert', split_axis=0, concat_axis=0, tiled=True)  57.7 us
    all_to_all x1, blocking collectives, on_device(): lax.all_to_all(outbound, 'expert', split_axis=0, concat_axis=0, tiled=True)  54.5 us
    all_to_all x1, waiting for transfers between devices, on_device(): lax.all_to_all(expert_out, 'expert', split_axis=0, concat_axis=0, tiled=T...  44.5 us
    all_to_all x1, waiting for transfers between devices, on_device(): lax.all_to_all(grad_in, 'expert', split_axis=0, concat_axis=0, tiled=True)  40.9 us
    all_to_all x1, starting transfers between devices, all_reduce_by_exchange(): lax.all_to_all(chunks, axes, 0, 0, tiled=True)  16.9 us
  transfers between devices with their start and end apart: 6, of which 4 were waited for; matrix products, arithmetic and copies ran while one was open for 17% of the time, Pallas kernels for 0%

profile of v2, /device:TPU:20, one launch (start us, length us, event | category | flops | bytes accessed | tf_op | source)
XLA Modules:
  0.0 595.2 jit_solution(14647506740202349538)
XLA Ops:
  0.6 0.7 broadcast_multiply_fusion
  1.4 0.8 copy.64
  2.1 0.1 eq.38
  2.3 0.1 eq.42
  2.4 0.1 copy.63
  2.5 0.1 mul.95
  2.7 0.6 reduce-window.6
  3.3 0.2 slice_reduce_fusion
  3.5 0.1 fusion.29
  3.6 1.4 scatter_custom_fusion
  5.0 1.3 concatenate.7
  6.4 4.4 gather_fusion
  10.8 54.5 %all_to_all.41 = bf16[16,32,4096]{2,1,0:T(8,128)(2,1)S(1)} all-to-all(bf16[16,32,4096]{2,1,0:T(8,128)(2,1)} %bitcast.106), channel_id=1, replica_groups=mesh['expert'=16,'dp'=8] {'expert'}, dimensions={0} | all-to-all | bytes 8388608 | tf_op jit(solution)/shard_map/all_to_all | solution.py:90
  65.3 7.1 %fusion.10 = f32[16,32,768]{2,1,0:T(8,128)S(1)} fusion(bf16[16,32,4096]{2,1,0:T(8,128)(2,1)S(1)} %all_to_all.41, bf16[1,4096,768]{2,1,0:T(8,128)(2,1)} %param.11), kind=kOutput, calls=%fused_computation.22 | convolution fusion | flops 3221225472 | bytes 12058624 | tf_op jit(solution)/shard_map/...d,dh->...h/dot_general | solution.py:31
  72.4 4.6 multiply_convert_fusion.3
  77.0 5.1 fusion.12
  82.2 9.7 %all-to-all-start.1 = ((bf16[16,32,4096]{2,1,0:T(8,128)(2,1)}), bf16[16,32,4096]{2,1,0:T(8,128)(2,1)}, u32[]{:S(2)}, u32[]{:S(2)}) async-start(bf16[16,32,4096]{2,1,0:T(8,128)(2,1)} %fusion.12), calls=%async_computation.1 | async-start | bytes 8388608 | tf_op jit(solution)/shard_map/all_to_all | solution.py:99
  91.9 0.1 copy.60
  92.0 0.1 reshape.220
  92.2 0.4 fusion.40
  92.6 2.0 gather_fusion.4
  94.6 0.1 reshape.223
  94.8 4.2 mul.102
  98.9 6.1 %mul.103 = f32[256,4096]{1,0:T(8,128)} reshape(f32[128,2,4096]{2,1,0:T(2,128)} %mul.102) | data formatting | bytes 8388608 | tf_op jit(solution)/shard_map/mul | solution.py:114
  105.0 44.5 %all-to-all-done.1 = bf16[16,32,4096]{2,1,0:T(8,128)(2,1)} async-done(((bf16[16,32,4096]{2,1,0:T(8,128)(2,1)}), bf16[16,32,4096]{2,1,0:T(8,128)(2,1)}, u32[]{:S(2)}, u32[]{:S(2)}) %all-to-all-start.1) | async-done | bytes 4194336 | tf_op jit(solution)/shard_map/all_to_all | solution.py:99
  149.5 6.6 %gather_fusion.1 = bf16[256,4096]{1,0:T(8,128)(2,1)S(1)} fusion(bf16[512,4096]{1,0:T(8,128)(2,1)} %bitcast.11, s32[1024]{0:T(1024)S(1)} %pad_clamp_fusion.1), kind=kCustom, calls=%fused_computation.1 | custom fusion | bytes 4195328 | tf_op jit(solution)/shard_map/gather | solution.py:102
  156.2 2.7 reshape.184
  158.8 7.3 %fusion.18 = f32[128,1,2]{2,1,0:T(1,128)S(1)} fusion(bf16[128,2,4096]{2,1,0:T(2,128)(2,1)} %reshape.184, bf16[128,4096,1]{1,0,2:T(8,128)(2,1)} %bitcast.112), kind=kOutput, calls=%fused_computation.30 | convolution fusion | flops 2097152 | bytes 3146752 | tf_op jit(solution)/shard_map/td,tkd->tk/dot_general | solution.py:106
  166.3 0.1 copy.62
  166.4 0.1 mul.100
  166.6 0.3 convolution_bitcast_fusion
  166.8 0.6 copy.68
  167.4 1.5 all_to_all.33
  168.9 16.9 %all-to-all-start.4 = ((f32[128,1,512]{2,1,0:T(1,128)}), f32[128,1,512]{2,1,0:T(1,128)S(1)}, u32[]{:S(2)}, u32[]{:S(2)}) async-start(f32[128,1,512]{2,1,0:T(1,128)} %all_to_all.33), calls=%async_computation.4 | async-start | bytes 524288 | tf_op jit(solution)/shard_map/all_to_all | solution.py:58
  185.8 2.6 multiply_convert_fusion
  188.4 0.3 concatenate.8
  188.7 4.4 gather_fusion.2
  193.1 9.8 %all-to-all-start.2 = ((bf16[16,32,4096]{2,1,0:T(8,128)(2,1)}), bf16[16,32,4096]{2,1,0:T(8,128)(2,1)}, u32[]{:S(2)}, u32[]{:S(2)}) async-start(bf16[16,32,4096]{2,1,0:T(8,128)(2,1)} %bitcast.105), calls=%async_computation.2 | async-start | bytes 8388608 | tf_op jit(solution)/shard_map/all_to_all | solution.py:119
  202.9 0.2 reduce_sum.81
  203.1 57.7 %all-to-all-done.2 = bf16[16,32,4096]{2,1,0:T(8,128)(2,1)} async-done(((bf16[16,32,4096]{2,1,0:T(8,128)(2,1)}), bf16[16,32,4096]{2,1,0:T(8,128)(2,1)}, u32[]{:S(2)}, u32[]{:S(2)}) %all-to-all-start.2) | async-done | bytes 4194336 | tf_op jit(solution)/shard_map/all_to_all | solution.py:119
  260.8 0.8 broadcast_in_dim.16
  261.6 9.7 %all-to-all-start.5 = ((f32[128,1,512]{2,1,0:T(1,128)}), f32[128,1,512]{2,1,0:T(1,128)S(1)}, u32[]{:S(2)}, u32[]{:S(2)}) async-start(f32[128,1,512]{2,1,0:T(1,128)} %broadcast_in_dim.16), calls=%async_computation.5 | async-start | bytes 524288 | tf_op jit(solution)/shard_map/all_to_all | solution.py:60
  271.4 9.6 %multiply_convert_fusion.2 = (bf16[16,32,768]{2,1,0:T(8,128)(2,1)}, bf16[16,32,768]{2,1,0:T(8,128)(2,1)S(1)}) fusion(f32[16,32,768]{2,1,0:T(8,128)} %copy-done.14, f32[16,32,768]{2,1,0:T(8,128)} %get-tuple-element.42, bf16[16,32,4096]{2,1,0:T(8,128)(2,1)} %all-to-all-done.2, bf16[1,4096,768]{2,1,0:T(8,128)(2,1)} %param.13), kind=kOutput, calls=%fused_computation.39 | convolution fusion | flops 3226337280 | bytes 15204352 | tf_op jit(solution)/shard_map/...d,dh->...h/dot_general | solution.py:42
  281.0 0.9 copy-done.12
  281.9 5.7 fusion.4
  287.6 8.5 %bitcast_convert_fusion = bf16[4096,768]{1,0:T(8,128)(2,1)} fusion(bf16[16,32,4096]{2,1,0:T(8,128)(2,1)} %all-to-all-done.2, bf16[16,32,768]{2,1,0:T(8,128)(2,1)S(1)} %copy-done.16), kind=kOutput, calls=%fused_computation.8 | convolution fusion | flops 3224371200 | bytes 11272192 | tf_op jit(solution)/shard_map/nkd,nkh->dh/dot_general | solution.py:132
  296.2 6.3 %add_convert_fusion = bf16[16,32,4096]{2,1,0:T(8,128)(2,1)} fusion(f32[16,32,4096]{2,1,0:T(8,128)S(1)} %copy-done.10, bf16[16,32,768]{2,1,0:T(8,128)(2,1)} %get-tuple-element.37, bf16[1,4096,768]{2,1,0:T(8,128)(2,1)S(1)} %bitcast.123), kind=kOutput, calls=%fused_computation.11 | convolution fusion | flops 3225419776 | bytes 19660800 | tf_op jit(solution)/shard_map/...h,dh->...d/dot_general | solution.py:48
  302.5 7.4 %all-to-all-start.3 = ((bf16[16,32,4096]{2,1,0:T(8,128)(2,1)}), bf16[16,32,4096]{2,1,0:T(8,128)(2,1)}, u32[]{:S(2)}, u32[]{:S(2)}) async-start(bf16[16,32,4096]{2,1,0:T(8,128)(2,1)} %add_convert_fusion), calls=%async_computation.3 | async-start | bytes 8388608 | tf_op jit(solution)/shard_map/all_to_all | solution.py:121
  309.9 5.8 bitcast_convert_fusion.1
  315.8 3.8 bitcast_convert_fusion.2
  319.6 8.5 %pad_maximum_fusion = bf16[8,512,3,768]{3,1,2,0:T(8,128)(2,1)} fusion(bf16[8,512,1,768]{3,1,2,0:T(8,128)(2,1)S(1)} %bitcast.109, bf16[8,512,1,768]{3,1,2,0:T(8,128)(2,1)S(1)} %bitcast.110, bf16[8,512,1,768]{3,1,2,0:T(8,128)(2,1)S(1)} %bitcast.111), kind=kLoop, calls=%fused_computation.7 | loop fusion | flops 18874368 | bytes 37748736 | tf_op jit(solution)/shard_map/stack | solution.py:66
  328.1 40.9 %all-to-all-done.3 = bf16[16,32,4096]{2,1,0:T(8,128)(2,1)} async-done(((bf16[16,32,4096]{2,1,0:T(8,128)(2,1)}), bf16[16,32,4096]{2,1,0:T(8,128)(2,1)}, u32[]{:S(2)}, u32[]{:S(2)}) %all-to-all-start.3) | async-done | bytes 4194336 | tf_op jit(solution)/shard_map/all_to_all | solution.py:121
  369.1 6.3 %all-to-all-start.6 = ((bf16[8,512,3,768]{3,1,2,0:T(8,128)(2,1)}), bf16[8,512,3,768]{3,1,2,0:T(8,128)(2,1)}, u32[]{:S(2)}, u32[]{:S(2)}) async-start(bf16[8,512,3,768]{3,1,2,0:T(8,128)(2,1)} %pad_maximum_fusion), calls=%async_computation.6 | async-start | bytes 37748736 | tf_op jit(solution)/shard_map/all_to_all | solution.py:69
  375.4 7.5 %multiply_reduce_fusion = bf16[128,4096]{1,0:T(8,128)(2,1)} fusion(bf16[128,2,4096]{2,1,0:T(2,128)(2,1)S(1)} %copy-done.2, f32[128,2]{1,0:T(8,128)S(1)} %copy.62), kind=kLoop, calls=%fused_computation.29 | loop fusion | flops 2621440 | bytes 3146752 | tf_op jit(solution)/shard_map/reduce_sum | solution.py:103
  382.9 0.7 multiply_reduce_fusion.1
  383.6 0.7 div.45
  384.3 1.3 copy.73
  385.6 6.9 %gather_fusion.3 = bf16[256,4096]{1,0:T(8,128)(2,1)S(1)} fusion(bf16[512,4096]{1,0:T(8,128)(2,1)} %bitcast.13, s32[1024]{0:T(1024)} %copy-done.9), kind=kCustom, calls=%fused_computation.3 | custom fusion | bytes 4195328 | tf_op jit(solution)/shard_map/gather | solution.py:125
  392.5 4.0 reshape.187
  396.6 7.5 %reduce_sum.78 = f32[128,4096]{1,0:T(8,128)S(1)} reduce(f32[128,2,4096]{2,1,0:T(2,128)} %reshape.187, f32[]{:T(128)} %constant.56.clone.1), dimensions={1}, to_apply=%region_6.7 | reduce | flops 524288 | bytes 6291460 | tf_op jit(solution)/shard_map/reduce_sum | solution.py:124
  404.1 1.4 fusion.17
  405.5 177.5 %all-to-all-done.6 = bf16[8,512,3,768]{3,1,2,0:T(8,128)(2,1)} async-done(((bf16[8,512,3,768]{3,1,2,0:T(8,128)(2,1)}), bf16[8,512,3,768]{3,1,2,0:T(8,128)(2,1)}, u32[]{:S(2)}, u32[]{:S(2)}) %all-to-all-start.6) | async-done | bytes 18874400 | tf_op jit(solution)/shard_map/all_to_all | solution.py:69
  583.0 10.4 %convert_reduce_fusion = f32[512,3,768]{2,0,1:T(8,128)S(1)} fusion(bf16[8,512,3,768]{3,1,2,0:T(8,128)(2,1)} %all-to-all-done.6), kind=kLoop, calls=%fused_computation.6 | loop fusion | flops 17694720 | bytes 23592960 | tf_op jit(solution)/shard_map/reduce_sum | solution.py:70
  593.5 1.5 fusion.26
  (75 shorter events, 0.4 us)
Async XLA Ops:
  0.6 91.5 %copy-start = (bf16[4096,16]{0,1:T(8,128)(2,1)S(1)}, bf16[4096,16]{0,1:T(8,128)(2,1)}, u32[]{:S(2)}) copy-start(bf16[4096,16]{0,1:T(8,128)(2,1)} %param.10) | copy-start | bytes 393220
  10.8 61.6 %slice-start.4 = ((s8[6291456]{0:T(1024)(128)(4,1)}), s8[4194304]{0:T(1024)(128)(4,1)S(1)}, s32[]{:S(2)}) async-start(s8[6291456]{0:T(1024)(128)(4,1)} %bitcast.118), calls=%async_computation.11 | async-start | bytes 8388608
  65.3 7.1 %copy-start.3 = (bf16[16,32,4096]{2,1,0:T(8,128)(2,1)}, bf16[16,32,4096]{2,1,0:T(8,128)(2,1)S(1)}, u32[]{:S(2)}) copy-start(bf16[16,32,4096]{2,1,0:T(8,128)(2,1)S(1)} %all_to_all.41) | copy-start | bytes 12582916
  65.3 7.1 %slice-start.5 = ((s8[6291456]{0:T(1024)(128)(4,1)}), s8[2097152]{0:T(1024)(128)(4,1)S(1)}, s32[]{:S(2)}) async-start(s8[6291456]{0:T(1024)(128)(4,1)} %bitcast.118), calls=%async_computation.12 | async-start | bytes 4194304
  65.3 11.7 %slice-start.2 = ((s8[6291456]{0:T(1024)(128)(4,1)}), s8[4194304]{0:T(1024)(128)(4,1)S(1)}, s32[]{:S(2)}) async-start(s8[6291456]{0:T(1024)(128)(4,1)} %bitcast.116), calls=%async_computation.9 | async-start | bytes 8388608
  72.4 4.6 copy-start.14
  72.4 4.6 slice-start.3
  77.0 5.1 copy-start.15
  82.2 9.7 %copy-start.8 = (s32[128,2]{0,1:T(2,128)S(1)}, s32[128,2]{0,1:T(2,128)}, u32[]{:S(2)}) copy-start(s32[128,2]{0,1:T(2,128)} %param.9) | copy-start | bytes 3076
  82.2 10.0 %copy-start.1 = (bf16[128,4096]{1,0:T(8,128)(2,1)S(1)}, bf16[128,4096]{1,0:T(8,128)(2,1)}, u32[]{:S(2)}) copy-start(bf16[128,4096]{1,0:T(8,128)(2,1)} %param.7) | copy-start | bytes 3145732
  82.2 67.4 %all-to-all-start.1 = ((bf16[16,32,4096]{2,1,0:T(8,128)(2,1)}), bf16[16,32,4096]{2,1,0:T(8,128)(2,1)}, u32[]{:S(2)}, u32[]{:S(2)}) async-start(bf16[16,32,4096]{2,1,0:T(8,128)(2,1)} %fusion.12), calls=%async_computation.1 | async-start | bytes 8388608 | tf_op jit(solution)/shard_map/all_to_all | solution.py:99
  92.6 2.2 copy-start.5
  105.0 51.2 %copy-start.9 = (s32[1024]{0:T(1024)}, s32[1024]{0:T(1024)S(1)}, u32[]{:S(2)}) copy-start(s32[1024]{0:T(1024)S(1)} %pad_clamp_fusion.1) | copy-start | bytes 12292
  166.6 2.3 copy-start.6
  168.9 24.2 %all-to-all-start.4 = ((f32[128,1,512]{2,1,0:T(1,128)}), f32[128,1,512]{2,1,0:T(1,128)S(1)}, u32[]{:S(2)}, u32[]{:S(2)}) async-start(f32[128,1,512]{2,1,0:T(1,128)} %all_to_all.33), calls=%async_computation.4 | async-start | bytes 524288 | tf_op jit(solution)/shard_map/all_to_all | solution.py:58
  193.1 88.8 %slice-start.6 = ((s8[6291456]{0:T(1024)(128)(4,1)}), s8[2097152]{0:T(1024)(128)(4,1)S(1)}, s32[]{:S(2)}) async-start(s8[6291456]{0:T(1024)(128)(4,1)} %bitcast.120), calls=%async_computation.13 | async-start | bytes 4194304
  193.1 67.7 %all-to-all-start.2 = ((bf16[16,32,4096]{2,1,0:T(8,128)(2,1)}), bf16[16,32,4096]{2,1,0:T(8,128)(2,1)}, u32[]{:S(2)}, u32[]{:S(2)}) async-start(bf16[16,32,4096]{2,1,0:T(8,128)(2,1)} %bitcast.105), calls=%async_computation.2 | async-start | bytes 8388608 | tf_op jit(solution)/shard_map/all_to_all | solution.py:119
  261.6 40.9 %all-to-all-start.5 = ((f32[128,1,512]{2,1,0:T(1,128)}), f32[128,1,512]{2,1,0:T(1,128)S(1)}, u32[]{:S(2)}, u32[]{:S(2)}) async-start(f32[128,1,512]{2,1,0:T(1,128)} %broadcast_in_dim.16), calls=%async_computation.5 | async-start | bytes 524288 | tf_op jit(solution)/shard_map/all_to_all | solution.py:60
  271.4 10.5 %slice-start.7 = ((s8[6291456]{0:T(1024)(128)(4,1)}), s8[4194304]{0:T(1024)(128)(4,1)S(1)}, s32[]{:S(2)}) async-start(s8[6291456]{0:T(1024)(128)(4,1)} %bitcast.120), calls=%async_computation.14 | async-start | bytes 8388608
  281.0 0.9 copy-start.12
  281.9 5.7 copy-start.16
  281.9 14.3 %slice-start.8 = ((s8[6291456]{0:T(1024)(128)(4,1)}), s8[4194304]{0:T(1024)(128)(4,1)S(1)}, s32[]{:S(2)}) async-start(s8[6291456]{0:T(1024)(128)(4,1)} %bitcast.122), calls=%async_computation.15 | async-start | bytes 8388608
  287.6 8.6 %slice-start.9 = ((s8[6291456]{0:T(1024)(128)(4,1)}), s8[2097152]{0:T(1024)(128)(4,1)S(1)}, s32[]{:S(2)}) async-start(s8[6291456]{0:T(1024)(128)(4,1)} %bitcast.122), calls=%async_computation.16 | async-start | bytes 4194304
  287.6 8.6 %copy-start.10 = (f32[16,32,4096]{2,1,0:T(8,128)S(1)}, f32[16,32,4096]{2,1,0:T(8,128)}, u32[]{:S(2)}) copy-start(f32[16,32,4096]{2,1,0:T(8,128)} %fusion.4) | copy-start | bytes 25165828
  302.5 7.4 %copy-start.13 = (bf16[16,32,768]{2,1,0:T(8,128)(2,1)S(1)}, bf16[16,32,768]{2,1,0:T(8,128)(2,1)}, u32[]{:S(2)}) copy-start(bf16[16,32,768]{2,1,0:T(8,128)(2,1)} %copy-done.12) | copy-start | bytes 2359300
  302.5 66.5 %all-to-all-start.3 = ((bf16[16,32,4096]{2,1,0:T(8,128)(2,1)}), bf16[16,32,4096]{2,1,0:T(8,128)(2,1)}, u32[]{:S(2)}, u32[]{:S(2)}) async-start(bf16[16,32,4096]{2,1,0:T(8,128)(2,1)} %add_convert_fusion), calls=%async_computation.3 | async-start | bytes 8388608 | tf_op jit(solution)/shard_map/all_to_all | solution.py:121
  309.9 5.9 copy-start.4
  309.9 5.9 copy-start.11
  309.9 9.7 %slice-start = ((s8[6291456]{0:T(1024)(128)(4,1)}), s8[4194304]{0:T(1024)(128)(4,1)S(1)}, s32[]{:S(2)}) async-start(s8[6291456]{0:T(1024)(128)(4,1)} %bitcast.107), calls=%async_computation.7 | async-start | bytes 8388608
  315.8 3.8 slice-start.1
  328.1 47.3 %copy-start.2 = (bf16[128,2,4096]{2,1,0:T(2,128)(2,1)S(1)}, bf16[128,2,4096]{2,1,0:T(2,128)(2,1)}, u32[]{:S(2)}) copy-start(bf16[128,2,4096]{2,1,0:T(2,128)(2,1)} %reshape.184) | copy-start | bytes 6291460
  369.1 214.0 %all-to-all-start.6 = ((bf16[8,512,3,768]{3,1,2,0:T(8,128)(2,1)}), bf16[8,512,3,768]{3,1,2,0:T(8,128)(2,1)}, u32[]{:S(2)}, u32[]{:S(2)}) async-start(bf16[8,512,3,768]{3,1,2,0:T(8,128)(2,1)} %pad_maximum_fusion), calls=%async_computation.6 | async-start | bytes 37748736 | tf_op jit(solution)/shard_map/all_to_all | solution.py:69
  396.6 7.5 %copy-start.7 = (bf16[128,16]{0,1:T(8,128)(2,1)S(1)}, bf16[128,16]{0,1:T(8,128)(2,1)}, u32[]{:S(2)}) copy-start(bf16[128,16]{0,1:T(8,128)(2,1)} %copy-done.6) | copy-start | bytes 12292

commit v3 on v2

--- a/solution.py
+++ b/solution.py
@@ -65,9 +65,12 @@
     rows = parts[0].shape[0] // replica_count
     blocks = jnp.stack([p.astype(jnp.bfloat16) for p in parts], axis=1)
     blocks = blocks.reshape((replica_count, rows) + blocks.shape[1:])
-    blocks = blocks.reshape(replica_count, rows, len(parts), parts[0].shape[1])
-    arrived = lax.all_to_all(blocks, axis, 0, 0, tiled=True)
-    total = jnp.sum(arrived.astype(jnp.float32), axis=0)
+    me = lax.axis_index(axis)
+    total = lax.dynamic_index_in_dim(blocks, me, axis=0, keepdims=False).astype(jnp.float32)
+    for shift in range(1, replica_count):
+        ahead = lax.dynamic_index_in_dim(blocks, (me + shift) % replica_count, axis=0, keepdims=False)
+        pairs = [(j, (j + shift) % replica_count) for j in range(replica_count)]
+        total = total + lax.ppermute(ahead, axis, pairs).astype(jnp.float32)
     return tuple(total[:, i] for i in range(len(parts)))
 
 
@@ -130,9 +133,8 @@
     gate_part = jnp.einsum("nkd,nkh->dh", received, grad_gate, preferred_element_type=jnp.float32)
     up_part = jnp.einsum("nkd,nkh->dh", received, grad_up, preferred_element_type=jnp.float32)
     down_part = jnp.einsum("nkd,nkh->dh", grad_recv, hidden, preferred_element_type=jnp.float32)
-    gate_total, up_total, down_total = reduce_scatter_by_exchange(
-        (gate_part, up_part, down_part), "dp"
-    )
+    (down_total,) = reduce_scatter_by_exchange((down_part,), "dp")
+    gate_total, up_total = reduce_scatter_by_exchange((gate_part, up_part), "dp")
     gate_grad = (gate_total / replica_count).astype(jnp.bfloat16)[None]
     up_grad = (up_total / replica_count).astype(jnp.bfloat16)[None]
     down_grad = (down_total / replica_count).astype(jnp.bfloat16)[None]

time: 603 us -> 653 us (1.083)
  the two profiles are of different devices: /device:TPU:20 before, /device:TPU:4 now
where the time goes in v3:
time: 653 us; the launch traced here: 645 us
  waiting for transfers between devices  349 us (53%)
  starting transfers between devices  85.5 us (13%)
  matrix products  57.6 us (9%)
  local copies, waits for them, and re-layouts  57.5 us (9%)
  blocking collectives  56.9 us (9%)
  other arithmetic  37.4 us (6%)
    ppermute x14, waiting for transfers between devices, reduce_scatter_by_exchange(): total = total + lax.ppermute(ahead, axis, pairs).astype(jnp.float32)  252 us
    all_to_all x1, blocking collectives, on_device(): lax.all_to_all(outbound, 'expert', split_axis=0, concat_axis=0, tiled=True)  56.9 us
    all_to_all x1, waiting for transfers between devices, on_device(): lax.all_to_all(grad_out, 'expert', split_axis=0, concat_axis=0, tiled=True)  54.1 us
    all_to_all x1, waiting for transfers between devices, on_device(): lax.all_to_all(expert_out, 'expert', split_axis=0, concat_axis=0, tiled=T...  41 us
    ppermute x14, starting transfers between devices, reduce_scatter_by_exchange(): total = total + lax.ppermute(ahead, axis, pairs).astype(jnp.float32)  36.5 us
    all_to_all x1, starting transfers between devices, all_reduce_by_exchange(): lax.all_to_all(chunks, axes, 0, 0, tiled=True)  13.7 us
    all_to_all x1, starting transfers between devices, all_reduce_by_exchange(): return lax.all_to_all(spread, axes, 0, 0, tiled=True).reshape(part.shape)  13.2 us
  transfers between devices with their start and end apart: 19, of which 9 were waited for; matrix products, arithmetic and copies ran while one was open for 13% of the time, Pallas kernels for 0%

profile of v3, /device:TPU:4, one launch (start us, length us, event | category | flops | bytes accessed | tf_op | source)
XLA Modules:
  0.0 645.0 jit_solution(2475729775137306743)
XLA Ops:
  0.6 0.7 broadcast_multiply_fusion
  1.4 0.8 copy.70
  3.6 1.4 scatter_custom_fusion
  5.1 1.3 concatenate.7
  6.4 4.4 gather_fusion
  10.8 56.9 %all_to_all.36 = bf16[16,32,4096]{2,1,0:T(8,128)(2,1)S(1)} all-to-all(bf16[16,32,4096]{2,1,0:T(8,128)(2,1)} %bitcast.147), channel_id=1, replica_groups=mesh['expert'=16,'dp'=8] {'expert'}, dimensions={0} | all-to-all | bytes 8388608 | tf_op jit(solution)/shard_map/all_to_all | solution.py:93
  67.7 7.1 %fusion.10 = f32[16,32,768]{2,1,0:T(8,128)S(1)} fusion(bf16[16,32,4096]{2,1,0:T(8,128)(2,1)S(1)} %all_to_all.36, bf16[1,4096,768]{2,1,0:T(8,128)(2,1)} %param.11), kind=kOutput, calls=%fused_computation.36 | convolution fusion | flops 3221225472 | bytes 12058624 | tf_op jit(solution)/shard_map/...d,dh->...h/dot_general | solution.py:31
  74.8 4.6 multiply_convert_fusion.3
  79.4 5.1 fusion.12
  84.5 7.7 %all-to-all-start.1 = ((bf16[16,32,4096]{2,1,0:T(8,128)(2,1)}), bf16[16,32,4096]{2,1,0:T(8,128)(2,1)}, u32[]{:S(2)}, u32[]{:S(2)}) async-start(bf16[16,32,4096]{2,1,0:T(8,128)(2,1)} %fusion.12), calls=%async_computation.1 | async-start | bytes 8388608 | tf_op jit(solution)/shard_map/all_to_all | solution.py:102
  92.9 2.0 gather_fusion.4
  95.1 4.1 mul.102
  99.2 6.2 mul.103
  105.3 41.0 %all-to-all-done.1 = bf16[16,32,4096]{2,1,0:T(8,128)(2,1)} async-done(((bf16[16,32,4096]{2,1,0:T(8,128)(2,1)}), bf16[16,32,4096]{2,1,0:T(8,128)(2,1)}, u32[]{:S(2)}, u32[]{:S(2)}) %all-to-all-start.1) | async-done | bytes 4194336 | tf_op jit(solution)/shard_map/all_to_all | solution.py:102
  146.4 6.6 %gather_fusion.1 = bf16[256,4096]{1,0:T(8,128)(2,1)S(1)} fusion(bf16[512,4096]{1,0:T(8,128)(2,1)} %bitcast.11, s32[1024]{0:T(1024)S(1)} %pad_clamp_fusion.1), kind=kCustom, calls=%fused_computation.1 | custom fusion | bytes 4195328 | tf_op jit(solution)/shard_map/gather | solution.py:105
  153.0 2.6 reshape.198
  155.7 7.3 %fusion.24 = f32[128,1,2]{2,1,0:T(1,128)S(1)} fusion(bf16[128,2,4096]{2,1,0:T(2,128)(2,1)} %reshape.198, bf16[128,4096,1]{1,0,2:T(8,128)(2,1)} %bitcast.150), kind=kOutput, calls=%fused_computation.51 | convolution fusion | flops 2097152 | bytes 3146752 | tf_op jit(solution)/shard_map/td,tkd->tk/dot_general | solution.py:109
  164.7 1.5 all_to_all.29
  166.2 13.7 %all-to-all-start.4 = ((f32[128,1,512]{2,1,0:T(1,128)}), f32[128,1,512]{2,1,0:T(1,128)S(1)}, u32[]{:S(2)}, u32[]{:S(2)}) async-start(f32[128,1,512]{2,1,0:T(1,128)} %all_to_all.29), calls=%async_computation.4 | async-start | bytes 524288 | tf_op jit(solution)/shard_map/all_to_all | solution.py:58
  179.9 2.6 multiply_convert_fusion
  182.8 4.5 gather_fusion.2
  187.3 1.9 all-to-all-done.4
  189.2 7.2 %all-to-all-start.2 = ((bf16[16,32,4096]{2,1,0:T(8,128)(2,1)}), bf16[16,32,4096]{2,1,0:T(8,128)(2,1)}, u32[]{:S(2)}, u32[]{:S(2)}) async-start(bf16[16,32,4096]{2,1,0:T(8,128)(2,1)} %bitcast.146), calls=%async_computation.2 | async-start | bytes 8388608 | tf_op jit(solution)/shard_map/all_to_all | solution.py:122
  196.6 54.1 %all-to-all-done.2 = bf16[16,32,4096]{2,1,0:T(8,128)(2,1)} async-done(((bf16[16,32,4096]{2,1,0:T(8,128)(2,1)}), bf16[16,32,4096]{2,1,0:T(8,128)(2,1)}, u32[]{:S(2)}, u32[]{:S(2)}) %all-to-all-start.2) | async-done | bytes 4194336 | tf_op jit(solution)/shard_map/all_to_all | solution.py:122
  250.7 0.8 broadcast_in_dim.16
  251.6 13.2 %all-to-all-start.5 = ((f32[128,1,512]{2,1,0:T(1,128)}), f32[128,1,512]{2,1,0:T(1,128)S(1)}, u32[]{:S(2)}, u32[]{:S(2)}) async-start(f32[128,1,512]{2,1,0:T(1,128)} %broadcast_in_dim.16), calls=%async_computation.5 | async-start | bytes 524288 | tf_op jit(solution)/shard_map/all_to_all | solution.py:60
  264.8 8.3 %multiply_convert_fusion.2 = (bf16[16,32,768]{2,1,0:T(8,128)(2,1)S(1)}, bf16[16,32,768]{2,1,0:T(8,128)(2,1)S(1)}) fusion(f32[16,32,768]{2,1,0:T(8,128)S(1)} %copy-done.19, f32[16,32,768]{2,1,0:T(8,128)} %get-tuple-element.54, bf16[16,32,4096]{2,1,0:T(8,128)(2,1)} %all-to-all-done.2, bf16[1,4096,768]{2,1,0:T(8,128)(2,1)} %param.13), kind=kOutput, calls=%fused_computation.75 | convolution fusion | flops 3226337280 | bytes 15204352 | tf_op jit(solution)/shard_map/...d,dh->...h/dot_general | solution.py:42
  273.1 3.8 bitcast_convert_fusion.2
  277.0 3.8 bitcast_convert_fusion.1
  280.8 1.5 fusion.51
  282.3 1.6 copy-done.2
  283.9 4.1 fusion.50
  287.9 5.8 bitcast_convert_fusion
  293.8 2.2 dynamic-slice_bitcast_fusion.6
  296.0 1.8 copy-done.5
  297.8 1.5 collective-permute-start.7
  299.2 3.6 collective-permute-start.12
  302.9 1.4 collective-permute-start.11
  304.3 1.6 collective-permute-start.10
  305.8 2.6 collective-permute-start.6
  308.5 3.5 fusion.4
  311.9 8.6 %collective-permute-done.7 = bf16[512,1,768]{2,0,1:T(8,128)(2,1)S(1)} collective-permute-done((bf16[512,1,768]{2,0,1:T(8,128)(2,1)S(1)}, bf16[512,1,768]{2,0,1:T(8,128)(2,1)S(1)}, u32[]{:S(2)}, u32[]{:S(2)}) %collective-permute-start.7) | collective-permute-done | bytes 786464 | tf_op jit(solution)/shard_map/ppermute | solution.py:73
  320.6 6.3 add_convert_fusion
  326.9 7.2 %all-to-all-start.3 = ((bf16[16,32,4096]{2,1,0:T(8,128)(2,1)}), bf16[16,32,4096]{2,1,0:T(8,128)(2,1)}, u32[]{:S(2)}, u32[]{:S(2)}) async-start(bf16[16,32,4096]{2,1,0:T(8,128)(2,1)} %add_convert_fusion), calls=%async_computation.3 | async-start | bytes 8388608 | tf_op jit(solution)/shard_map/all_to_all | solution.py:124
  334.1 19.7 %collective-permute-done.12 = bf16[512,1,768]{2,0,1:T(8,128)(2,1)} collective-permute-done((bf16[512,1,768]{2,0,1:T(8,128)(2,1)}, bf16[512,1,768]{2,0,1:T(8,128)(2,1)}, u32[]{:S(2)}, u32[]{:S(2)}) %collective-permute-start.12) | collective-permute-done | bytes 786464 | tf_op jit(solution)/shard_map/ppermute | solution.py:73
  353.7 17.8 %collective-permute-start.13 = (bf16[512,1,768]{2,0,1:T(8,128)(2,1)}, bf16[512,1,768]{2,0,1:T(8,128)(2,1)}, u32[]{:S(2)}, u32[]{:S(2)}) collective-permute-start(bf16[512,1,768]{2,0,1:T(8,128)(2,1)} %get-tuple-element.46), channel_id=1, source_target_pairs={{0,7},{1,0},{2,1},{3,2},{4,3},{5,4},{6,5},{7,6},{8,15},{9,8},{10,9... | collective-permute-start | bytes 2359304 | tf_op jit(solution)/shard_map/ppermute | solution.py:73
  371.6 96.5 %collective-permute-done.9 = bf16[512,1,768]{2,0,1:T(8,128)(2,1)} collective-permute-done((bf16[512,1,768]{2,0,1:T(8,128)(2,1)}, bf16[512,1,768]{2,0,1:T(8,128)(2,1)}, u32[]{:S(2)}, u32[]{:S(2)}) %collective-permute-start.9) | collective-permute-done | bytes 786464 | tf_op jit(solution)/shard_map/ppermute | solution.py:73
  468.6 14.1 %collective-permute-done.13 = bf16[512,1,768]{2,0,1:T(8,128)(2,1)} collective-permute-done((bf16[512,1,768]{2,0,1:T(8,128)(2,1)}, bf16[512,1,768]{2,0,1:T(8,128)(2,1)}, u32[]{:S(2)}, u32[]{:S(2)}) %collective-permute-start.13) | collective-permute-done | bytes 786464 | tf_op jit(solution)/shard_map/ppermute | solution.py:73
  482.6 2.9 collective-permute-start.3
  485.5 1.4 collective-permute-start.4
  486.9 3.2 collective-permute-start.5
  490.2 7.5 %multiply_reduce_fusion = bf16[128,4096]{1,0:T(8,128)(2,1)} fusion(bf16[128,2,4096]{2,1,0:T(2,128)(2,1)S(1)} %copy-done.4, f32[128,2]{1,0:T(8,128)S(1)} %copy-done.10), kind=kLoop, calls=%fused_computation.43 | loop fusion | flops 2621440 | bytes 3146752 | tf_op jit(solution)/shard_map/reduce_sum | solution.py:106
  497.7 0.7 multiply_reduce_fusion.1
  498.4 0.7 div.45
  499.1 1.3 copy.79
  500.4 4.3 fusion.52
  504.6 67.1 %collective-permute-done.1 = bf16[512,2,768]{2,0,1:T(8,128)(2,1)} collective-permute-done((bf16[512,2,768]{2,0,1:T(8,128)(2,1)}, bf16[512,2,768]{2,0,1:T(8,128)(2,1)}, u32[]{:S(2)}, u32[]{:S(2)}) %collective-permute-start.1) | collective-permute-done | bytes 1572896 | tf_op jit(solution)/shard_map/ppermute | solution.py:73
  571.8 45.8 %collective-permute-done.5 = bf16[512,2,768]{2,0,1:T(8,128)(2,1)} collective-permute-done((bf16[512,2,768]{2,0,1:T(8,128)(2,1)}, bf16[512,2,768]{2,0,1:T(8,128)(2,1)}, u32[]{:S(2)}, u32[]{:S(2)}) %collective-permute-start.5) | collective-permute-done | bytes 1572896 | tf_op jit(solution)/shard_map/ppermute | solution.py:73
  617.6 6.1 fusion.23
  623.7 1.4 fusion.54
  625.1 6.9 %gather_fusion.3 = bf16[256,4096]{1,0:T(8,128)(2,1)S(1)} fusion(bf16[512,4096]{1,0:T(8,128)(2,1)} %bitcast.13, s32[1024]{0:T(1024)} %copy-done.14), kind=kCustom, calls=%fused_computation.3 | custom fusion | bytes 4195328 | tf_op jit(solution)/shard_map/gather | solution.py:128
  632.0 3.9 reshape.201
  635.9 7.5 %reduce_sum.69 = f32[128,4096]{1,0:T(8,128)S(1)} reduce(f32[128,2,4096]{2,1,0:T(2,128)} %reshape.201, f32[]{:T(128)} %constant.149.clone.1), dimensions={1}, to_apply=%region_6.7 | reduce | flops 524288 | bytes 6291460 | tf_op jit(solution)/shard_map/reduce_sum | solution.py:127
  643.4 1.4 fusion.17
  (109 shorter events, 5.1 us)
Async XLA Ops:
  0.6 91.8 %copy-start = (bf16[4096,16]{0,1:T(8,128)(2,1)S(1)}, bf16[4096,16]{0,1:T(8,128)(2,1)}, u32[]{:S(2)}) copy-start(bf16[4096,16]{0,1:T(8,128)(2,1)} %param.10) | copy-start | bytes 393220
  10.8 64.0 %slice-start.2 = ((s8[6291456]{0:T(1024)(128)(4,1)}), s8[4194304]{0:T(1024)(128)(4,1)S(1)}, s32[]{:S(2)}) async-start(s8[6291456]{0:T(1024)(128)(4,1)} %bitcast.156), calls=%async_computation.8 | async-start | bytes 8388608
  67.7 7.1 %copy-start.6 = (bf16[16,32,4096]{2,1,0:T(8,128)(2,1)}, bf16[16,32,4096]{2,1,0:T(8,128)(2,1)S(1)}, u32[]{:S(2)}) copy-start(bf16[16,32,4096]{2,1,0:T(8,128)(2,1)S(1)} %all_to_all.36) | copy-start | bytes 12582916
  67.7 7.1 %slice-start.3 = ((s8[6291456]{0:T(1024)(128)(4,1)}), s8[2097152]{0:T(1024)(128)(4,1)S(1)}, s32[]{:S(2)}) async-start(s8[6291456]{0:T(1024)(128)(4,1)} %bitcast.156), calls=%async_computation.9 | async-start | bytes 4194304
  67.7 11.7 %slice-start = ((s8[6291456]{0:T(1024)(128)(4,1)}), s8[4194304]{0:T(1024)(128)(4,1)S(1)}, s32[]{:S(2)}) async-start(s8[6291456]{0:T(1024)(128)(4,1)} %bitcast.154), calls=%async_computation.6 | async-start | bytes 8388608
  74.8 4.6 copy-start.18
  74.8 4.6 slice-start.1
  79.4 5.1 copy-start.20
  84.5 7.7 %copy-start.13 = (s32[128,2]{0,1:T(2,128)S(1)}, s32[128,2]{0,1:T(2,128)}, u32[]{:S(2)}) copy-start(s32[128,2]{0,1:T(2,128)} %param.9) | copy-start | bytes 3076
  84.5 8.0 %copy-start.3 = (bf16[128,4096]{1,0:T(8,128)(2,1)S(1)}, bf16[128,4096]{1,0:T(8,128)(2,1)}, u32[]{:S(2)}) copy-start(bf16[128,4096]{1,0:T(8,128)(2,1)} %param.7) | copy-start | bytes 3145732
  84.5 61.9 %all-to-all-start.1 = ((bf16[16,32,4096]{2,1,0:T(8,128)(2,1)}), bf16[16,32,4096]{2,1,0:T(8,128)(2,1)}, u32[]{:S(2)}, u32[]{:S(2)}) async-start(bf16[16,32,4096]{2,1,0:T(8,128)(2,1)} %fusion.12), calls=%async_computation.1 | async-start | bytes 8388608 | tf_op jit(solution)/shard_map/all_to_all | solution.py:102
  92.9 2.2 copy-start.8
  105.3 47.7 %copy-start.14 = (s32[1024]{0:T(1024)}, s32[1024]{0:T(1024)S(1)}, u32[]{:S(2)}) copy-start(s32[1024]{0:T(1024)S(1)} %pad_clamp_fusion.1) | copy-start | bytes 12292
  163.2 0.6 copy-start.9
  163.3 0.6 copy-start.11
  166.2 23.0 %all-to-all-start.4 = ((f32[128,1,512]{2,1,0:T(1,128)}), f32[128,1,512]{2,1,0:T(1,128)S(1)}, u32[]{:S(2)}, u32[]{:S(2)}) async-start(f32[128,1,512]{2,1,0:T(1,128)} %all_to_all.29), calls=%async_computation.4 | async-start | bytes 524288 | tf_op jit(solution)/shard_map/all_to_all | solution.py:58
  189.2 75.6 %copy-start.19 = (f32[16,32,768]{2,1,0:T(8,128)S(1)}, f32[16,32,768]{2,1,0:T(8,128)}, u32[]{:S(2)}) copy-start(f32[16,32,768]{2,1,0:T(8,128)} %copy-done.18) | copy-start | bytes 4718596
  189.2 61.6 %all-to-all-start.2 = ((bf16[16,32,4096]{2,1,0:T(8,128)(2,1)}), bf16[16,32,4096]{2,1,0:T(8,128)(2,1)}, u32[]{:S(2)}, u32[]{:S(2)}) async-start(bf16[16,32,4096]{2,1,0:T(8,128)(2,1)} %bitcast.146), calls=%async_computation.2 | async-start | bytes 8388608 | tf_op jit(solution)/shard_map/all_to_all | solution.py:122
  251.6 75.3 %all-to-all-start.5 = ((f32[128,1,512]{2,1,0:T(1,128)}), f32[128,1,512]{2,1,0:T(1,128)S(1)}, u32[]{:S(2)}, u32[]{:S(2)}) async-start(f32[128,1,512]{2,1,0:T(1,128)} %broadcast_in_dim.16), calls=%async_computation.5 | async-start | bytes 524288 | tf_op jit(solution)/shard_map/all_to_all | solution.py:60
  264.8 8.4 %copy-start.7 = (bf16[16,32,4096]{2,1,0:T(8,128)(2,1)S(1)}, bf16[16,32,4096]{2,1,0:T(8,128)(2,1)}, u32[]{:S(2)}) copy-start(bf16[16,32,4096]{2,1,0:T(8,128)(2,1)} %copy-done.6) | copy-start | bytes 12582916
  273.1 3.8 copy-start.15
  273.1 3.8 copy-start.16
  276.9 5.3 copy-start.1
  280.7 3.1 copy-start.2
  283.8 4.1 copy-start.21
  283.9 24.6 %slice-start.4 = ((s8[6291456]{0:T(1024)(128)(4,1)}), s8[2097152]{0:T(1024)(128)(4,1)S(1)}, s32[]{:S(2)}) async-start(s8[6291456]{0:T(1024)(128)(4,1)} %bitcast.158), calls=%async_computation.10 | async-start | bytes 4194304
  287.9 20.6 %slice-start.5 = ((s8[6291456]{0:T(1024)(128)(4,1)}), s8[4194304]{0:T(1024)(128)(4,1)S(1)}, s32[]{:S(2)}) async-start(s8[6291456]{0:T(1024)(128)(4,1)} %bitcast.158), calls=%async_computation.11 | async-start | bytes 8388608
  293.8 4.0 copy-start.5
  293.8 14.7 %copy-start.17 = (bf16[16,32,768]{2,1,0:T(8,128)(2,1)S(1)}, bf16[16,32,768]{2,1,0:T(8,128)(2,1)}, u32[]{:S(2)}) copy-start(bf16[16,32,768]{2,1,0:T(8,128)(2,1)} %copy-done.16) | copy-start | bytes 2359300
  297.8 22.8 %collective-permute-start.7 = (bf16[512,1,768]{2,0,1:T(8,128)(2,1)S(1)}, bf16[512,1,768]{2,0,1:T(8,128)(2,1)S(1)}, u32[]{:S(2)}, u32[]{:S(2)}) collective-permute-start(bf16[512,1,768]{2,0,1:T(8,128)(2,1)S(1)} %get-tuple-element.40), channel_id=1, source_target_pairs={{0,1},{1,2},{2,3},{3,4},{4,5},{5,6},{6,7},{7,0},{8,9},{9,10},{10,1... | collective-permute-start | bytes 2359304 | tf_op jit(solution)/shard_map/ppermute | solution.py:73
  299.2 54.5 %collective-permute-start.12 = (bf16[512,1,768]{2,0,1:T(8,128)(2,1)}, bf16[512,1,768]{2,0,1:T(8,128)(2,1)}, u32[]{:S(2)}, u32[]{:S(2)}) collective-permute-start(bf16[512,1,768]{2,0,1:T(8,128)(2,1)} %get-tuple-element.41), channel_id=1, source_target_pairs={{0,6},{1,7},{2,0},{3,1},{4,2},{5,3},{6,4},{7,5},{8,14},{9,15},{10,... | collective-permute-start | bytes 2359304 | tf_op jit(solution)/shard_map/ppermute | solution.py:73
  302.9 50.8 %collective-permute-start.11 = (bf16[512,1,768]{2,0,1:T(8,128)(2,1)}, bf16[512,1,768]{2,0,1:T(8,128)(2,1)}, u32[]{:S(2)}, u32[]{:S(2)}) collective-permute-start(bf16[512,1,768]{2,0,1:T(8,128)(2,1)} %get-tuple-element.42), channel_id=1, source_target_pairs={{0,5},{1,6},{2,7},{3,0},{4,1},{5,2},{6,3},{7,4},{8,13},{9,14},{10,... | collective-permute-start | bytes 2359304 | tf_op jit(solution)/shard_map/ppermute | solution.py:73
  304.3 16.3 %slice-start.6 = ((s8[6291456]{0:T(1024)(128)(4,1)}), s8[4194304]{0:T(1024)(128)(4,1)S(1)}, s32[]{:S(2)}) async-start(s8[6291456]{0:T(1024)(128)(4,1)} %bitcast.160), calls=%async_computation.12 | async-start | bytes 8388608
  304.3 16.3 %slice-start.7 = ((s8[6291456]{0:T(1024)(128)(4,1)}), s8[2097152]{0:T(1024)(128)(4,1)S(1)}, s32[]{:S(2)}) async-start(s8[6291456]{0:T(1024)(128)(4,1)} %bitcast.160), calls=%async_computation.13 | async-start | bytes 4194304
  304.3 49.4 %collective-permute-start.10 = (bf16[512,1,768]{2,0,1:T(8,128)(2,1)}, bf16[512,1,768]{2,0,1:T(8,128)(2,1)}, u32[]{:S(2)}, u32[]{:S(2)}) collective-permute-start(bf16[512,1,768]{2,0,1:T(8,128)(2,1)} %get-tuple-element.43), channel_id=1, source_target_pairs={{0,4},{1,5},{2,6},{3,7},{4,0},{5,1},{6,2},{7,3},{8,12},{9,13},{10,... | collective-permute-start | bytes 2359304 | tf_op jit(solution)/shard_map/ppermute | solution.py:73
  305.8 179.7 %collective-permute-start.6 = (bf16[512,2,768]{2,0,1:T(8,128)(2,1)}, bf16[512,2,768]{2,0,1:T(8,128)(2,1)}, u32[]{:S(2)}, u32[]{:S(2)}) collective-permute-start(bf16[512,2,768]{2,0,1:T(8,128)(2,1)} %fusion.51), channel_id=1, source_target_pairs={{0,7},{1,0},{2,1},{3,2},{4,3},{5,4},{6,5},{7,6},{8,15},{9,8},{10,9... | collective-permute-start | bytes 4718600 | tf_op jit(solution)/shard_map/ppermute | solution.py:73
  320.6 166.4 %collective-permute-start = (bf16[512,2,768]{2,0,1:T(8,128)(2,1)}, bf16[512,2,768]{2,0,1:T(8,128)(2,1)}, u32[]{:S(2)}, u32[]{:S(2)}) collective-permute-start(bf16[512,2,768]{2,0,1:T(8,128)(2,1)} %get-tuple-element.34), channel_id=1, source_target_pairs={{0,1},{1,2},{2,3},{3,4},{4,5},{5,6},{6,7},{7,0},{8,9},{9,10},{10,1... | collective-permute-start | bytes 4718600 | tf_op jit(solution)/shard_map/ppermute | solution.py:73
  326.8 163.3 %copy-start.4 = (bf16[128,2,4096]{2,1,0:T(2,128)(2,1)S(1)}, bf16[128,2,4096]{2,1,0:T(2,128)(2,1)}, u32[]{:S(2)}) copy-start(bf16[128,2,4096]{2,1,0:T(2,128)(2,1)} %reshape.198) | copy-start | bytes 6291460
  326.8 163.3 %copy-start.10 = (f32[128,2]{1,0:T(8,128)S(1)}, f32[128,2]{1,0:T(8,128)}, u32[]{:S(2)}) copy-start(f32[128,2]{1,0:T(8,128)} %copy-done.9) | copy-start | bytes 3076
  326.9 298.2 %all-to-all-start.3 = ((bf16[16,32,4096]{2,1,0:T(8,128)(2,1)}), bf16[16,32,4096]{2,1,0:T(8,128)(2,1)}, u32[]{:S(2)}, u32[]{:S(2)}) async-start(bf16[16,32,4096]{2,1,0:T(8,128)(2,1)} %add_convert_fusion), calls=%async_computation.3 | async-start | bytes 8388608 | tf_op jit(solution)/shard_map/all_to_all | solution.py:124
  353.7 114.4 %collective-permute-start.9 = (bf16[512,1,768]{2,0,1:T(8,128)(2,1)}, bf16[512,1,768]{2,0,1:T(8,128)(2,1)}, u32[]{:S(2)}, u32[]{:S(2)}) collective-permute-start(bf16[512,1,768]{2,0,1:T(8,128)(2,1)} %get-tuple-element.44), channel_id=1, source_target_pairs={{0,3},{1,4},{2,5},{3,6},{4,7},{5,0},{6,1},{7,2},{8,11},{9,12},{10,... | collective-permute-start | bytes 2359304 | tf_op jit(solution)/shard_map/ppermute | solution.py:73
  353.7 114.4 %collective-permute-start.8 = (bf16[512,1,768]{2,0,1:T(8,128)(2,1)}, bf16[512,1,768]{2,0,1:T(8,128)(2,1)}, u32[]{:S(2)}, u32[]{:S(2)}) collective-permute-start(bf16[512,1,768]{2,0,1:T(8,128)(2,1)} %get-tuple-element.45), channel_id=1, source_target_pairs={{0,2},{1,3},{2,4},{3,5},{4,6},{5,7},{6,0},{7,1},{8,10},{9,11},{10,... | collective-permute-start | bytes 2359304 | tf_op jit(solution)/shard_map/ppermute | solution.py:73
  353.7 128.9 %collective-permute-start.13 = (bf16[512,1,768]{2,0,1:T(8,128)(2,1)}, bf16[512,1,768]{2,0,1:T(8,128)(2,1)}, u32[]{:S(2)}, u32[]{:S(2)}) collective-permute-start(bf16[512,1,768]{2,0,1:T(8,128)(2,1)} %get-tuple-element.46), channel_id=1, source_target_pairs={{0,7},{1,0},{2,1},{3,2},{4,3},{5,4},{6,5},{7,6},{8,15},{9,8},{10,9... | collective-permute-start | bytes 2359304 | tf_op jit(solution)/shard_map/ppermute | solution.py:73
  468.1 103.7 %collective-permute-start.1 = (bf16[512,2,768]{2,0,1:T(8,128)(2,1)}, bf16[512,2,768]{2,0,1:T(8,128)(2,1)}, u32[]{:S(2)}, u32[]{:S(2)}) collective-permute-start(bf16[512,2,768]{2,0,1:T(8,128)(2,1)} %get-tuple-element.35), channel_id=1, source_target_pairs={{0,2},{1,3},{2,4},{3,5},{4,6},{5,7},{6,0},{7,1},{8,10},{9,11},{10,... | collective-permute-start | bytes 4718600 | tf_op jit(solution)/shard_map/ppermute | solution.py:73
  468.1 103.7 %collective-permute-start.2 = (bf16[512,2,768]{2,0,1:T(8,128)(2,1)}, bf16[512,2,768]{2,0,1:T(8,128)(2,1)}, u32[]{:S(2)}, u32[]{:S(2)}) collective-permute-start(bf16[512,2,768]{2,0,1:T(8,128)(2,1)} %get-tuple-element.36), channel_id=1, source_target_pairs={{0,3},{1,4},{2,5},{3,6},{4,7},{5,0},{6,1},{7,2},{8,11},{9,12},{10,... | collective-permute-start | bytes 4718600 | tf_op jit(solution)/shard_map/ppermute | solution.py:73
  482.6 89.2 %collective-permute-start.3 = (bf16[512,2,768]{2,0,1:T(8,128)(2,1)}, bf16[512,2,768]{2,0,1:T(8,128)(2,1)}, u32[]{:S(2)}, u32[]{:S(2)}) collective-permute-start(bf16[512,2,768]{2,0,1:T(8,128)(2,1)} %get-tuple-element.37), channel_id=1, source_target_pairs={{0,4},{1,5},{2,6},{3,7},{4,0},{5,1},{6,2},{7,3},{8,12},{9,13},{10,... | collective-permute-start | bytes 4718600 | tf_op jit(solution)/shard_map/ppermute | solution.py:73
  485.5 86.2 %collective-permute-start.4 = (bf16[512,2,768]{2,0,1:T(8,128)(2,1)}, bf16[512,2,768]{2,0,1:T(8,128)(2,1)}, u32[]{:S(2)}, u32[]{:S(2)}) collective-permute-start(bf16[512,2,768]{2,0,1:T(8,128)(2,1)} %get-tuple-element.38), channel_id=1, source_target_pairs={{0,5},{1,6},{2,7},{3,0},{4,1},{5,2},{6,3},{7,4},{8,13},{9,14},{10,... | collective-permute-start | bytes 4718600 | tf_op jit(solution)/shard_map/ppermute | solution.py:73
  486.9 130.7 %collective-permute-start.5 = (bf16[512,2,768]{2,0,1:T(8,128)(2,1)}, bf16[512,2,768]{2,0,1:T(8,128)(2,1)}, u32[]{:S(2)}, u32[]{:S(2)}) collective-permute-start(bf16[512,2,768]{2,0,1:T(8,128)(2,1)} %get-tuple-element.39), channel_id=1, source_target_pairs={{0,6},{1,7},{2,0},{3,1},{4,2},{5,3},{6,4},{7,5},{8,14},{9,15},{10,... | collective-permute-start | bytes 4718600 | tf_op jit(solution)/shard_map/ppermute | solution.py:73
  635.9 7.5 %copy-start.12 = (bf16[128,16]{0,1:T(8,128)(2,1)S(1)}, bf16[128,16]{0,1:T(8,128)(2,1)}, u32[]{:S(2)}) copy-start(bf16[128,16]{0,1:T(8,128)(2,1)} %copy-done.11) | copy-start | bytes 12292

commit v4 on v2

--- a/solution.py
+++ b/solution.py
@@ -130,9 +130,10 @@
     gate_part = jnp.einsum("nkd,nkh->dh", received, grad_gate, preferred_element_type=jnp.float32)
     up_part = jnp.einsum("nkd,nkh->dh", received, grad_up, preferred_element_type=jnp.float32)
     down_part = jnp.einsum("nkd,nkh->dh", grad_recv, hidden, preferred_element_type=jnp.float32)
-    gate_total, up_total, down_total = reduce_scatter_by_exchange(
-        (gate_part, up_part, down_part), "dp"
-    )
+    down_total = lax.psum_scatter(
+        down_part.astype(jnp.bfloat16), "dp", scatter_dimension=0, tiled=True
+    ).astype(jnp.float32)
+    gate_total, up_total = reduce_scatter_by_exchange((gate_part, up_part), "dp")
     gate_grad = (gate_total / replica_count).astype(jnp.bfloat16)[None]
     up_grad = (up_total / replica_count).astype(jnp.bfloat16)[None]
     down_grad = (down_total / replica_count).astype(jnp.bfloat16)[None]

time: 603 us -> 617 us (1.023)
  the two profiles are of different devices: /device:TPU:20 before, /device:TPU:4 now
where the time goes in v4:
time: 617 us; the launch traced here: 609 us
  waiting for transfers between devices  329 us (53%)
  matrix products  65.7 us (11%)
  blocking collectives  56.9 us (9%)
  starting transfers between devices  54.7 us (9%)
  local copies, waits for them, and re-layouts  51.7 us (8%)
  other arithmetic  35.9 us (6%)
  between operations  14.7 us (2%)
    all_to_all x1, waiting for transfers between devices, reduce_scatter_by_exchange(): arrived = lax.all_to_all(blocks, axis, 0, 0, tiled=True)  187 us
    all_to_all x1, blocking collectives, on_device(): lax.all_to_all(outbound, 'expert', split_axis=0, concat_axis=0, tiled=True)  56.9 us
    all_to_all x1, waiting for transfers between devices, on_device(): lax.all_to_all(grad_out, 'expert', split_axis=0, concat_axis=0, tiled=True)  54.1 us
    all_to_all x1, waiting for transfers between devices, on_device(): lax.all_to_all(grad_in, 'expert', split_axis=0, concat_axis=0, tiled=True)  44.9 us
    all_to_all x1, waiting for transfers between devices, on_device(): lax.all_to_all(expert_out, 'expert', split_axis=0, concat_axis=0, tiled=T...  41.2 us
    all_to_all x1, starting transfers between devices, all_reduce_by_exchange(): lax.all_to_all(chunks, axes, 0, 0, tiled=True)  13.7 us
    all_to_all x1, starting transfers between devices, all_reduce_by_exchange(): return lax.all_to_all(spread, axes, 0, 0, tiled=True).reshape(part.shape)  12.8 us
  transfers between devices with their start and end apart: 7, of which 5 were waited for; matrix products, arithmetic and copies ran while one was open for 17% of the time, Pallas kernels for 0%

profile of v4, /device:TPU:4, one launch (start us, length us, event | category | flops | bytes accessed | tf_op | source)
XLA Modules:
  0.0 608.9 jit_solution(7216675021431735035)
XLA Ops:
  7.2 0.7 broadcast_multiply_fusion
  7.9 0.8 copy.62
  8.7 0.1 eq.42
  8.8 0.1 eq.38
  9.0 0.1 copy.61
  9.1 0.1 mul.95
  9.2 0.6 reduce-window.6
  9.8 0.2 slice_reduce_fusion
  10.2 1.4 scatter_custom_fusion
  11.6 1.3 concatenate.7
  12.9 4.4 gather_fusion
  17.3 56.9 %all_to_all.41 = bf16[16,32,4096]{2,1,0:T(8,128)(2,1)S(1)} all-to-all(bf16[16,32,4096]{2,1,0:T(8,128)(2,1)} %bitcast.104), channel_id=1, replica_groups=mesh['expert'=16,'dp'=8] {'expert'}, dimensions={0} | all-to-all | bytes 8388608 | tf_op jit(solution)/shard_map/all_to_all | solution.py:90
  74.2 7.1 %fusion.10 = f32[16,32,768]{2,1,0:T(8,128)S(1)} fusion(bf16[16,32,4096]{2,1,0:T(8,128)(2,1)S(1)} %all_to_all.41, bf16[1,4096,768]{2,1,0:T(8,128)(2,1)} %param.11), kind=kOutput, calls=%fused_computation.22 | convolution fusion | flops 3221225472 | bytes 12058624 | tf_op jit(solution)/shard_map/...d,dh->...h/dot_general | solution.py:31
  81.3 4.6 multiply_convert_fusion.4
  86.0 5.0 fusion.12
  91.0 7.6 %all-to-all-start.1 = ((bf16[16,32,4096]{2,1,0:T(8,128)(2,1)}), bf16[16,32,4096]{2,1,0:T(8,128)(2,1)}, u32[]{:S(2)}, u32[]{:S(2)}) async-start(bf16[16,32,4096]{2,1,0:T(8,128)(2,1)} %fusion.12), calls=%async_computation.1 | async-start | bytes 8388608 | tf_op jit(solution)/shard_map/all_to_all | solution.py:99
  98.7 0.1 reshape.202
  98.9 0.4 fusion.39
  99.3 2.0 gather_fusion.4
  101.3 0.1 reshape.205
  101.5 4.1 mul.102
  105.5 6.0 mul.103
  111.6 41.2 %all-to-all-done.1 = bf16[16,32,4096]{2,1,0:T(8,128)(2,1)} async-done(((bf16[16,32,4096]{2,1,0:T(8,128)(2,1)}), bf16[16,32,4096]{2,1,0:T(8,128)(2,1)}, u32[]{:S(2)}, u32[]{:S(2)}) %all-to-all-start.1) | async-done | bytes 4194336 | tf_op jit(solution)/shard_map/all_to_all | solution.py:99
  152.8 6.6 %gather_fusion.1 = bf16[256,4096]{1,0:T(8,128)(2,1)S(1)} fusion(bf16[512,4096]{1,0:T(8,128)(2,1)} %bitcast.11, s32[1024]{0:T(1024)S(1)} %pad_clamp_fusion.1), kind=kCustom, calls=%fused_computation.1 | custom fusion | bytes 4195328 | tf_op jit(solution)/shard_map/gather | solution.py:102
  159.4 2.7 reshape.166
  162.1 7.3 %fusion.18 = f32[128,1,2]{2,1,0:T(1,128)S(1)} fusion(bf16[128,2,4096]{2,1,0:T(2,128)(2,1)} %reshape.166, bf16[128,4096,1]{1,0,2:T(8,128)(2,1)} %bitcast.107), kind=kOutput, calls=%fused_computation.30 | convolution fusion | flops 2097152 | bytes 3146752 | tf_op jit(solution)/shard_map/td,tkd->tk/dot_general | solution.py:106
  169.5 0.1 copy.60
  169.7 0.1 mul.100
  169.8 0.4 copy-done.6
  170.3 0.3 convolution_bitcast_fusion
  170.5 0.6 copy.66
  171.1 1.5 all_to_all.33
  172.6 13.7 %all-to-all-start.4 = ((f32[128,1,512]{2,1,0:T(1,128)}), f32[128,1,512]{2,1,0:T(1,128)S(1)}, u32[]{:S(2)}, u32[]{:S(2)}) async-start(f32[128,1,512]{2,1,0:T(1,128)} %all_to_all.33), calls=%async_computation.4 | async-start | bytes 524288 | tf_op jit(solution)/shard_map/all_to_all | solution.py:58
  186.3 2.6 multiply_convert_fusion
  189.0 0.3 concatenate.8
  189.2 4.4 gather_fusion.2
  193.6 1.9 all-to-all-done.4
  195.6 7.2 %all-to-all-start.2 = ((bf16[16,32,4096]{2,1,0:T(8,128)(2,1)}), bf16[16,32,4096]{2,1,0:T(8,128)(2,1)}, u32[]{:S(2)}, u32[]{:S(2)}) async-start(bf16[16,32,4096]{2,1,0:T(8,128)(2,1)} %bitcast.103), calls=%async_computation.2 | async-start | bytes 8388608 | tf_op jit(solution)/shard_map/all_to_all | solution.py:119
  202.8 0.2 reduce_sum.81
  203.0 54.1 %all-to-all-done.2 = bf16[16,32,4096]{2,1,0:T(8,128)(2,1)} async-done(((bf16[16,32,4096]{2,1,0:T(8,128)(2,1)}), bf16[16,32,4096]{2,1,0:T(8,128)(2,1)}, u32[]{:S(2)}, u32[]{:S(2)}) %all-to-all-start.2) | async-done | bytes 4194336 | tf_op jit(solution)/shard_map/all_to_all | solution.py:119
  257.1 0.8 broadcast_in_dim.18
  258.0 12.8 %all-to-all-start.5 = ((f32[128,1,512]{2,1,0:T(1,128)}), f32[128,1,512]{2,1,0:T(1,128)S(1)}, u32[]{:S(2)}, u32[]{:S(2)}) async-start(f32[128,1,512]{2,1,0:T(1,128)} %broadcast_in_dim.18), calls=%async_computation.5 | async-start | bytes 524288 | tf_op jit(solution)/shard_map/all_to_all | solution.py:60
  270.9 8.4 %bitcast_convert_fusion = bf16[4096,768]{1,0:T(8,128)(2,1)} fusion(bf16[16,32,4096]{2,1,0:T(8,128)(2,1)} %all-to-all-done.2, bf16[16,32,768]{2,1,0:T(8,128)(2,1)S(1)} %copy-done.15), kind=kOutput, calls=%fused_computation.8 | convolution fusion | flops 3224371200 | bytes 11272192 | tf_op jit(solution)/shard_map/nkd,nkh->dh/dot_general | solution.py:132
  279.3 9.6 %multiply_convert_fusion.3 = (bf16[16,32,768]{2,1,0:T(8,128)(2,1)}, bf16[16,32,768]{2,1,0:T(8,128)(2,1)S(1)}) fusion(f32[16,32,768]{2,1,0:T(8,128)} %copy-done.13, f32[16,32,768]{2,1,0:T(8,128)} %get-tuple-element.41, bf16[16,32,4096]{2,1,0:T(8,128)(2,1)} %all-to-all-done.2, bf16[1,4096,768]{2,1,0:T(8,128)(2,1)} %param.13), kind=kOutput, calls=%fused_computation.38 | convolution fusion | flops 3226337280 | bytes 15204352 | tf_op jit(solution)/shard_map/...d,dh->...h/dot_general | solution.py:42
  288.9 3.5 fusion.4
  292.4 8.6 %add_convert_fusion = bf16[16,32,4096]{2,1,0:T(8,128)(2,1)} fusion(f32[16,32,4096]{2,1,0:T(8,128)S(1)} %fusion.4, bf16[16,32,768]{2,1,0:T(8,128)(2,1)} %get-tuple-element.36, bf16[1,4096,768]{2,1,0:T(8,128)(2,1)} %param.11), kind=kOutput, calls=%fused_computation.11 | convolution fusion | flops 3225419776 | bytes 19660800 | tf_op jit(solution)/shard_map/...h,dh->...d/dot_general | solution.py:48
  301.0 7.9 %all-to-all-start.3 = ((bf16[16,32,4096]{2,1,0:T(8,128)(2,1)}), bf16[16,32,4096]{2,1,0:T(8,128)(2,1)}, u32[]{:S(2)}, u32[]{:S(2)}) async-start(bf16[16,32,4096]{2,1,0:T(8,128)(2,1)} %add_convert_fusion), calls=%async_computation.3 | async-start | bytes 8388608 | tf_op jit(solution)/shard_map/all_to_all | solution.py:121
  308.9 5.8 bitcast_convert_fusion.2
  314.8 3.8 bitcast_convert_fusion.1
  318.6 5.7 pad_maximum_fusion
  324.3 44.9 %all-to-all-done.3 = bf16[16,32,4096]{2,1,0:T(8,128)(2,1)} async-done(((bf16[16,32,4096]{2,1,0:T(8,128)(2,1)}), bf16[16,32,4096]{2,1,0:T(8,128)(2,1)}, u32[]{:S(2)}, u32[]{:S(2)}) %all-to-all-start.3) | async-done | bytes 4194336 | tf_op jit(solution)/shard_map/all_to_all | solution.py:121
  369.2 5.4 all-to-all-start.6
  374.6 7.5 %multiply_reduce_fusion = bf16[128,4096]{1,0:T(8,128)(2,1)} fusion(bf16[128,2,4096]{2,1,0:T(2,128)(2,1)S(1)} %copy-done.2, f32[128,2]{1,0:T(8,128)S(1)} %copy.60), kind=kLoop, calls=%fused_computation.29 | loop fusion | flops 2621440 | bytes 3146752 | tf_op jit(solution)/shard_map/reduce_sum | solution.py:103
  382.1 0.7 multiply_reduce_fusion.1
  382.8 0.7 div.45
  383.5 1.3 copy.70
  384.8 6.9 %gather_fusion.3 = bf16[256,4096]{1,0:T(8,128)(2,1)S(1)} fusion(bf16[512,4096]{1,0:T(8,128)(2,1)} %bitcast.13, s32[1024]{0:T(1024)} %copy-done.9), kind=kCustom, calls=%fused_computation.3 | custom fusion | bytes 4195328 | tf_op jit(solution)/shard_map/gather | solution.py:125
  391.7 4.0 reshape.169
  395.7 7.5 %reduce_sum.78 = f32[128,4096]{1,0:T(8,128)S(1)} reduce(f32[128,2,4096]{2,1,0:T(2,128)} %reshape.169, f32[]{:T(128)} %constant.56.clone.1), dimensions={1}, to_apply=%region_6.7 | reduce | flops 524288 | bytes 6291460 | tf_op jit(solution)/shard_map/reduce_sum | solution.py:124
  403.2 1.4 fusion.17
  404.7 187.0 %all-to-all-done.6 = bf16[8,512,2,768]{3,1,2,0:T(8,128)(2,1)} async-done(((bf16[8,512,2,768]{3,1,2,0:T(8,128)(2,1)}), bf16[8,512,2,768]{3,1,2,0:T(8,128)(2,1)}, u32[]{:S(2)}, u32[]{:S(2)}) %all-to-all-start.6) | async-done | bytes 12582944 | tf_op jit(solution)/shard_map/all_to_all | solution.py:69
  591.7 6.6 %convert_reduce_fusion = f32[512,2,768]{2,0,1:T(8,128)S(1)} fusion(bf16[8,512,2,768]{3,1,2,0:T(8,128)(2,1)} %all-to-all-done.6), kind=kLoop, calls=%fused_computation.6 | loop fusion | flops 11796480 | bytes 15728640 | tf_op jit(solution)/shard_map/reduce_sum | solution.py:70
  598.3 1.4 fusion.25
  599.7 2.1 fusion.23
  (67 shorter events, 0.7 us)
Async XLA Ops:
  7.2 91.7 %copy-start = (bf16[4096,16]{0,1:T(8,128)(2,1)S(1)}, bf16[4096,16]{0,1:T(8,128)(2,1)}, u32[]{:S(2)}) copy-start(bf16[4096,16]{0,1:T(8,128)(2,1)} %param.10) | copy-start | bytes 393220
  17.3 64.0 %slice-start.2 = ((s8[6291456]{0:T(1024)(128)(4,1)}), s8[4194304]{0:T(1024)(128)(4,1)S(1)}, s32[]{:S(2)}) async-start(s8[6291456]{0:T(1024)(128)(4,1)} %bitcast.113), calls=%async_computation.11 | async-start | bytes 8388608
  74.2 7.1 %copy-start.3 = (bf16[16,32,4096]{2,1,0:T(8,128)(2,1)}, bf16[16,32,4096]{2,1,0:T(8,128)(2,1)S(1)}, u32[]{:S(2)}) copy-start(bf16[16,32,4096]{2,1,0:T(8,128)(2,1)S(1)} %all_to_all.41) | copy-start | bytes 12582916
  74.2 7.1 %slice-start.3 = ((s8[6291456]{0:T(1024)(128)(4,1)}), s8[2097152]{0:T(1024)(128)(4,1)S(1)}, s32[]{:S(2)}) async-start(s8[6291456]{0:T(1024)(128)(4,1)} %bitcast.113), calls=%async_computation.12 | async-start | bytes 4194304
  74.2 11.7 %slice-start = ((s8[6291456]{0:T(1024)(128)(4,1)}), s8[4194304]{0:T(1024)(128)(4,1)S(1)}, s32[]{:S(2)}) async-start(s8[6291456]{0:T(1024)(128)(4,1)} %bitcast.111), calls=%async_computation.9 | async-start | bytes 8388608
  81.3 4.6 copy-start.13
  81.3 4.6 slice-start.1
  85.9 5.0 copy-start.14
  91.0 7.6 %copy-start.8 = (s32[128,2]{0,1:T(2,128)S(1)}, s32[128,2]{0,1:T(2,128)}, u32[]{:S(2)}) copy-start(s32[128,2]{0,1:T(2,128)} %param.9) | copy-start | bytes 3076
  91.0 7.9 %copy-start.1 = (bf16[128,4096]{1,0:T(8,128)(2,1)S(1)}, bf16[128,4096]{1,0:T(8,128)(2,1)}, u32[]{:S(2)}) copy-start(bf16[128,4096]{1,0:T(8,128)(2,1)} %param.7) | copy-start | bytes 3145732
  91.0 61.8 %all-to-all-start.1 = ((bf16[16,32,4096]{2,1,0:T(8,128)(2,1)}), bf16[16,32,4096]{2,1,0:T(8,128)(2,1)}, u32[]{:S(2)}, u32[]{:S(2)}) async-start(bf16[16,32,4096]{2,1,0:T(8,128)(2,1)} %fusion.12), calls=%async_computation.1 | async-start | bytes 8388608 | tf_op jit(solution)/shard_map/all_to_all | solution.py:99
  99.3 2.2 copy-start.5
  111.6 47.8 %copy-start.9 = (s32[1024]{0:T(1024)}, s32[1024]{0:T(1024)S(1)}, u32[]{:S(2)}) copy-start(s32[1024]{0:T(1024)S(1)} %pad_clamp_fusion.1) | copy-start | bytes 12292
  169.7 0.6 copy-start.6
  172.6 23.0 %all-to-all-start.4 = ((f32[128,1,512]{2,1,0:T(1,128)}), f32[128,1,512]{2,1,0:T(1,128)S(1)}, u32[]{:S(2)}, u32[]{:S(2)}) async-start(f32[128,1,512]{2,1,0:T(1,128)} %all_to_all.33), calls=%async_computation.4 | async-start | bytes 524288 | tf_op jit(solution)/shard_map/all_to_all | solution.py:58
  195.6 75.3 %copy-start.15 = (bf16[16,32,768]{2,1,0:T(8,128)(2,1)S(1)}, bf16[16,32,768]{2,1,0:T(8,128)(2,1)}, u32[]{:S(2)}) copy-start(bf16[16,32,768]{2,1,0:T(8,128)(2,1)} %copy-done.14) | copy-start | bytes 2359300
  195.6 61.5 %all-to-all-start.2 = ((bf16[16,32,4096]{2,1,0:T(8,128)(2,1)}), bf16[16,32,4096]{2,1,0:T(8,128)(2,1)}, u32[]{:S(2)}, u32[]{:S(2)}) async-start(bf16[16,32,4096]{2,1,0:T(8,128)(2,1)} %bitcast.103), calls=%async_computation.2 | async-start | bytes 8388608 | tf_op jit(solution)/shard_map/all_to_all | solution.py:119
  258.0 43.0 %all-to-all-start.5 = ((f32[128,1,512]{2,1,0:T(1,128)}), f32[128,1,512]{2,1,0:T(1,128)S(1)}, u32[]{:S(2)}, u32[]{:S(2)}) async-start(f32[128,1,512]{2,1,0:T(1,128)} %broadcast_in_dim.18), calls=%async_computation.5 | async-start | bytes 524288 | tf_op jit(solution)/shard_map/all_to_all | solution.py:60
  270.8 328.9 %reduce-scatter.2.cloned.1.call-start = ((), (), s32[]{:S(2)}) async-start(), calls=%async_computation.8 | async-start | bytes 7077888 | tf_op jit(solution)/shard_map/reduce_scatter | solution.py:133
  279.2 9.7 %slice-start.4 = ((s8[6291456]{0:T(1024)(128)(4,1)}), s8[2097152]{0:T(1024)(128)(4,1)S(1)}, s32[]{:S(2)}) async-start(s8[6291456]{0:T(1024)(128)(4,1)} %bitcast.115), calls=%async_computation.13 | async-start | bytes 4194304
  279.3 9.7 %slice-start.5 = ((s8[6291456]{0:T(1024)(128)(4,1)}), s8[4194304]{0:T(1024)(128)(4,1)S(1)}, s32[]{:S(2)}) async-start(s8[6291456]{0:T(1024)(128)(4,1)} %bitcast.115), calls=%async_computation.14 | async-start | bytes 8388608
  288.9 3.5 copy-start.11
  301.0 7.9 %copy-start.10 = (bf16[16,32,768]{2,1,0:T(8,128)(2,1)S(1)}, bf16[16,32,768]{2,1,0:T(8,128)(2,1)}, u32[]{:S(2)}) copy-start(bf16[16,32,768]{2,1,0:T(8,128)(2,1)} %get-tuple-element.36) | copy-start | bytes 2359300
  301.0 68.2 %all-to-all-start.3 = ((bf16[16,32,4096]{2,1,0:T(8,128)(2,1)}), bf16[16,32,4096]{2,1,0:T(8,128)(2,1)}, u32[]{:S(2)}, u32[]{:S(2)}) async-start(bf16[16,32,4096]{2,1,0:T(8,128)(2,1)} %add_convert_fusion), calls=%async_computation.3 | async-start | bytes 8388608 | tf_op jit(solution)/shard_map/all_to_all | solution.py:121
  308.9 5.9 copy-start.4
  308.9 5.9 copy-start.12
  324.3 50.3 %copy-start.2 = (bf16[128,2,4096]{2,1,0:T(2,128)(2,1)S(1)}, bf16[128,2,4096]{2,1,0:T(2,128)(2,1)}, u32[]{:S(2)}) copy-start(bf16[128,2,4096]{2,1,0:T(2,128)(2,1)} %reshape.166) | copy-start | bytes 6291460
  369.2 222.5 %all-to-all-start.6 = ((bf16[8,512,2,768]{3,1,2,0:T(8,128)(2,1)}), bf16[8,512,2,768]{3,1,2,0:T(8,128)(2,1)}, u32[]{:S(2)}, u32[]{:S(2)}) async-start(bf16[8,512,2,768]{3,1,2,0:T(8,128)(2,1)} %pad_maximum_fusion), calls=%async_computation.6 | async-start | bytes 25165824 | tf_op jit(solution)/shard_map/all_to_all | solution.py:69
  395.7 7.5 %copy-start.7 = (bf16[128,16]{0,1:T(8,128)(2,1)S(1)}, bf16[128,16]{0,1:T(8,128)(2,1)}, u32[]{:S(2)}) copy-start(bf16[128,16]{0,1:T(8,128)(2,1)} %copy-done.6) | copy-start | bytes 12292
Sparse Core Ops, SparseCore 0:
  279.4 253.1 reduce-scatter.1

commit v5 on v4

--- a/solution.py
+++ b/solution.py
@@ -88,14 +88,14 @@
         expert_count, capacity, feature_count
     )
     received = lax.all_to_all(outbound, "expert", split_axis=0, concat_axis=0, tiled=True)
+    weighted = (route_probs[:, :, None] * cotangent[:, None, :].astype(jnp.float32)).astype(
+        jnp.bfloat16
+    )
+    weighted = weighted.reshape(row_count * top_count, feature_count)
+    grad_out = padded_rows(weighted, owners).reshape(expert_count, capacity, feature_count)
+    grad_recv = lax.all_to_all(grad_out, "expert", split_axis=0, concat_axis=0, tiled=True)
     expert_out, hidden, gate_pre, up_pre = expert_forward(received, expert_weights)
-    received, expert_out, hidden, gate_pre, up_pre = (
-        received,
-        expert_out,
-        hidden,
-        gate_pre,
-        up_pre,
-    )
+    expert_out, grad_recv = lax.optimization_barrier((expert_out, grad_recv))
     returned = lax.all_to_all(
         expert_out, "expert", split_axis=0, concat_axis=0, tiled=True
     ).reshape(slot_count, feature_count)
@@ -111,12 +111,6 @@
     grad_logits = jnp.sum(grad_chosen[:, :, None] * match, axis=1).astype(jnp.bfloat16)
     router_part = jnp.dot(tokens.T, grad_logits, preferred_element_type=jnp.float32)
     router_grad = all_reduce_by_exchange(router_part, ("expert", "dp")) / replica_count
-    weighted = (route_probs[:, :, None] * cotangent[:, None, :].astype(jnp.float32)).astype(
-        jnp.bfloat16
-    )
-    weighted = weighted.reshape(row_count * top_count, feature_count)
-    grad_out = padded_rows(weighted, owners).reshape(expert_count, capacity, feature_count)
-    grad_recv = lax.all_to_all(grad_out, "expert", split_axis=0, concat_axis=0, tiled=True)
     grad_in, grad_gate, grad_up = expert_backward(grad_recv, gate_pre, up_pre, expert_weights)
     grad_back = lax.all_to_all(grad_in, "expert", split_axis=0, concat_axis=0, tiled=True).reshape(
         slot_count, feature_count

time: 617 us -> 539 us (0.87)
  waiting for transfers between devices: 329 us -> 269 us
  blocking collectives: 56.9 us -> 0 us
  matrix products: 65.7 us -> 81.4 us
  starting transfers between devices: 54.7 us -> 69.5 us
    all_to_all x1, waiting for transfers between devices: 187 us -> 129 us  [reduce_scatter_by_exchange(): arrived = lax.all_to_all(blocks, axis, 0, 0, tiled=True)]
    all_to_all x1 -> x0, blocking collectives: 56.9 us -> none  [on_device(): lax.all_to_all(outbound, 'expert', split_axis=0, concat_axis=0, tiled=True)]
    all_to_all x0 -> x1, waiting for transfers between devices: none -> 33.7 us  [on_device(): lax.all_to_all(outbound, 'expert', split_axis=0, concat_axis=0, tiled=True)]
    all_to_all x1, waiting for transfers between devices: 54.1 us -> 33.6 us  [on_device(): lax.all_to_all(grad_out, 'expert', split_axis=0, concat_axis=0, tiled=True)]
    all_to_all x1, waiting for transfers between devices: 41.2 us -> 29.3 us  [on_device(): lax.all_to_all(expert_out, 'expert', split_axis=0, concat_axis=0, tiled=T...]
    all_to_all x0 -> x1, starting transfers between devices: none -> 7.58 us  [on_device(): lax.all_to_all(outbound, 'expert', split_axis=0, concat_axis=0, tiled=True)]
  transfers between devices with their start and end apart: 7 -> 8, of which waited for: 5 -> 5; matrix products, arithmetic and copies ran while one was open for 17% -> 30% of each run, Pallas kernels for 0% -> 0%
where the time goes in v5:
time: 539 us; the launch traced here: 531 us
  waiting for transfers between devices  269 us (50%)
  matrix products  81.4 us (15%)
  starting transfers between devices  69.5 us (13%)
  local copies, waits for them, and re-layouts  54.5 us (10%)
  other arithmetic  41.6 us (8%)
  between operations  14.9 us (3%)
    all_to_all x1, waiting for transfers between devices, reduce_scatter_by_exchange(): arrived = lax.all_to_all(blocks, axis, 0, 0, tiled=True)  129 us
    all_to_all x1, waiting for transfers between devices, on_device(): lax.all_to_all(grad_in, 'expert', split_axis=0, concat_axis=0, tiled=True)  43.5 us
    all_to_all x1, waiting for transfers between devices, on_device(): lax.all_to_all(outbound, 'expert', split_axis=0, concat_axis=0, tiled=True)  33.7 us
    all_to_all x1, waiting for transfers between devices, on_device(): lax.all_to_all(grad_out, 'expert', split_axis=0, concat_axis=0, tiled=True)  33.6 us
    all_to_all x1, waiting for transfers between devices, on_device(): lax.all_to_all(expert_out, 'expert', split_axis=0, concat_axis=0, tiled=T...  29.3 us
    all_to_all x1, starting transfers between devices, all_reduce_by_exchange(): lax.all_to_all(chunks, axes, 0, 0, tiled=True)  15.4 us
    all_to_all x1, starting transfers between devices, on_device(): lax.all_to_all(grad_out, 'expert', split_axis=0, concat_axis=0, tiled=True)  12.6 us
    all_to_all x1, starting transfers between devices, on_device(): lax.all_to_all(expert_out, 'expert', split_axis=0, concat_axis=0, tiled=T...  11.8 us
  transfers between devices with their start and end apart: 8, of which 5 were waited for; matrix products, arithmetic and copies ran while one was open for 30% of the time, Pallas kernels for 0%

profile of v5, /device:TPU:4, one launch (start us, length us, event | category | flops | bytes accessed | tf_op | source)
XLA Modules:
  0.0 530.7 jit_solution(13665422425495284216)
XLA Ops:
  7.2 0.7 broadcast_multiply_fusion
  7.9 0.8 copy.62
  8.7 0.1 eq.42
  8.8 0.1 eq.38
  9.1 0.1 mul.95
  9.2 0.6 reduce-window.6
  9.8 0.2 slice_reduce_fusion
  10.2 1.4 scatter_custom_fusion
  11.6 1.3 concatenate.7
  12.9 4.4 gather_fusion
  17.3 7.6 %all-to-all-start = ((bf16[16,32,4096]{2,1,0:T(8,128)(2,1)}), bf16[16,32,4096]{2,1,0:T(8,128)(2,1)}, u32[]{:S(2)}, u32[]{:S(2)}) async-start(bf16[16,32,4096]{2,1,0:T(8,128)(2,1)} %bitcast.103), calls=%async_computation | async-start | bytes 8388608 | tf_op jit(solution)/shard_map/all_to_all | solution.py:90
  25.0 0.1 reshape.202
  25.2 0.4 fusion.39
  25.6 2.0 gather_fusion.4
  27.9 0.1 mul.99
  28.1 4.1 mul.101
  32.2 6.0 %mul.102 = f32[256,4096]{1,0:T(8,128)} reshape(f32[128,2,4096]{2,1,0:T(2,128)} %mul.101) | data formatting | bytes 8388608 | tf_op jit(solution)/shard_map/mul | solution.py:91
  38.2 2.6 multiply_convert_fusion
  40.9 0.3 concatenate.8
  41.1 4.4 gather_fusion.1
  45.6 33.7 %all-to-all-done = bf16[16,32,4096]{2,1,0:T(8,128)(2,1)} async-done(((bf16[16,32,4096]{2,1,0:T(8,128)(2,1)}), bf16[16,32,4096]{2,1,0:T(8,128)(2,1)}, u32[]{:S(2)}, u32[]{:S(2)}) %all-to-all-start) | async-done | bytes 4194336 | tf_op jit(solution)/shard_map/all_to_all | solution.py:90
  79.2 12.6 %all-to-all-start.1 = ((bf16[16,32,4096]{2,1,0:T(8,128)(2,1)}), bf16[16,32,4096]{2,1,0:T(8,128)(2,1)}, u32[]{:S(2)}, u32[]{:S(2)}) async-start(bf16[16,32,4096]{2,1,0:T(8,128)(2,1)} %bitcast.104), calls=%async_computation.1 | async-start | bytes 8388608 | tf_op jit(solution)/shard_map/all_to_all | solution.py:96
  91.8 7.2 %fusion.10 = f32[16,32,768]{2,1,0:T(8,128)S(1)} fusion(bf16[16,32,4096]{2,1,0:T(8,128)(2,1)} %all-to-all-done, bf16[1,4096,768]{2,1,0:T(8,128)(2,1)} %param.11), kind=kOutput, calls=%fused_computation.22 | convolution fusion | flops 3221225472 | bytes 12058624 | tf_op jit(solution)/shard_map/...d,dh->...h/dot_general | solution.py:31
  99.1 7.4 %multiply_convert_fusion.4 = (bf16[16,32,768]{2,1,0:T(8,128)(2,1)S(1)}, f32[16,32,768]{2,1,0:T(8,128)}) fusion(f32[16,32,768]{2,1,0:T(8,128)S(1)} %fusion.10, bf16[16,32,4096]{2,1,0:T(8,128)(2,1)} %all-to-all-done, bf16[1,4096,768]{2,1,0:T(8,128)(2,1)S(1)} %bitcast.114), kind=kOutput, calls=%fused_computation.39 | convolution fusion | flops 3223584768 | bytes 14417920 | tf_op jit(solution)/shard_map/...d,dh->...h/dot_general | solution.py:32
  106.5 0.9 copy-done.11
  107.4 5.0 fusion.12
  112.4 33.6 %all-to-all-done.1 = bf16[16,32,4096]{2,1,0:T(8,128)(2,1)} async-done(((bf16[16,32,4096]{2,1,0:T(8,128)(2,1)}), bf16[16,32,4096]{2,1,0:T(8,128)(2,1)}, u32[]{:S(2)}, u32[]{:S(2)}) %all-to-all-start.1) | async-done | bytes 4194336 | tf_op jit(solution)/shard_map/all_to_all | solution.py:96
  146.0 11.8 %all-to-all-start.2 = ((bf16[16,32,4096]{2,1,0:T(8,128)(2,1)}), bf16[16,32,4096]{2,1,0:T(8,128)(2,1)}, u32[]{:S(2)}, u32[]{:S(2)}) async-start(bf16[16,32,4096]{2,1,0:T(8,128)(2,1)} %fusion.12), calls=%async_computation.2 | async-start | bytes 8388608 | tf_op jit(solution)/shard_map/all_to_all | solution.py:99
  157.8 0.3 reduce-scatter.2.cloned.1.call-start
  158.1 8.4 %bitcast_convert_fusion = bf16[4096,768]{1,0:T(8,128)(2,1)} fusion(bf16[16,32,4096]{2,1,0:T(8,128)(2,1)} %all-to-all-done.1, bf16[16,32,768]{2,1,0:T(8,128)(2,1)S(1)} %copy-done.12), kind=kOutput, calls=%fused_computation.8 | convolution fusion | flops 3224371200 | bytes 11272192 | tf_op jit(solution)/shard_map/nkd,nkh->dh/dot_general | solution.py:126
  166.5 9.6 %multiply_convert_fusion.3 = (bf16[16,32,768]{2,1,0:T(8,128)(2,1)}, bf16[16,32,768]{2,1,0:T(8,128)(2,1)S(1)}) fusion(f32[16,32,768]{2,1,0:T(8,128)} %copy-done.10, f32[16,32,768]{2,1,0:T(8,128)} %get-tuple-element.43, bf16[16,32,4096]{2,1,0:T(8,128)(2,1)} %all-to-all-done.1, bf16[1,4096,768]{2,1,0:T(8,128)(2,1)} %param.13), kind=kOutput, calls=%fused_computation.38 | convolution fusion | flops 3226337280 | bytes 15204352 | tf_op jit(solution)/shard_map/...d,dh->...h/dot_general | solution.py:42
  176.2 0.9 copy-done.8
  177.0 6.2 %fusion.4 = f32[16,32,4096]{2,1,0:T(8,128)} fusion(bf16[16,32,768]{2,1,0:T(8,128)(2,1)S(1)} %get-tuple-element.39, bf16[1,4096,768]{2,1,0:T(8,128)(2,1)S(1)} %bitcast.116), kind=kOutput, calls=%fused_computation.16 | convolution fusion | flops 3221225472 | bytes 15466496 | tf_op jit(solution)/shard_map/...h,dh->...d/dot_general | solution.py:49
  183.2 29.3 %all-to-all-done.2 = bf16[16,32,4096]{2,1,0:T(8,128)(2,1)} async-done(((bf16[16,32,4096]{2,1,0:T(8,128)(2,1)}), bf16[16,32,4096]{2,1,0:T(8,128)(2,1)}, u32[]{:S(2)}, u32[]{:S(2)}) %all-to-all-start.2) | async-done | bytes 4194336 | tf_op jit(solution)/shard_map/all_to_all | solution.py:99
  212.5 6.6 %gather_fusion.2 = bf16[256,4096]{1,0:T(8,128)(2,1)S(1)} fusion(bf16[512,4096]{1,0:T(8,128)(2,1)} %bitcast.12, s32[1024]{0:T(1024)S(1)} %pad_clamp_fusion), kind=kCustom, calls=%fused_computation.2 | custom fusion | bytes 4195328 | tf_op jit(solution)/shard_map/gather | solution.py:102
  219.1 2.7 reshape.167
  221.8 7.3 %fusion.18 = f32[128,1,2]{2,1,0:T(1,128)S(1)} fusion(bf16[128,2,4096]{2,1,0:T(2,128)(2,1)} %reshape.167, bf16[128,4096,1]{1,0,2:T(8,128)(2,1)} %bitcast.107), kind=kOutput, calls=%fused_computation.30 | convolution fusion | flops 2097152 | bytes 3146752 | tf_op jit(solution)/shard_map/td,tkd->tk/dot_general | solution.py:106
  229.2 1.0 convolution_bitcast_fusion
  230.2 1.5 copy.66
  231.8 1.5 all_to_all.33
  233.2 15.4 %all-to-all-start.4 = ((f32[128,1,512]{2,1,0:T(1,128)}), f32[128,1,512]{2,1,0:T(1,128)S(1)}, u32[]{:S(2)}, u32[]{:S(2)}) async-start(f32[128,1,512]{2,1,0:T(1,128)} %all_to_all.33), calls=%async_computation.4 | async-start | bytes 524288 | tf_op jit(solution)/shard_map/all_to_all | solution.py:58
  248.7 10.8 %add_convert_fusion = bf16[16,32,4096]{2,1,0:T(8,128)(2,1)} fusion(f32[16,32,4096]{2,1,0:T(8,128)} %fusion.4, bf16[16,32,768]{2,1,0:T(8,128)(2,1)} %get-tuple-element.38, bf16[1,4096,768]{2,1,0:T(8,128)(2,1)} %param.11), kind=kOutput, calls=%fused_computation.11 | convolution fusion | flops 3225419776 | bytes 19660800 | tf_op jit(solution)/shard_map/...h,dh->...d/dot_general | solution.py:48
  259.5 7.4 %all-to-all-start.3 = ((bf16[16,32,4096]{2,1,0:T(8,128)(2,1)}), bf16[16,32,4096]{2,1,0:T(8,128)(2,1)}, u32[]{:S(2)}, u32[]{:S(2)}) async-start(bf16[16,32,4096]{2,1,0:T(8,128)(2,1)} %add_convert_fusion), calls=%async_computation.3 | async-start | bytes 8388608 | tf_op jit(solution)/shard_map/all_to_all | solution.py:115
  266.9 8.4 %bitcast_convert_fusion.2 = bf16[4096,768]{1,0:T(8,128)(2,1)} fusion(bf16[16,32,4096]{2,1,0:T(8,128)(2,1)} %all-to-all-done, bf16[16,32,768]{2,1,0:T(8,128)(2,1)S(1)} %copy-done.7), kind=kOutput, calls=%fused_computation.10 | convolution fusion | flops 3224371200 | bytes 11272192 | tf_op jit(solution)/shard_map/nkd,nkh->dh/dot_general | solution.py:124
  275.4 8.3 %bitcast_convert_fusion.1 = bf16[4096,768]{1,0:T(8,128)(2,1)} fusion(bf16[16,32,4096]{2,1,0:T(8,128)(2,1)} %all-to-all-done, bf16[16,32,768]{2,1,0:T(8,128)(2,1)S(1)} %copy-done.9), kind=kOutput, calls=%fused_computation.9 | convolution fusion | flops 3224371200 | bytes 11272192 | tf_op jit(solution)/shard_map/nkd,nkh->dh/dot_general | solution.py:125
  283.7 0.2 reduce_sum.81
  283.9 43.5 %all-to-all-done.3 = bf16[16,32,4096]{2,1,0:T(8,128)(2,1)} async-done(((bf16[16,32,4096]{2,1,0:T(8,128)(2,1)}), bf16[16,32,4096]{2,1,0:T(8,128)(2,1)}, u32[]{:S(2)}, u32[]{:S(2)}) %all-to-all-start.3) | async-done | bytes 4194336 | tf_op jit(solution)/shard_map/all_to_all | solution.py:115
  327.3 0.8 broadcast_in_dim.18
  328.2 8.8 %all-to-all-start.5 = ((f32[128,1,512]{2,1,0:T(1,128)}), f32[128,1,512]{2,1,0:T(1,128)S(1)}, u32[]{:S(2)}, u32[]{:S(2)}) async-start(f32[128,1,512]{2,1,0:T(1,128)} %broadcast_in_dim.18), calls=%async_computation.5 | async-start | bytes 524288 | tf_op jit(solution)/shard_map/all_to_all | solution.py:60
  336.9 10.8 %pad_maximum_fusion = bf16[8,512,2,768]{3,1,2,0:T(8,128)(2,1)} fusion(bf16[8,512,1,768]{3,1,2,0:T(8,128)(2,1)} %bitcast.106, bf16[8,512,1,768]{3,1,2,0:T(8,128)(2,1)} %bitcast.105), kind=kLoop, calls=%fused_computation.7 | loop fusion | flops 6291456 | bytes 25165824 | tf_op jit(solution)/shard_map/stack | solution.py:66
  347.7 5.7 %all-to-all-start.6 = ((bf16[8,512,2,768]{3,1,2,0:T(8,128)(2,1)}), bf16[8,512,2,768]{3,1,2,0:T(8,128)(2,1)}, u32[]{:S(2)}, u32[]{:S(2)}) async-start(bf16[8,512,2,768]{3,1,2,0:T(8,128)(2,1)} %pad_maximum_fusion), calls=%async_computation.6 | async-start | bytes 25165824 | tf_op jit(solution)/shard_map/all_to_all | solution.py:69
  353.4 6.7 %gather_fusion.3 = bf16[256,4096]{1,0:T(8,128)(2,1)S(1)} fusion(bf16[512,4096]{1,0:T(8,128)(2,1)} %bitcast.13, s32[1024]{0:T(1024)S(1)} %pad_clamp_fusion), kind=kCustom, calls=%fused_computation.3 | custom fusion | bytes 4195328 | tf_op jit(solution)/shard_map/gather | solution.py:119
  360.1 4.2 reshape.169
  364.3 7.5 %reduce_sum.78 = f32[128,4096]{1,0:T(8,128)S(1)} reduce(f32[128,2,4096]{2,1,0:T(2,128)} %reshape.169, f32[]{:T(128)} %constant.56.clone.1), dimensions={1}, to_apply=%region_6.7 | reduce | flops 524288 | bytes 6291460 | tf_op jit(solution)/shard_map/reduce_sum | solution.py:118
  371.8 1.4 fusion.17
  373.2 0.5 copy-done.2
  373.8 8.0 %multiply_reduce_fusion = bf16[128,4096]{1,0:T(8,128)(2,1)} fusion(bf16[128,2,4096]{2,1,0:T(2,128)(2,1)S(1)} %copy-done.2, f32[128,2]{1,0:T(8,128)S(1)} %copy-done.5), kind=kLoop, calls=%fused_computation.28 | loop fusion | flops 2621440 | bytes 3146752 | tf_op jit(solution)/shard_map/reduce_sum | solution.py:103
  381.8 0.7 multiply_reduce_fusion.1
  382.5 0.7 div.45
  383.2 1.3 copy.70
  384.5 128.7 %all-to-all-done.6 = bf16[8,512,2,768]{3,1,2,0:T(8,128)(2,1)} async-done(((bf16[8,512,2,768]{3,1,2,0:T(8,128)(2,1)}), bf16[8,512,2,768]{3,1,2,0:T(8,128)(2,1)}, u32[]{:S(2)}, u32[]{:S(2)}) %all-to-all-start.6) | async-done | bytes 12582944 | tf_op jit(solution)/shard_map/all_to_all | solution.py:69
  513.2 6.6 %convert_reduce_fusion = f32[512,2,768]{2,0,1:T(8,128)S(1)} fusion(bf16[8,512,2,768]{3,1,2,0:T(8,128)(2,1)} %all-to-all-done.6), kind=kLoop, calls=%fused_computation.6 | loop fusion | flops 11796480 | bytes 15728640 | tf_op jit(solution)/shard_map/reduce_sum | solution.py:70
  519.8 1.4 fusion.25
  521.2 2.1 fusion.23
  (63 shorter events, 1.0 us)
Async XLA Ops:
  7.2 18.0 %copy-start = (bf16[4096,16]{0,1:T(8,128)(2,1)S(1)}, bf16[4096,16]{0,1:T(8,128)(2,1)}, u32[]{:S(2)}) copy-start(bf16[4096,16]{0,1:T(8,128)(2,1)} %param.10) | copy-start | bytes 393220
  17.3 7.6 %copy-start.6 = (s32[128,2]{0,1:T(2,128)S(1)}, s32[128,2]{0,1:T(2,128)}, u32[]{:S(2)}) copy-start(s32[128,2]{0,1:T(2,128)} %param.9) | copy-start | bytes 3076
  17.3 7.9 %copy-start.1 = (bf16[128,4096]{1,0:T(8,128)(2,1)S(1)}, bf16[128,4096]{1,0:T(8,128)(2,1)}, u32[]{:S(2)}) copy-start(bf16[128,4096]{1,0:T(8,128)(2,1)} %param.7) | copy-start | bytes 3145732
  17.3 61.9 %all-to-all-start = ((bf16[16,32,4096]{2,1,0:T(8,128)(2,1)}), bf16[16,32,4096]{2,1,0:T(8,128)(2,1)}, u32[]{:S(2)}, u32[]{:S(2)}) async-start(bf16[16,32,4096]{2,1,0:T(8,128)(2,1)} %bitcast.103), calls=%async_computation | async-start | bytes 8388608 | tf_op jit(solution)/shard_map/all_to_all | solution.py:90
  25.6 2.5 copy-start.3
  27.9 10.3 %copy-start.4 = (f32[128,2]{1,0:T(8,128)}, f32[128,2]{1,0:T(8,128)S(1)}, u32[]{:S(2)}) copy-start(f32[128,2]{1,0:T(8,128)S(1)} %copy.60) | copy-start | bytes 3076
  79.2 19.9 %slice-start.2 = ((s8[6291456]{0:T(1024)(128)(4,1)}), s8[2097152]{0:T(1024)(128)(4,1)S(1)}, s32[]{:S(2)}) async-start(s8[6291456]{0:T(1024)(128)(4,1)} %bitcast.113), calls=%async_computation.11 | async-start | bytes 4194304
  79.2 66.8 %all-to-all-start.1 = ((bf16[16,32,4096]{2,1,0:T(8,128)(2,1)}), bf16[16,32,4096]{2,1,0:T(8,128)(2,1)}, u32[]{:S(2)}, u32[]{:S(2)}) async-start(bf16[16,32,4096]{2,1,0:T(8,128)(2,1)} %bitcast.104), calls=%async_computation.1 | async-start | bytes 8388608 | tf_op jit(solution)/shard_map/all_to_all | solution.py:96
  91.8 7.3 %slice-start.3 = ((s8[6291456]{0:T(1024)(128)(4,1)}), s8[4194304]{0:T(1024)(128)(4,1)S(1)}, s32[]{:S(2)}) async-start(s8[6291456]{0:T(1024)(128)(4,1)} %bitcast.113), calls=%async_computation.12 | async-start | bytes 8388608
  91.8 15.6 %slice-start = ((s8[6291456]{0:T(1024)(128)(4,1)}), s8[4194304]{0:T(1024)(128)(4,1)S(1)}, s32[]{:S(2)}) async-start(s8[6291456]{0:T(1024)(128)(4,1)} %bitcast.111), calls=%async_computation.9 | async-start | bytes 8388608
  99.1 7.4 %copy-start.10 = (f32[16,32,768]{2,1,0:T(8,128)}, f32[16,32,768]{2,1,0:T(8,128)S(1)}, u32[]{:S(2)}) copy-start(f32[16,32,768]{2,1,0:T(8,128)S(1)} %fusion.10) | copy-start | bytes 4718596
  99.1 8.3 %slice-start.1 = ((s8[6291456]{0:T(1024)(128)(4,1)}), s8[2097152]{0:T(1024)(128)(4,1)S(1)}, s32[]{:S(2)}) async-start(s8[6291456]{0:T(1024)(128)(4,1)} %bitcast.111), calls=%async_computation.10 | async-start | bytes 4194304
  106.5 0.9 copy-start.11
  112.4 45.7 %copy-start.12 = (bf16[16,32,768]{2,1,0:T(8,128)(2,1)S(1)}, bf16[16,32,768]{2,1,0:T(8,128)(2,1)}, u32[]{:S(2)}) copy-start(bf16[16,32,768]{2,1,0:T(8,128)(2,1)} %copy-done.11) | copy-start | bytes 2359300
  146.0 66.4 %all-to-all-start.2 = ((bf16[16,32,4096]{2,1,0:T(8,128)(2,1)}), bf16[16,32,4096]{2,1,0:T(8,128)(2,1)}, u32[]{:S(2)}, u32[]{:S(2)}) async-start(bf16[16,32,4096]{2,1,0:T(8,128)(2,1)} %fusion.12), calls=%async_computation.2 | async-start | bytes 8388608 | tf_op jit(solution)/shard_map/all_to_all | solution.py:99
  157.8 363.4 %reduce-scatter.2.cloned.1.call-start = ((), (), s32[]{:S(2)}) async-start(), calls=%async_computation.8 | async-start | bytes 7077888 | tf_op jit(solution)/shard_map/reduce_scatter | solution.py:127
  166.5 10.6 %slice-start.4 = ((s8[6291456]{0:T(1024)(128)(4,1)}), s8[2097152]{0:T(1024)(128)(4,1)S(1)}, s32[]{:S(2)}) async-start(s8[6291456]{0:T(1024)(128)(4,1)} %bitcast.115), calls=%async_computation.13 | async-start | bytes 4194304
  166.5 10.5 %slice-start.5 = ((s8[6291456]{0:T(1024)(128)(4,1)}), s8[4194304]{0:T(1024)(128)(4,1)S(1)}, s32[]{:S(2)}) async-start(s8[6291456]{0:T(1024)(128)(4,1)} %bitcast.115), calls=%async_computation.14 | async-start | bytes 8388608
  176.2 0.9 copy-start.8
  233.2 26.3 %all-to-all-start.4 = ((f32[128,1,512]{2,1,0:T(1,128)}), f32[128,1,512]{2,1,0:T(1,128)S(1)}, u32[]{:S(2)}, u32[]{:S(2)}) async-start(f32[128,1,512]{2,1,0:T(1,128)} %all_to_all.33), calls=%async_computation.4 | async-start | bytes 524288 | tf_op jit(solution)/shard_map/all_to_all | solution.py:58
  259.5 7.4 %copy-start.7 = (bf16[16,32,768]{2,1,0:T(8,128)(2,1)S(1)}, bf16[16,32,768]{2,1,0:T(8,128)(2,1)}, u32[]{:S(2)}) copy-start(bf16[16,32,768]{2,1,0:T(8,128)(2,1)} %get-tuple-element.38) | copy-start | bytes 2359300
  259.5 67.8 %all-to-all-start.3 = ((bf16[16,32,4096]{2,1,0:T(8,128)(2,1)}), bf16[16,32,4096]{2,1,0:T(8,128)(2,1)}, u32[]{:S(2)}, u32[]{:S(2)}) async-start(bf16[16,32,4096]{2,1,0:T(8,128)(2,1)} %add_convert_fusion), calls=%async_computation.3 | async-start | bytes 8388608 | tf_op jit(solution)/shard_map/all_to_all | solution.py:115
  266.9 8.4 %copy-start.9 = (bf16[16,32,768]{2,1,0:T(8,128)(2,1)S(1)}, bf16[16,32,768]{2,1,0:T(8,128)(2,1)}, u32[]{:S(2)}) copy-start(bf16[16,32,768]{2,1,0:T(8,128)(2,1)} %copy-done.8) | copy-start | bytes 2359300
  328.2 19.6 %all-to-all-start.5 = ((f32[128,1,512]{2,1,0:T(1,128)}), f32[128,1,512]{2,1,0:T(1,128)S(1)}, u32[]{:S(2)}, u32[]{:S(2)}) async-start(f32[128,1,512]{2,1,0:T(1,128)} %broadcast_in_dim.18), calls=%async_computation.5 | async-start | bytes 524288 | tf_op jit(solution)/shard_map/all_to_all | solution.py:60
  347.7 165.5 %all-to-all-start.6 = ((bf16[8,512,2,768]{3,1,2,0:T(8,128)(2,1)}), bf16[8,512,2,768]{3,1,2,0:T(8,128)(2,1)}, u32[]{:S(2)}, u32[]{:S(2)}) async-start(bf16[8,512,2,768]{3,1,2,0:T(8,128)(2,1)} %pad_maximum_fusion), calls=%async_computation.6 | async-start | bytes 25165824 | tf_op jit(solution)/shard_map/all_to_all | solution.py:69
  364.3 9.0 %copy-start.5 = (f32[128,2]{1,0:T(8,128)S(1)}, f32[128,2]{1,0:T(8,128)}, u32[]{:S(2)}) copy-start(f32[128,2]{1,0:T(8,128)} %copy-done.4) | copy-start | bytes 3076
  371.8 2.0 copy-start.2
Sparse Core Ops, SparseCore 0:
  166.6 230.1 reduce-scatter.1

commit v6 on v5

--- a/solution.py
+++ b/solution.py
@@ -60,14 +60,33 @@
     return lax.all_to_all(spread, axes, 0, 0, tiled=True).reshape(part.shape)
 
 
-def reduce_scatter_by_exchange(parts, axis):
+def reduce_scatter_by_ring(parts, axis):
     replica_count = lax.axis_size(axis)
     rows = parts[0].shape[0] // replica_count
     blocks = jnp.stack([p.astype(jnp.bfloat16) for p in parts], axis=1)
     blocks = blocks.reshape((replica_count, rows) + blocks.shape[1:])
-    blocks = blocks.reshape(replica_count, rows, len(parts), parts[0].shape[1])
-    arrived = lax.all_to_all(blocks, axis, 0, 0, tiled=True)
-    total = jnp.sum(arrived.astype(jnp.float32), axis=0)
+    half = blocks.shape[-1] // 2
+    rows_along = replica_count // 2
+    ring = [2 * z for z in range(rows_along)] + [2 * z + 1 for z in reversed(range(rows_along))]
+    place = [ring.index(i) for i in range(replica_count)]
+    ring_at = jnp.asarray(ring, jnp.int32)
+    pos = jnp.asarray(place, jnp.int32)[lax.axis_index(axis)]
+    forward = [(ring[q], ring[(q + 1) % replica_count]) for q in range(replica_count)]
+    backward = [(ring[q], ring[(q - 1) % replica_count]) for q in range(replica_count)]
+
+    def block(step, lower):
+        owner = ring_at[(pos + step) % replica_count]
+        rows_of = lax.dynamic_index_in_dim(blocks, owner, axis=0, keepdims=False)
+        return (rows_of[..., :half] if lower else rows_of[..., half:]).astype(jnp.float32)
+
+    ahead = block(-1, True)
+    behind = block(1, False)
+    for step in range(1, replica_count):
+        ahead = lax.ppermute(ahead.astype(jnp.bfloat16), axis, forward).astype(jnp.float32)
+        ahead = ahead + block(-1 - step, True)
+        behind = lax.ppermute(behind.astype(jnp.bfloat16), axis, backward).astype(jnp.float32)
+        behind = behind + block(1 + step, False)
+    total = jnp.concatenate([ahead, behind], axis=-1)
     return tuple(total[:, i] for i in range(len(parts)))
 
 
@@ -127,7 +146,7 @@
     down_total = lax.psum_scatter(
         down_part.astype(jnp.bfloat16), "dp", scatter_dimension=0, tiled=True
     ).astype(jnp.float32)
-    gate_total, up_total = reduce_scatter_by_exchange((gate_part, up_part), "dp")
+    gate_total, up_total = reduce_scatter_by_ring((gate_part, up_part), "dp")
     gate_grad = (gate_total / replica_count).astype(jnp.bfloat16)[None]
     up_grad = (up_total / replica_count).astype(jnp.bfloat16)[None]
     down_grad = (down_total / replica_count).astype(jnp.bfloat16)[None]

time: 539 us -> 598 us (1.11)
  between operations: 14.9 us -> 56.3 us
  other arithmetic: 41.6 us -> 57.9 us
  starting transfers between devices: 69.5 us -> 84.1 us
  waiting for transfers between devices: 269 us -> 257 us
  matrix products: 81.4 us -> 73.3 us
    ppermute x0 -> x14, waiting for transfers between devices: none -> 207 us  [the longest x7 155 us: reduce_scatter_by_ring(): lax.ppermute(ahead.astype(jnp.bfloat16), axis, forward).astype(jnp.float32)]
    all_to_all x1 -> x0, waiting for transfers between devices: 129 us -> none  [reduce_scatter_by_exchange(): arrived = lax.all_to_all(blocks, axis, 0, 0, tiled=True)]
    all_to_all x1, waiting for transfers between devices: 43.5 us -> 0.01 us  [on_device(): lax.all_to_all(grad_in, 'expert', split_axis=0, concat_axis=0, tiled=True)]
    all_to_all x1, waiting for transfers between devices: 29.3 us -> 0.01 us  [on_device(): lax.all_to_all(expert_out, 'expert', split_axis=0, concat_axis=0, tiled=T...]
    all_to_all x1, waiting for transfers between devices: 33.6 us -> 9.53 us  [on_device(): lax.all_to_all(grad_out, 'expert', split_axis=0, concat_axis=0, tiled=True)]
    convert_element_type x0 -> x12, other arithmetic: none -> 18 us  [the longest x6 9.59 us: reduce_scatter_by_ring(): ahead.astype(jnp.bfloat16)]
    ppermute x0 -> x14, starting transfers between devices: none -> 17.6 us  [the longest x7 15.6 us: reduce_scatter_by_ring(): lax.ppermute(behind.astype(jnp.bfloat16), axis, backward)]
    squeeze x0 -> x3, other arithmetic: none -> 13.5 us  [block(): rows_of = lax.dynamic_index_in_dim(blocks, owner, axis=0, keepdims=False)]
  transfers between devices with their start and end apart: 8 -> 21, of which waited for: 5 -> 14; matrix products, arithmetic and copies ran while one was open for 30% -> 26% of each run, Pallas kernels for 0% -> 0%
where the time goes in v6:
time: 598 us; the launch traced here: 587 us
  waiting for transfers between devices  257 us (43%)
  starting transfers between devices  84.1 us (14%)
  matrix products  73.3 us (12%)
  local copies, waits for them, and re-layouts  59 us (10%)
  other arithmetic  57.9 us (10%)
  between operations  56.3 us (9%)
    ppermute x7, waiting for transfers between devices, reduce_scatter_by_ring(): lax.ppermute(ahead.astype(jnp.bfloat16), axis, forward).astype(jnp.float32)  155 us
    ppermute x7, waiting for transfers between devices, reduce_scatter_by_ring(): lax.ppermute(behind.astype(jnp.bfloat16), axis, backward)  51.5 us
    all_to_all x1, waiting for transfers between devices, on_device(): lax.all_to_all(outbound, 'expert', split_axis=0, concat_axis=0, tiled=True)  32.5 us
    ppermute x7, starting transfers between devices, reduce_scatter_by_ring(): lax.ppermute(behind.astype(jnp.bfloat16), axis, backward)  15.6 us
    squeeze x3, other arithmetic, block(): rows_of = lax.dynamic_index_in_dim(blocks, owner, axis=0, keepdims=False)  13.5 us
    all_to_all x1, starting transfers between devices, on_device(): lax.all_to_all(grad_in, 'expert', split_axis=0, concat_axis=0, tiled=True)  13.2 us
    all_to_all x1, starting transfers between devices, on_device(): lax.all_to_all(expert_out, 'expert', split_axis=0, concat_axis=0, tiled=T...  12.6 us
    all_to_all x1, starting transfers between devices, on_device(): lax.all_to_all(grad_out, 'expert', split_axis=0, concat_axis=0, tiled=True)  12.2 us
  transfers between devices with their start and end apart: 21, of which 14 were waited for; matrix products, arithmetic and copies ran while one was open for 26% of the time, Pallas kernels for 0%

profile of v6, /device:TPU:4, one launch (start us, length us, event | category | flops | bytes accessed | tf_op | source)
XLA Modules:
  0.0 587.1 jit_solution(10304586420746703721)
XLA Ops:
  10.2 1.4 scatter_custom_fusion
  13.0 4.5 gather_fusion
  17.4 7.6 %all-to-all-start = ((bf16[16,32,4096]{2,1,0:T(8,128)(2,1)}), bf16[16,32,4096]{2,1,0:T(8,128)(2,1)}, u32[]{:S(2)}, u32[]{:S(2)}) async-start(bf16[16,32,4096]{2,1,0:T(8,128)(2,1)} %bitcast.169), calls=%async_computation | async-start | bytes 8388608 | tf_op jit(solution)/shard_map/all_to_all | solution.py:109
  25.0 4.1 mul.101
  29.1 6.2 %mul.102 = f32[256,4096]{1,0:T(8,128)} reshape(f32[128,2,4096]{2,1,0:T(2,128)} %mul.101) | data formatting | bytes 8388608 | tf_op jit(solution)/shard_map/mul | solution.py:110
  36.0 2.0 gather_fusion.4
  39.5 2.6 multiply_convert_fusion
  42.5 4.4 gather_fusion.1
  46.8 32.5 %all-to-all-done = bf16[16,32,4096]{2,1,0:T(8,128)(2,1)} async-done(((bf16[16,32,4096]{2,1,0:T(8,128)(2,1)}), bf16[16,32,4096]{2,1,0:T(8,128)(2,1)}, u32[]{:S(2)}, u32[]{:S(2)}) %all-to-all-start) | async-done | bytes 4194336 | tf_op jit(solution)/shard_map/all_to_all | solution.py:109
  79.4 12.2 %all-to-all-start.1 = ((bf16[16,32,4096]{2,1,0:T(8,128)(2,1)}), bf16[16,32,4096]{2,1,0:T(8,128)(2,1)}, u32[]{:S(2)}, u32[]{:S(2)}) async-start(bf16[16,32,4096]{2,1,0:T(8,128)(2,1)} %bitcast.168), calls=%async_computation.1 | async-start | bytes 8388608 | tf_op jit(solution)/shard_map/all_to_all | solution.py:115
  115.6 7.2 %fusion.10 = f32[16,32,768]{2,1,0:T(8,128)S(1)} fusion(bf16[16,32,4096]{2,1,0:T(8,128)(2,1)} %all-to-all-done, bf16[1,4096,768]{2,1,0:T(8,128)(2,1)} %param.13), kind=kOutput, calls=%fused_computation.52 | convolution fusion | flops 3221225472 | bytes 12058624 | tf_op jit(solution)/shard_map/...d,dh->...h/dot_general | solution.py:31
  122.9 7.4 %multiply_convert_fusion.4 = (bf16[16,32,768]{2,1,0:T(8,128)(2,1)S(1)}, f32[16,32,768]{2,1,0:T(8,128)}) fusion(f32[16,32,768]{2,1,0:T(8,128)S(1)} %fusion.10, bf16[16,32,4096]{2,1,0:T(8,128)(2,1)} %all-to-all-done, bf16[1,4096,768]{2,1,0:T(8,128)(2,1)S(1)} %bitcast.177), kind=kOutput, calls=%fused_computation.103 | convolution fusion | flops 3223584768 | bytes 14417920 | tf_op jit(solution)/shard_map/...d,dh->...h/dot_general | solution.py:32
  131.2 5.2 fusion.12
  136.4 9.5 %all-to-all-done.1 = bf16[16,32,4096]{2,1,0:T(8,128)(2,1)} async-done(((bf16[16,32,4096]{2,1,0:T(8,128)(2,1)}), bf16[16,32,4096]{2,1,0:T(8,128)(2,1)}, u32[]{:S(2)}, u32[]{:S(2)}) %all-to-all-start.1) | async-done | bytes 4194336 | tf_op jit(solution)/shard_map/all_to_all | solution.py:115
  145.9 8.5 %bitcast_convert_fusion = bf16[4096,768]{1,0:T(8,128)(2,1)} fusion(bf16[16,32,4096]{2,1,0:T(8,128)(2,1)} %all-to-all-done.1, bf16[16,32,768]{2,1,0:T(8,128)(2,1)} %copy-done.33), kind=kOutput, calls=%fused_computation.38 | convolution fusion | flops 3224371200 | bytes 11272192 | tf_op jit(solution)/shard_map/nkd,nkh->dh/dot_general | solution.py:145
  154.5 8.2 %multiply_convert_fusion.3 = (bf16[16,32,768]{2,1,0:T(8,128)(2,1)S(1)}, bf16[16,32,768]{2,1,0:T(8,128)(2,1)S(1)}) fusion(f32[16,32,768]{2,1,0:T(8,128)S(1)} %copy-done.32, f32[16,32,768]{2,1,0:T(8,128)} %get-tuple-element.75, bf16[16,32,4096]{2,1,0:T(8,128)(2,1)} %all-to-all-done.1, bf16[1,4096,768]{2,1,0:T(8,128)(2,1)} %param.15), kind=kOutput, calls=%fused_computation.102 | convolution fusion | flops 3226337280 | bytes 15204352 | tf_op jit(solution)/shard_map/...d,dh->...h/dot_general | solution.py:42
  163.5 5.7 bitcast_convert_fusion.1
  169.2 8.2 %bitcast_convert_fusion.2 = bf16[4096,768]{1,0:T(8,128)(2,1)S(1)} fusion(bf16[16,32,4096]{2,1,0:T(8,128)(2,1)} %all-to-all-done, bf16[16,32,768]{2,1,0:T(8,128)(2,1)S(1)} %get-tuple-element.54), kind=kOutput, calls=%fused_computation.40 | convolution fusion | flops 3224371200 | bytes 11272192 | tf_op jit(solution)/shard_map/nkd,nkh->dh/dot_general | solution.py:143
  177.4 3.4 fusion.50
  195.1 12.6 %all-to-all-start.2 = ((bf16[16,32,4096]{2,1,0:T(8,128)(2,1)}), bf16[16,32,4096]{2,1,0:T(8,128)(2,1)}, u32[]{:S(2)}, u32[]{:S(2)}) async-start(bf16[16,32,4096]{2,1,0:T(8,128)(2,1)} %fusion.12), calls=%async_computation.2 | async-start | bytes 8388608 | tf_op jit(solution)/shard_map/all_to_all | solution.py:118
  207.8 5.9 %fusion.49 = (bf16[512,2,768]{2,0,1:T(8,128)(2,1)}, bf16[512,2,768]{2,0,1:T(8,128)(2,1)S(1)}, bf16[512,2,768]{2,0,1:T(8,128)(2,1)}, bf16[512,2,768]{2,0,1:T(8,12...) fusion(s32[]{:T(128)S(6)} %select_n.230, bf16[8,512,1,768]{3,1,0,2:T(8,128)(2,1)} %bitcast.163, ...), kind=kLoop, calls=%fused_computation.113 | loop fusion | flops 4718592 | bytes 22020120 | tf_op jit(solution)/shard_map/jit(dynamic_index_in_dim)/squeeze | solution.py:79
  215.7 8.6 %collective-permute-done.7 = bf16[512,2,384]{2,0,1:T(8,128)(2,1)} collective-permute-done((bf16[512,2,384]{2,0,1:T(8,128)(2,1)}, bf16[512,2,384]{2,0,1:T(8,128)(2,1)}, u32[]{:S(2)}, u32[]{:S(2)}) %collective-permute-start.7) | collective-permute-done | bytes 786464 | tf_op jit(solution)/shard_map/ppermute | solution.py:87
  224.3 2.2 add_convert_fusion.6
  226.5 2.5 collective-permute-start.8
  236.8 64.1 %collective-permute-done = bf16[512,2,384]{2,0,1:T(8,128)(2,1)} collective-permute-done((bf16[512,2,384]{2,0,1:T(8,128)(2,1)}, bf16[512,2,384]{2,0,1:T(8,128)(2,1)}, u32[]{:S(2)}, u32[]{:S(2)}) %collective-permute-start) | collective-permute-done | bytes 786464 | tf_op jit(solution)/shard_map/ppermute | solution.py:85
  300.9 1.6 add_convert_fusion.12
  302.5 5.6 collective-permute-done.8
  308.2 1.3 add_convert_fusion.5
  309.5 2.5 collective-permute-start.9
  312.1 5.6 fusion.4
  317.7 20.4 %collective-permute-done.1 = bf16[512,2,384]{2,0,1:T(8,128)(2,1)S(1)} collective-permute-done((bf16[512,2,384]{2,0,1:T(8,128)(2,1)S(1)}, bf16[512,2,384]{2,0,1:T(8,128)(2,1)S(1)}, u32[]{:S(2)}, u32[]{:S(2)}) %collective-permute-start.1) | collective-permute-done | bytes 786464 | tf_op jit(solution)/shard_map/ppermute | solution.py:85
  339.2 7.0 %collective-permute-done.9 = bf16[512,2,384]{2,0,1:T(8,128)(2,1)S(1)} collective-permute-done((bf16[512,2,384]{2,0,1:T(8,128)(2,1)S(1)}, bf16[512,2,384]{2,0,1:T(8,128)(2,1)S(1)}, u32[]{:S(2)}, u32[]{:S(2)}) %collective-permute-start.9) | collective-permute-done | bytes 786464 | tf_op jit(solution)/shard_map/ppermute | solution.py:87
  347.3 2.5 collective-permute-start.10
  349.7 8.0 %add_convert_fusion = bf16[16,32,4096]{2,1,0:T(8,128)(2,1)} fusion(f32[16,32,4096]{2,1,0:T(8,128)S(1)} %fusion.4, bf16[16,32,768]{2,1,0:T(8,128)(2,1)S(1)} %copy-done.28, bf16[1,4096,768]{2,1,0:T(8,128)(2,1)} %param.13), kind=kOutput, calls=%fused_computation.41 | convolution fusion | flops 3225419776 | bytes 19660800 | tf_op jit(solution)/shard_map/...h,dh->...d/dot_general | solution.py:48
  357.8 13.2 %all-to-all-start.3 = ((bf16[16,32,4096]{2,1,0:T(8,128)(2,1)}), bf16[16,32,4096]{2,1,0:T(8,128)(2,1)}, u32[]{:S(2)}, u32[]{:S(2)}) async-start(bf16[16,32,4096]{2,1,0:T(8,128)(2,1)} %add_convert_fusion), calls=%async_computation.3 | async-start | bytes 8388608 | tf_op jit(solution)/shard_map/all_to_all | solution.py:134
  371.0 4.3 fusion.57
  375.3 1.5 collective-permute-done.2
  376.8 1.4 add_convert_fusion.10
  378.2 12.3 %collective-permute-done.10 = bf16[512,2,384]{2,0,1:T(8,128)(2,1)S(1)} collective-permute-done((bf16[512,2,384]{2,0,1:T(8,128)(2,1)}, bf16[512,2,384]{2,0,1:T(8,128)(2,1)S(1)}, u32[]{:S(2)}, u32[]{:S(2)}) %collective-permute-start.10) | collective-permute-done | bytes 786464 | tf_op jit(solution)/shard_map/ppermute | solution.py:87
  390.7 2.4 collective-permute-start.11
  393.1 62.4 %collective-permute-done.3 = bf16[512,2,384]{2,0,1:T(8,128)(2,1)S(1)} collective-permute-done((bf16[512,2,384]{2,0,1:T(8,128)(2,1)S(1)}, bf16[512,2,384]{2,0,1:T(8,128)(2,1)S(1)}, u32[]{:S(2)}, u32[]{:S(2)}) %collective-permute-start.3) | collective-permute-done | bytes 786464 | tf_op jit(solution)/shard_map/ppermute | solution.py:85
  457.0 13.4 %collective-permute-done.11 = bf16[512,2,384]{2,0,1:T(8,128)(2,1)S(1)} collective-permute-done((bf16[512,2,384]{2,0,1:T(8,128)(2,1)S(1)}, bf16[512,2,384]{2,0,1:T(8,128)(2,1)S(1)}, u32[]{:S(2)}, u32[]{:S(2)}) %collective-permute-start.11) | collective-permute-done | bytes 786464 | tf_op jit(solution)/shard_map/ppermute | solution.py:87
  471.5 6.6 %gather_fusion.2 = bf16[256,4096]{1,0:T(8,128)(2,1)S(1)} fusion(bf16[512,4096]{1,0:T(8,128)(2,1)} %bitcast.12, s32[1024]{0:T(1024)S(1)} %pad_clamp_fusion), kind=kCustom, calls=%fused_computation.2 | custom fusion | bytes 4195328 | tf_op jit(solution)/shard_map/gather | solution.py:121
  478.2 2.7 reshape.199
  480.8 2.5 collective-permute-start.12
  483.3 7.2 %fusion.18 = f32[128,1,2]{2,1,0:T(1,128)S(1)} fusion(bf16[128,2,4096]{2,1,0:T(2,128)(2,1)} %reshape.199, bf16[128,4096,1]{1,0,2:T(8,128)(2,1)S(1)} %bitcast.170), kind=kOutput, calls=%fused_computation.62 | convolution fusion | flops 2097152 | bytes 3146752 | tf_op jit(solution)/shard_map/td,tkd->tk/dot_general | solution.py:125
  490.5 2.3 add_convert_fusion.8
  493.9 1.5 all_to_all.29
  495.4 4.5 collective-permute-done.12
  499.9 2.4 add_convert_fusion.1
  502.4 2.5 collective-permute-start.13
  504.9 6.9 %collective-permute-done.5 = bf16[512,2,384]{2,0,1:T(8,128)(2,1)} collective-permute-done((bf16[512,2,384]{2,0,1:T(8,128)(2,1)}, bf16[512,2,384]{2,0,1:T(8,128)(2,1)}, u32[]{:S(2)}, u32[]{:S(2)}) %collective-permute-start.5) | collective-permute-done | bytes 786464 | tf_op jit(solution)/shard_map/ppermute | solution.py:85
  511.8 2.2 add_convert_fusion.7
  514.3 10.7 %all-to-all-start.4 = ((f32[128,1,512]{2,1,0:T(1,128)}), f32[128,1,512]{2,1,0:T(1,128)S(1)}, u32[]{:S(2)}, u32[]{:S(2)}) async-start(f32[128,1,512]{2,1,0:T(1,128)} %all_to_all.29), calls=%async_computation.4 | async-start | bytes 524288 | tf_op jit(solution)/shard_map/all_to_all | solution.py:58
  525.0 7.5 %multiply_reduce_fusion = bf16[128,4096]{1,0:T(8,128)(2,1)} fusion(bf16[128,2,4096]{2,1,0:T(2,128)(2,1)S(1)} %copy-done.5, f32[128,2]{1,0:T(8,128)S(1)} %copy-done.16), kind=kLoop, calls=%fused_computation.58 | loop fusion | flops 2621440 | bytes 3146752 | tf_op jit(solution)/shard_map/reduce_sum | solution.py:122
  532.5 6.6 %gather_fusion.3 = bf16[256,4096]{1,0:T(8,128)(2,1)S(1)} fusion(bf16[512,4096]{1,0:T(8,128)(2,1)} %bitcast.13, s32[1024]{0:T(1024)S(1)} %pad_clamp_fusion), kind=kCustom, calls=%fused_computation.3 | custom fusion | bytes 4195328 | tf_op jit(solution)/shard_map/gather | solution.py:138
  539.1 4.2 reshape.201
  543.3 7.5 %reduce_sum.69 = f32[128,4096]{1,0:T(8,128)S(1)} reduce(f32[128,2,4096]{2,1,0:T(2,128)} %reshape.201, f32[]{:T(128)} %constant.197.clone.1), dimensions={1}, to_apply=%region_6.7 | reduce | flops 524288 | bytes 6291460 | tf_op jit(solution)/shard_map/reduce_sum | solution.py:137
  551.9 9.8 %all-to-all-start.5 = ((f32[128,1,512]{2,1,0:T(1,128)}), f32[128,1,512]{2,1,0:T(1,128)S(1)}, u32[]{:S(2)}, u32[]{:S(2)}) async-start(f32[128,1,512]{2,1,0:T(1,128)} %broadcast_in_dim.18), calls=%async_computation.5 | async-start | bytes 524288 | tf_op jit(solution)/shard_map/all_to_all | solution.py:60
  561.6 1.4 fusion.17
  563.1 7.8 %all-to-all-done.5 = f32[128,1,512]{2,1,0:T(1,128)S(1)} async-done(((f32[128,1,512]{2,1,0:T(1,128)}), f32[128,1,512]{2,1,0:T(1,128)S(1)}, u32[]{:S(2)}, u32[]{:S(2)}) %all-to-all-start.5) | async-done | bytes 262176 | tf_op jit(solution)/shard_map/all_to_all | solution.py:60
  573.6 1.4 convert_add_fusion
  576.5 1.4 fusion.59
  577.9 2.1 fusion.58
  (145 shorter events, 27.1 us)
Async XLA Ops:
  7.2 28.4 %copy-start = (bf16[4096,16]{0,1:T(8,128)(2,1)S(1)}, bf16[4096,16]{0,1:T(8,128)(2,1)}, u32[]{:S(2)}) copy-start(bf16[4096,16]{0,1:T(8,128)(2,1)} %param.12) | copy-start | bytes 393220
  10.2 1.4 copy-start.24
  17.4 7.6 %copy-start.13 = (bf16[128,4096]{1,0:T(8,128)(2,1)S(1)}, bf16[128,4096]{1,0:T(8,128)(2,1)}, u32[]{:S(2)}) copy-start(bf16[128,4096]{1,0:T(8,128)(2,1)} %param.10) | copy-start | bytes 3145732
  17.4 61.9 %all-to-all-start = ((bf16[16,32,4096]{2,1,0:T(8,128)(2,1)}), bf16[16,32,4096]{2,1,0:T(8,128)(2,1)}, u32[]{:S(2)}, u32[]{:S(2)}) async-start(bf16[16,32,4096]{2,1,0:T(8,128)(2,1)} %bitcast.169), calls=%async_computation | async-start | bytes 8388608 | tf_op jit(solution)/shard_map/all_to_all | solution.py:109
  29.1 6.2 %copy-start.18 = (s32[128,2]{0,1:T(2,128)S(1)}, s32[128,2]{0,1:T(2,128)}, u32[]{:S(2)}) copy-start(s32[128,2]{0,1:T(2,128)} %param.11) | copy-start | bytes 3076
  29.1 6.4 %copy-start.3 = (bf16[128,4096]{1,0:T(8,128)(2,1)S(1)}, bf16[128,4096]{1,0:T(8,128)(2,1)}, u32[]{:S(2)}) copy-start(bf16[128,4096]{1,0:T(8,128)(2,1)} %param.9) | copy-start | bytes 3145732
  38.2 0.6 copy-start.20
  38.2 0.9 copy-start.22
  38.9 0.6 copy-start.15
  79.4 12.7 %copy-start.26 = (s32[8]{0:T(128)S(1)}, s32[8]{0:T(128)}, u32[]{:S(2)}) copy-start(s32[8]{0:T(128)} %constant.227.clone) | copy-start | bytes 100
  79.4 24.0 %copy-start.17 = (s32[8]{0:T(128)S(1)}, s32[8]{0:T(128)}, u32[]{:S(2)}) copy-start(s32[8]{0:T(128)} %constant.226.clone) | copy-start | bytes 100
  79.4 43.5 %slice-start.2 = ((s8[6291456]{0:T(1024)(128)(4,1)}), s8[2097152]{0:T(1024)(128)(4,1)S(1)}, s32[]{:S(2)}) async-start(s8[6291456]{0:T(1024)(128)(4,1)} %bitcast.176), calls=%async_computation.10 | async-start | bytes 4194304
  79.4 66.5 %all-to-all-start.1 = ((bf16[16,32,4096]{2,1,0:T(8,128)(2,1)}), bf16[16,32,4096]{2,1,0:T(8,128)(2,1)}, u32[]{:S(2)}, u32[]{:S(2)}) async-start(bf16[16,32,4096]{2,1,0:T(8,128)(2,1)} %bitcast.168), calls=%async_computation.1 | async-start | bytes 8388608 | tf_op jit(solution)/shard_map/all_to_all | solution.py:115
  91.6 486.4 %reduce-scatter.2.cloned.1.call-start = ((), (), s32[]{:S(2)}) async-start(), calls=%async_computation.7 | async-start | bytes 7077888 | tf_op jit(solution)/shard_map/reduce_scatter | solution.py:146
  115.5 7.3 %slice-start.3 = ((s8[6291456]{0:T(1024)(128)(4,1)}), s8[4194304]{0:T(1024)(128)(4,1)S(1)}, s32[]{:S(2)}) async-start(s8[6291456]{0:T(1024)(128)(4,1)} %bitcast.176), calls=%async_computation.11 | async-start | bytes 8388608
  115.6 15.6 %slice-start = ((s8[6291456]{0:T(1024)(128)(4,1)}), s8[4194304]{0:T(1024)(128)(4,1)S(1)}, s32[]{:S(2)}) async-start(s8[6291456]{0:T(1024)(128)(4,1)} %bitcast.174), calls=%async_computation.8 | async-start | bytes 8388608
  122.8 7.5 %copy-start.31 = (f32[16,32,768]{2,1,0:T(8,128)}, f32[16,32,768]{2,1,0:T(8,128)S(1)}, u32[]{:S(2)}) copy-start(f32[16,32,768]{2,1,0:T(8,128)S(1)} %fusion.10) | copy-start | bytes 4718596
  122.9 8.3 %slice-start.1 = ((s8[6291456]{0:T(1024)(128)(4,1)}), s8[2097152]{0:T(1024)(128)(4,1)S(1)}, s32[]{:S(2)}) async-start(s8[6291456]{0:T(1024)(128)(4,1)} %bitcast.174), calls=%async_computation.9 | async-start | bytes 4194304
  130.3 0.9 copy-start.33
  136.4 18.1 %copy-start.32 = (f32[16,32,768]{2,1,0:T(8,128)S(1)}, f32[16,32,768]{2,1,0:T(8,128)}, u32[]{:S(2)}) copy-start(f32[16,32,768]{2,1,0:T(8,128)} %copy-done.31) | copy-start | bytes 4718596
  162.6 0.9 copy-start.29
  162.6 6.6 %copy-start.27 = (bf16[16,32,768]{2,1,0:T(8,128)(2,1)}, bf16[16,32,768]{2,1,0:T(8,128)(2,1)S(1)}, u32[]{:S(2)}) copy-start(bf16[16,32,768]{2,1,0:T(8,128)(2,1)S(1)} %get-tuple-element.54) | copy-start | bytes 2359300
  169.2 8.2 %copy-start.1 = (bf16[4096,768]{1,0:T(8,128)(2,1)}, bf16[4096,768]{1,0:T(8,128)(2,1)S(1)}, u32[]{:S(2)}) copy-start(bf16[4096,768]{1,0:T(8,128)(2,1)S(1)} %bitcast_convert_fusion.1) | copy-start | bytes 18874372
  177.4 4.6 copy-start.2
  182.9 41.4 %collective-permute-start.7 = (bf16[512,2,384]{2,0,1:T(8,128)(2,1)}, bf16[512,2,384]{2,0,1:T(8,128)(2,1)}, u32[]{:S(2)}, u32[]{:S(2)}) collective-permute-start(bf16[512,2,384]{2,0,1:T(8,128)(2,1)} %slice.99), channel_id=1, source_target_pairs={{0,1},{2,0},{4,2},{6,4},{7,6},{5,7},{3,5},{1,3},{8,9},{10,8},{12,1... | collective-permute-start | bytes 2359304 | tf_op jit(solution)/shard_map/ppermute | solution.py:87
  195.1 162.6 %all-to-all-start.2 = ((bf16[16,32,4096]{2,1,0:T(8,128)(2,1)}), bf16[16,32,4096]{2,1,0:T(8,128)(2,1)}, u32[]{:S(2)}, u32[]{:S(2)}) async-start(bf16[16,32,4096]{2,1,0:T(8,128)(2,1)} %fusion.12), calls=%async_computation.2 | async-start | bytes 8388608 | tf_op jit(solution)/shard_map/all_to_all | solution.py:118
  213.7 10.7 %copy-start.12 = (bf16[512,2,768]{2,0,1:T(8,128)(2,1)S(1)}, bf16[512,2,768]{2,0,1:T(8,128)(2,1)}, u32[]{:S(2)}) copy-start(bf16[512,2,768]{2,0,1:T(8,128)(2,1)} %get-tuple-element.45) | copy-start | bytes 4718596
  214.6 86.3 %collective-permute-start = (bf16[512,2,384]{2,0,1:T(8,128)(2,1)}, bf16[512,2,384]{2,0,1:T(8,128)(2,1)}, u32[]{:S(2)}, u32[]{:S(2)}) collective-permute-start(bf16[512,2,384]{2,0,1:T(8,128)(2,1)} %slice.91), channel_id=1, source_target_pairs={{0,2},{2,4},{4,6},{6,7},{7,5},{5,3},{3,1},{1,0},{8,10},{10,12},{12... | collective-permute-start | bytes 2359304 | tf_op jit(solution)/shard_map/ppermute | solution.py:85
  226.5 81.6 %collective-permute-start.8 = (bf16[512,2,384]{2,0,1:T(8,128)(2,1)}, bf16[512,2,384]{2,0,1:T(8,128)(2,1)}, u32[]{:S(2)}, u32[]{:S(2)}) collective-permute-start(bf16[512,2,384]{2,0,1:T(8,128)(2,1)} %add_convert_fusion.6), channel_id=1, source_target_pairs={{0,1},{2,0},{4,2},{6,4},{7,6},{5,7},{3,5},{1,3},{8,9},{10,8},{12,1... | collective-permute-start | bytes 2359304 | tf_op jit(solution)/shard_map/ppermute | solution.py:87
  236.8 71.4 %copy-start.9 = (bf16[512,2,768]{2,0,1:T(8,128)(2,1)S(1)}, bf16[512,2,768]{2,0,1:T(8,128)(2,1)}, u32[]{:S(2)}) copy-start(bf16[512,2,768]{2,0,1:T(8,128)(2,1)} %get-tuple-element.46) | copy-start | bytes 4718596
  302.4 9.6 %copy-start.30 = (bf16[16,32,768]{2,1,0:T(8,128)(2,1)S(1)}, bf16[16,32,768]{2,1,0:T(8,128)(2,1)}, u32[]{:S(2)}) copy-start(bf16[16,32,768]{2,1,0:T(8,128)(2,1)} %copy-done.29) | copy-start | bytes 2359300
  302.4 35.6 %collective-permute-start.1 = (bf16[512,2,384]{2,0,1:T(8,128)(2,1)S(1)}, bf16[512,2,384]{2,0,1:T(8,128)(2,1)S(1)}, u32[]{:S(2)}, u32[]{:S(2)}) collective-permute-start(bf16[512,2,384]{2,0,1:T(8,128)(2,1)S(1)} %add_convert_fusion.12), channel_id=1, source_target_pairs={{0,2},{2,4},{4,6},{6,7},{7,5},{5,3},{3,1},{1,0},{8,10},{10,12},{12... | collective-permute-start | bytes 2359304 | tf_op jit(solution)/shard_map/ppermute | solution.py:85
  309.5 28.6 %copy-start.11 = (bf16[512,2,768]{2,0,1:T(8,128)(2,1)S(1)}, bf16[512,2,768]{2,0,1:T(8,128)(2,1)}, u32[]{:S(2)}) copy-start(bf16[512,2,768]{2,0,1:T(8,128)(2,1)} %get-tuple-element.39) | copy-start | bytes 4718596
  309.5 36.6 %collective-permute-start.9 = (bf16[512,2,384]{2,0,1:T(8,128)(2,1)S(1)}, bf16[512,2,384]{2,0,1:T(8,128)(2,1)S(1)}, u32[]{:S(2)}, u32[]{:S(2)}) collective-permute-start(bf16[512,2,384]{2,0,1:T(8,128)(2,1)S(1)} %add_convert_fusion.5), channel_id=1, source_target_pairs={{0,1},{2,0},{4,2},{6,4},{7,6},{5,7},{3,5},{1,3},{8,9},{10,8},{12,1... | collective-permute-start | bytes 2359304 | tf_op jit(solution)/shard_map/ppermute | solution.py:87
  339.2 10.6 %copy-start.28 = (bf16[16,32,768]{2,1,0:T(8,128)(2,1)S(1)}, bf16[16,32,768]{2,1,0:T(8,128)(2,1)}, u32[]{:S(2)}) copy-start(bf16[16,32,768]{2,1,0:T(8,128)(2,1)} %copy-done.27) | copy-start | bytes 2359300
  339.2 37.6 %collective-permute-start.2 = (bf16[512,2,384]{2,0,1:T(8,128)(2,1)}, bf16[512,2,384]{2,0,1:T(8,128)(2,1)}, u32[]{:S(2)}, u32[]{:S(2)}) collective-permute-start(bf16[512,2,384]{2,0,1:T(8,128)(2,1)} %add_convert_fusion.11), channel_id=1, source_target_pairs={{0,2},{2,4},{4,6},{6,7},{7,5},{5,3},{3,1},{1,0},{8,10},{10,12},{12... | collective-permute-start | bytes 2359304 | tf_op jit(solution)/shard_map/ppermute | solution.py:85
  347.3 43.2 %collective-permute-start.10 = (bf16[512,2,384]{2,0,1:T(8,128)(2,1)}, bf16[512,2,384]{2,0,1:T(8,128)(2,1)S(1)}, u32[]{:S(2)}, u32[]{:S(2)}) collective-permute-start(bf16[512,2,384]{2,0,1:T(8,128)(2,1)} %add_convert_fusion.4), channel_id=1, source_target_pairs={{0,1},{2,0},{4,2},{6,4},{7,6},{5,7},{3,5},{1,3},{8,9},{10,8},{12,1... | collective-permute-start | bytes 2359304 | tf_op jit(solution)/shard_map/ppermute | solution.py:87
  357.8 156.5 %all-to-all-start.3 = ((bf16[16,32,4096]{2,1,0:T(8,128)(2,1)}), bf16[16,32,4096]{2,1,0:T(8,128)(2,1)}, u32[]{:S(2)}, u32[]{:S(2)}) async-start(bf16[16,32,4096]{2,1,0:T(8,128)(2,1)} %add_convert_fusion), calls=%async_computation.3 | async-start | bytes 8388608 | tf_op jit(solution)/shard_map/all_to_all | solution.py:134
  371.0 5.8 copy-start.10
  378.1 15.0 %copy-start.25 = (s32[256,1]{0,1:T(1,128)S(1)}, s32[256,1]{0,1:T(1,128)}, u32[]{:S(2)}) copy-start(s32[256,1]{0,1:T(1,128)} %copy-done.24) | copy-start | bytes 3076
  378.1 77.4 %collective-permute-start.3 = (bf16[512,2,384]{2,0,1:T(8,128)(2,1)S(1)}, bf16[512,2,384]{2,0,1:T(8,128)(2,1)S(1)}, u32[]{:S(2)}, u32[]{:S(2)}) collective-permute-start(bf16[512,2,384]{2,0,1:T(8,128)(2,1)S(1)} %add_convert_fusion.10), channel_id=1, source_target_pairs={{0,2},{2,4},{4,6},{6,7},{7,5},{5,3},{3,1},{1,0},{8,10},{10,12},{12... | collective-permute-start | bytes 2359304 | tf_op jit(solution)/shard_map/ppermute | solution.py:85
  390.7 79.8 %collective-permute-start.11 = (bf16[512,2,384]{2,0,1:T(8,128)(2,1)S(1)}, bf16[512,2,384]{2,0,1:T(8,128)(2,1)S(1)}, u32[]{:S(2)}, u32[]{:S(2)}) collective-permute-start(bf16[512,2,384]{2,0,1:T(8,128)(2,1)S(1)} %add_convert_fusion.3), channel_id=1, source_target_pairs={{0,1},{2,0},{4,2},{6,4},{7,6},{5,7},{3,5},{1,3},{8,9},{10,8},{12,1... | collective-permute-start | bytes 2359304 | tf_op jit(solution)/shard_map/ppermute | solution.py:87
  456.6 33.9 %collective-permute-start.4 = (bf16[512,2,384]{2,0,1:T(8,128)(2,1)}, bf16[512,2,384]{2,0,1:T(8,128)(2,1)}, u32[]{:S(2)}, u32[]{:S(2)}) collective-permute-start(bf16[512,2,384]{2,0,1:T(8,128)(2,1)} %add_convert_fusion.9), channel_id=1, source_target_pairs={{0,2},{2,4},{4,6},{6,7},{7,5},{5,3},{3,1},{1,0},{8,10},{10,12},{12... | collective-permute-start | bytes 2359304 | tf_op jit(solution)/shard_map/ppermute | solution.py:85
  478.1 5.2 copy-start.14
  480.8 19.1 %collective-permute-start.12 = (bf16[512,2,384]{2,0,1:T(8,128)(2,1)}, bf16[512,2,384]{2,0,1:T(8,128)(2,1)}, u32[]{:S(2)}, u32[]{:S(2)}) collective-permute-start(bf16[512,2,384]{2,0,1:T(8,128)(2,1)} %add_convert_fusion.2), channel_id=1, source_target_pairs={{0,1},{2,0},{4,2},{6,4},{7,6},{5,7},{3,5},{1,3},{8,9},{10,8},{12,1... | collective-permute-start | bytes 2359304 | tf_op jit(solution)/shard_map/ppermute | solution.py:87
  483.3 7.2 %copy-start.8 = (bf16[512,2,768]{2,0,1:T(8,128)(2,1)S(1)}, bf16[512,2,768]{2,0,1:T(8,128)(2,1)}, u32[]{:S(2)}) copy-start(bf16[512,2,768]{2,0,1:T(8,128)(2,1)} %get-tuple-element.43) | copy-start | bytes 4718596
  490.5 2.5 copy-start.21
  490.5 2.5 copy-start.23
  490.5 2.5 copy-start.19
  490.5 2.5 copy-start.4
  492.9 18.8 %collective-permute-start.5 = (bf16[512,2,384]{2,0,1:T(8,128)(2,1)}, bf16[512,2,384]{2,0,1:T(8,128)(2,1)}, u32[]{:S(2)}, u32[]{:S(2)}) collective-permute-start(bf16[512,2,384]{2,0,1:T(8,128)(2,1)} %add_convert_fusion.8), channel_id=1, source_target_pairs={{0,2},{2,4},{4,6},{6,7},{7,5},{5,3},{3,1},{1,0},{8,10},{10,12},{12... | collective-permute-start | bytes 2359304 | tf_op jit(solution)/shard_map/ppermute | solution.py:85
  495.4 16.4 %copy-start.7 = (bf16[512,2,768]{2,0,1:T(8,128)(2,1)S(1)}, bf16[512,2,768]{2,0,1:T(8,128)(2,1)}, u32[]{:S(2)}) copy-start(bf16[512,2,768]{2,0,1:T(8,128)(2,1)} %get-tuple-element.42) | copy-start | bytes 4718596
  502.4 22.6 %copy-start.5 = (bf16[128,2,4096]{2,1,0:T(2,128)(2,1)S(1)}, bf16[128,2,4096]{2,1,0:T(2,128)(2,1)}, u32[]{:S(2)}) copy-start(bf16[128,2,4096]{2,1,0:T(2,128)(2,1)} %reshape.199) | copy-start | bytes 6291460
  502.4 22.6 %copy-start.16 = (f32[128,2]{1,0:T(8,128)S(1)}, f32[128,2]{1,0:T(8,128)}, u32[]{:S(2)}) copy-start(f32[128,2]{1,0:T(8,128)} %copy-done.15) | copy-start | bytes 3076
  502.4 71.2 %collective-permute-start.13 = (bf16[512,2,384]{2,0,1:T(8,128)(2,1)}, bf16[512,2,384]{2,0,1:T(8,128)(2,1)S(1)}, u32[]{:S(2)}, u32[]{:S(2)}) collective-permute-start(bf16[512,2,384]{2,0,1:T(8,128)(2,1)} %add_convert_fusion.1), channel_id=1, source_target_pairs={{0,1},{2,0},{4,2},{6,4},{7,6},{5,7},{3,5},{1,3},{8,9},{10,8},{12,1... | collective-permute-start | bytes 2359304 | tf_op jit(solution)/shard_map/ppermute | solution.py:87
  514.0 61.0 %collective-permute-start.6 = (bf16[512,2,384]{2,0,1:T(8,128)(2,1)}, bf16[512,2,384]{2,0,1:T(8,128)(2,1)}, u32[]{:S(2)}, u32[]{:S(2)}) collective-permute-start(bf16[512,2,384]{2,0,1:T(8,128)(2,1)} %add_convert_fusion.7), channel_id=1, source_target_pairs={{0,2},{2,4},{4,6},{6,7},{7,5},{5,3},{3,1},{1,0},{8,10},{10,12},{12... | collective-permute-start | bytes 2359304 | tf_op jit(solution)/shard_map/ppermute | solution.py:85
  514.3 36.5 %all-to-all-start.4 = ((f32[128,1,512]{2,1,0:T(1,128)}), f32[128,1,512]{2,1,0:T(1,128)S(1)}, u32[]{:S(2)}, u32[]{:S(2)}) async-start(f32[128,1,512]{2,1,0:T(1,128)} %all_to_all.29), calls=%async_computation.4 | async-start | bytes 524288 | tf_op jit(solution)/shard_map/all_to_all | solution.py:58
  551.9 19.0 %all-to-all-start.5 = ((f32[128,1,512]{2,1,0:T(1,128)}), f32[128,1,512]{2,1,0:T(1,128)S(1)}, u32[]{:S(2)}, u32[]{:S(2)}) async-start(f32[128,1,512]{2,1,0:T(1,128)} %broadcast_in_dim.18), calls=%async_computation.5 | async-start | bytes 524288 | tf_op jit(solution)/shard_map/all_to_all | solution.py:60
  573.6 1.6 copy-start.6
Sparse Core Ops, SparseCore 0:
  162.8 306.7 reduce-scatter.1

commit v7 on v5

--- a/solution.py
+++ b/solution.py
@@ -124,10 +124,18 @@
     gate_part = jnp.einsum("nkd,nkh->dh", received, grad_gate, preferred_element_type=jnp.float32)
     up_part = jnp.einsum("nkd,nkh->dh", received, grad_up, preferred_element_type=jnp.float32)
     down_part = jnp.einsum("nkd,nkh->dh", grad_recv, hidden, preferred_element_type=jnp.float32)
-    down_total = lax.psum_scatter(
-        down_part.astype(jnp.bfloat16), "dp", scatter_dimension=0, tiled=True
+    hidden_count = up_part.shape[1]
+    split = hidden_count // 3
+    on_sparse = jnp.concatenate([down_part, up_part[:, :split]], axis=1)
+    on_sparse = lax.psum_scatter(
+        on_sparse.astype(jnp.bfloat16), "dp", scatter_dimension=0, tiled=True
     ).astype(jnp.float32)
-    gate_total, up_total = reduce_scatter_by_exchange((gate_part, up_part), "dp")
+    (exchanged,) = reduce_scatter_by_exchange(
+        (jnp.concatenate([gate_part, up_part[:, split:]], axis=1),), "dp"
+    )
+    down_total = on_sparse[:, :hidden_count]
+    gate_total = exchanged[:, :hidden_count]
+    up_total = jnp.concatenate([on_sparse[:, hidden_count:], exchanged[:, hidden_count:]], axis=1)
     gate_grad = (gate_total / replica_count).astype(jnp.bfloat16)[None]
     up_grad = (up_total / replica_count).astype(jnp.bfloat16)[None]
     down_grad = (down_total / replica_count).astype(jnp.bfloat16)[None]

time: 539 us -> 575 us (1.067)
  local copies, waits for them, and re-layouts: 54.5 us -> 73.6 us
  waiting for transfers between devices: 269 us -> 281 us
  other arithmetic: 41.6 us -> 47.5 us
    all_to_all x1, waiting for transfers between devices: 129 us -> 159 us  [reduce_scatter_by_exchange(): arrived = lax.all_to_all(blocks, axis, 0, 0, tiled=True)]
    all_to_all x1, waiting for transfers between devices: 29.3 us -> 7.44 us  [on_device(): lax.all_to_all(expert_out, 'expert', split_axis=0, concat_axis=0, tiled=T...]
    concatenate x0 -> x2, other arithmetic: none -> 16.8 us  [the longest x1 9.65 us: on_device(): jnp.concatenate([gate_part, up_part[:, split:]], axis=1)]
    another operation x3 -> x2, other arithmetic: 11.4 us -> 0.63 us  [the longest x1 10.8 us: reduce_scatter_by_exchange(): blocks = jnp.stack([p.astype(jnp.bfloat16) for p in parts], axis=1)]
    slice x1 -> x5, local copies, waits for them, and re-layouts: 0.18 us -> 9.45 us  [the longest x1 4.48 us: on_device(): up_part[:, split:]]
    unnamed x40 -> x45, local copies, waits for them, and re-layouts: 4.45 us -> 12.7 us
  transfers between devices with their start and end apart: 8 -> 8, of which waited for: 5 -> 6; matrix products, arithmetic and copies ran while one was open for 30% -> 32% of each run, Pallas kernels for 0% -> 0%
where the time goes in v7:
time: 575 us; the launch traced here: 567 us
  waiting for transfers between devices  281 us (49%)
  matrix products  80.9 us (14%)
  local copies, waits for them, and re-layouts  73.6 us (13%)
  starting transfers between devices  69.1 us (12%)
  other arithmetic  47.5 us (8%)
  between operations  14.9 us (3%)
    all_to_all x1, waiting for transfers between devices, reduce_scatter_by_exchange(): arrived = lax.all_to_all(blocks, axis, 0, 0, tiled=True)  159 us
    all_to_all x1, waiting for transfers between devices, on_device(): lax.all_to_all(grad_in, 'expert', split_axis=0, concat_axis=0, tiled=True)  47.4 us
    all_to_all x1, waiting for transfers between devices, on_device(): lax.all_to_all(outbound, 'expert', split_axis=0, concat_axis=0, tiled=True)  33.7 us
    all_to_all x1, waiting for transfers between devices, on_device(): lax.all_to_all(grad_out, 'expert', split_axis=0, concat_axis=0, tiled=True)  33.6 us
    all_to_all x1, starting transfers between devices, all_reduce_by_exchange(): lax.all_to_all(chunks, axes, 0, 0, tiled=True)  15.3 us
    unnamed x45, local copies, waits for them, and re-layouts  12.7 us
    all_to_all x1, starting transfers between devices, on_device(): lax.all_to_all(grad_out, 'expert', split_axis=0, concat_axis=0, tiled=True)  12.6 us
    all_to_all x1, starting transfers between devices, on_device(): lax.all_to_all(expert_out, 'expert', split_axis=0, concat_axis=0, tiled=T...  11.8 us
  transfers between devices with their start and end apart: 8, of which 6 were waited for; matrix products, arithmetic and copies ran while one was open for 32% of the time, Pallas kernels for 0%

profile of v7, /device:TPU:4, one launch (start us, length us, event | category | flops | bytes accessed | tf_op | source)
XLA Modules:
  0.0 567.1 jit_solution(18380464546146359783)
XLA Ops:
  7.2 0.7 broadcast_multiply_fusion
  7.9 0.8 copy.82
  9.2 0.6 reduce-window.6
  10.2 1.4 scatter_custom_fusion
  11.6 1.3 concatenate.39
  12.9 4.4 gather_fusion
  17.3 7.6 %all-to-all-start = ((bf16[16,32,4096]{2,1,0:T(8,128)(2,1)}), bf16[16,32,4096]{2,1,0:T(8,128)(2,1)}, u32[]{:S(2)}, u32[]{:S(2)}) async-start(bf16[16,32,4096]{2,1,0:T(8,128)(2,1)} %bitcast.108), calls=%async_computation | async-start | bytes 8388608 | tf_op jit(solution)/shard_map/all_to_all | solution.py:90
  25.5 2.0 gather_fusion.4
  28.1 4.1 mul.101
  32.2 6.1 %mul.102 = f32[256,4096]{1,0:T(8,128)} reshape(f32[128,2,4096]{2,1,0:T(2,128)} %mul.101) | data formatting | bytes 8388608 | tf_op jit(solution)/shard_map/mul | solution.py:91
  38.2 2.6 multiply_convert_fusion
  41.1 4.4 gather_fusion.1
  45.5 33.7 %all-to-all-done = bf16[16,32,4096]{2,1,0:T(8,128)(2,1)} async-done(((bf16[16,32,4096]{2,1,0:T(8,128)(2,1)}), bf16[16,32,4096]{2,1,0:T(8,128)(2,1)}, u32[]{:S(2)}, u32[]{:S(2)}) %all-to-all-start) | async-done | bytes 4194336 | tf_op jit(solution)/shard_map/all_to_all | solution.py:90
  79.2 12.6 %all-to-all-start.1 = ((bf16[16,32,4096]{2,1,0:T(8,128)(2,1)}), bf16[16,32,4096]{2,1,0:T(8,128)(2,1)}, u32[]{:S(2)}, u32[]{:S(2)}) async-start(bf16[16,32,4096]{2,1,0:T(8,128)(2,1)} %bitcast.109), calls=%async_computation.1 | async-start | bytes 8388608 | tf_op jit(solution)/shard_map/all_to_all | solution.py:96
  91.8 7.2 %fusion.10 = f32[16,32,768]{2,1,0:T(8,128)S(1)} fusion(bf16[16,32,4096]{2,1,0:T(8,128)(2,1)} %all-to-all-done, bf16[1,4096,768]{2,1,0:T(8,128)(2,1)} %param.11), kind=kOutput, calls=%fused_computation.23 | convolution fusion | flops 3221225472 | bytes 12058624 | tf_op jit(solution)/shard_map/...d,dh->...h/dot_general | solution.py:31
  99.1 7.4 %multiply_convert_fusion.4 = (bf16[16,32,768]{2,1,0:T(8,128)(2,1)S(1)}, f32[16,32,768]{2,1,0:T(8,128)}) fusion(f32[16,32,768]{2,1,0:T(8,128)S(1)} %fusion.10, bf16[16,32,4096]{2,1,0:T(8,128)(2,1)} %all-to-all-done, bf16[1,4096,768]{2,1,0:T(8,128)(2,1)S(1)} %bitcast.119), kind=kOutput, calls=%fused_computation.40 | convolution fusion | flops 3223584768 | bytes 14417920 | tf_op jit(solution)/shard_map/...d,dh->...h/dot_general | solution.py:32
  106.6 0.9 copy-done.13
  107.5 5.0 fusion.12
  112.4 33.6 %all-to-all-done.1 = bf16[16,32,4096]{2,1,0:T(8,128)(2,1)} async-done(((bf16[16,32,4096]{2,1,0:T(8,128)(2,1)}), bf16[16,32,4096]{2,1,0:T(8,128)(2,1)}, u32[]{:S(2)}, u32[]{:S(2)}) %all-to-all-start.1) | async-done | bytes 4194336 | tf_op jit(solution)/shard_map/all_to_all | solution.py:96
  146.0 11.8 %all-to-all-start.2 = ((bf16[16,32,4096]{2,1,0:T(8,128)(2,1)}), bf16[16,32,4096]{2,1,0:T(8,128)(2,1)}, u32[]{:S(2)}, u32[]{:S(2)}) async-start(bf16[16,32,4096]{2,1,0:T(8,128)(2,1)} %fusion.12), calls=%async_computation.2 | async-start | bytes 8388608 | tf_op jit(solution)/shard_map/all_to_all | solution.py:99
  158.1 9.0 %multiply_convert_fusion.3 = (bf16[16,32,768]{2,1,0:T(8,128)(2,1)}, bf16[16,32,768]{2,1,0:T(8,128)(2,1)S(1)}) fusion(f32[16,32,768]{2,1,0:T(8,128)S(1)} %copy-done.15, f32[16,32,768]{2,1,0:T(8,128)} %get-tuple-element.47, bf16[16,32,4096]{2,1,0:T(8,128)(2,1)} %all-to-all-done.1, bf16[1,4096,768]{2,1,0:T(8,128)(2,1)} %param.13), kind=kOutput, calls=%fused_computation.39 | convolution fusion | flops 3226337280 | bytes 15204352 | tf_op jit(solution)/shard_map/...d,dh->...h/dot_general | solution.py:42
  167.1 6.0 %bitcast_convert_fusion.1 = bf16[4096,768]{1,0:T(8,128)(2,1)S(1)} fusion(bf16[16,32,4096]{2,1,0:T(8,128)(2,1)} %all-to-all-done, bf16[16,32,768]{2,1,0:T(8,128)(2,1)S(1)} %get-tuple-element.43), kind=kOutput, calls=%fused_computation.8 | convolution fusion | flops 3224371200 | bytes 11272192 | tf_op jit(solution)/shard_map/nkd,nkh->dh/dot_general | solution.py:125
  173.1 2.7 copy-done.4
  176.0 3.4 copy.92
  179.4 8.6 %bitcast_convert_fusion = bf16[4096,768]{0,1:T(8,128)(2,1)} fusion(bf16[16,32,4096]{2,1,0:T(8,128)(2,1)} %all-to-all-done.1, bf16[16,32,768]{2,1,0:T(8,128)(2,1)} %copy-done.13), kind=kOutput, calls=%fused_computation.7 | convolution fusion | flops 3224371200 | bytes 11272192 | tf_op jit(solution)/shard_map/nkd,nkh->dh/dot_general | solution.py:126
  187.9 7.1 %pad_maximum_fusion.1 = bf16[4096,1024]{0,1:T(8,128)(2,1)} fusion(bf16[4096,256]{0,1:T(8,128)(2,1)S(1)} %copy-done.3, bf16[4096,768]{0,1:T(8,128)(2,1)} %bitcast_convert_fusion), kind=kLoop, calls=%fused_computation.11 | loop fusion | flops 16777216 | bytes 16777216 | tf_op jit(solution)/shard_map/concatenate | solution.py:129
  195.1 1.1 copy-done.12
  196.2 8.5 %fusion.4 = f32[16,32,4096]{2,1,0:T(8,128)} fusion(bf16[16,32,768]{2,1,0:T(8,128)(2,1)S(1)} %copy-done.12, bf16[1,4096,768]{2,1,0:T(8,128)(2,1)} %param.12), kind=kOutput, calls=%fused_computation.17 | convolution fusion | flops 3221225472 | bytes 15466496 | tf_op jit(solution)/shard_map/...h,dh->...d/dot_general | solution.py:49
  204.7 7.4 %all-to-all-done.2 = bf16[16,32,4096]{2,1,0:T(8,128)(2,1)} async-done(((bf16[16,32,4096]{2,1,0:T(8,128)(2,1)}), bf16[16,32,4096]{2,1,0:T(8,128)(2,1)}, u32[]{:S(2)}, u32[]{:S(2)}) %all-to-all-start.2) | async-done | bytes 4194336 | tf_op jit(solution)/shard_map/all_to_all | solution.py:99
  212.1 6.6 %gather_fusion.2 = bf16[256,4096]{1,0:T(8,128)(2,1)S(1)} fusion(bf16[512,4096]{1,0:T(8,128)(2,1)} %bitcast.12, s32[1024]{0:T(1024)S(1)} %pad_clamp_fusion), kind=kCustom, calls=%fused_computation.2 | custom fusion | bytes 4195328 | tf_op jit(solution)/shard_map/gather | solution.py:102
  218.8 2.8 reshape.195
  221.6 7.3 %fusion.18 = f32[128,1,2]{2,1,0:T(1,128)S(1)} fusion(bf16[128,2,4096]{2,1,0:T(2,128)(2,1)} %reshape.195, bf16[128,4096,1]{1,0,2:T(8,128)(2,1)} %bitcast.112), kind=kOutput, calls=%fused_computation.31 | convolution fusion | flops 2097152 | bytes 3146752 | tf_op jit(solution)/shard_map/td,tkd->tk/dot_general | solution.py:106
  229.1 1.0 convolution_bitcast_fusion
  230.0 1.5 copy.86
  231.6 1.5 all_to_all.33
  233.0 15.3 %all-to-all-start.4 = ((f32[128,1,512]{2,1,0:T(1,128)}), f32[128,1,512]{2,1,0:T(1,128)S(1)}, u32[]{:S(2)}, u32[]{:S(2)}) async-start(f32[128,1,512]{2,1,0:T(1,128)} %all_to_all.33), calls=%async_computation.4 | async-start | bytes 524288 | tf_op jit(solution)/shard_map/all_to_all | solution.py:58
  248.3 10.8 %add_convert_fusion = bf16[16,32,4096]{2,1,0:T(8,128)(2,1)} fusion(f32[16,32,4096]{2,1,0:T(8,128)} %fusion.4, bf16[16,32,768]{2,1,0:T(8,128)(2,1)} %get-tuple-element.42, bf16[1,4096,768]{2,1,0:T(8,128)(2,1)} %param.11), kind=kOutput, calls=%fused_computation.12 | convolution fusion | flops 3225419776 | bytes 19660800 | tf_op jit(solution)/shard_map/...h,dh->...d/dot_general | solution.py:48
  259.1 7.2 %all-to-all-start.3 = ((bf16[16,32,4096]{2,1,0:T(8,128)(2,1)}), bf16[16,32,4096]{2,1,0:T(8,128)(2,1)}, u32[]{:S(2)}, u32[]{:S(2)}) async-start(bf16[16,32,4096]{2,1,0:T(8,128)(2,1)} %add_convert_fusion), calls=%async_computation.3 | async-start | bytes 8388608 | tf_op jit(solution)/shard_map/all_to_all | solution.py:115
  266.4 4.5 slice.45
  270.9 8.3 %bitcast_convert_fusion.2 = bf16[4096,768]{1,0:T(8,128)(2,1)} fusion(bf16[16,32,4096]{2,1,0:T(8,128)(2,1)} %all-to-all-done, bf16[16,32,768]{2,1,0:T(8,128)(2,1)S(1)} %copy-done.10), kind=kOutput, calls=%fused_computation.9 | convolution fusion | flops 3224371200 | bytes 11272192 | tf_op jit(solution)/shard_map/nkd,nkh->dh/dot_general | solution.py:124
  279.4 47.4 %all-to-all-done.3 = bf16[16,32,4096]{2,1,0:T(8,128)(2,1)} async-done(((bf16[16,32,4096]{2,1,0:T(8,128)(2,1)}), bf16[16,32,4096]{2,1,0:T(8,128)(2,1)}, u32[]{:S(2)}, u32[]{:S(2)}) %all-to-all-start.3) | async-done | bytes 4194336 | tf_op jit(solution)/shard_map/all_to_all | solution.py:115
  326.8 0.8 broadcast_in_dim.20
  327.6 8.8 %all-to-all-start.5 = ((f32[128,1,512]{2,1,0:T(1,128)}), f32[128,1,512]{2,1,0:T(1,128)S(1)}, u32[]{:S(2)}, u32[]{:S(2)}) async-start(f32[128,1,512]{2,1,0:T(1,128)} %broadcast_in_dim.20), calls=%async_computation.5 | async-start | bytes 524288 | tf_op jit(solution)/shard_map/all_to_all | solution.py:60
  336.4 9.7 %pad_maximum_fusion = bf16[8,512,1,1280]{3,1,2,0:T(8,128)(2,1)} fusion(bf16[8,512,1,512]{3,1,2,0:T(8,128)(2,1)} %bitcast.110, bf16[8,512,1,768]{3,1,2,0:T(8,128)(2,1)} %bitcast.111), kind=kLoop, calls=%fused_computation.10 | loop fusion | flops 20971520 | bytes 20971520 | tf_op jit(solution)/shard_map/concatenate | solution.py:134
  346.2 5.6 all-to-all-start.6
  351.7 6.7 %gather_fusion.3 = bf16[256,4096]{1,0:T(8,128)(2,1)S(1)} fusion(bf16[512,4096]{1,0:T(8,128)(2,1)} %bitcast.13, s32[1024]{0:T(1024)S(1)} %pad_clamp_fusion), kind=kCustom, calls=%fused_computation.3 | custom fusion | bytes 4195328 | tf_op jit(solution)/shard_map/gather | solution.py:119
  358.4 4.2 reshape.197
  362.6 7.5 %reduce_sum.78 = f32[128,4096]{1,0:T(8,128)S(1)} reduce(f32[128,2,4096]{2,1,0:T(2,128)} %reshape.197, f32[]{:T(128)} %constant.56.clone.1), dimensions={1}, to_apply=%region_6.7 | reduce | flops 524288 | bytes 6291460 | tf_op jit(solution)/shard_map/reduce_sum | solution.py:118
  370.1 1.4 fusion.17
  371.6 0.5 copy-done.2
  372.1 8.0 %multiply_reduce_fusion = bf16[128,4096]{1,0:T(8,128)(2,1)} fusion(bf16[128,2,4096]{2,1,0:T(2,128)(2,1)S(1)} %copy-done.2, f32[128,2]{1,0:T(8,128)S(1)} %copy-done.8), kind=kLoop, calls=%fused_computation.29 | loop fusion | flops 2621440 | bytes 3146752 | tf_op jit(solution)/shard_map/reduce_sum | solution.py:103
  380.1 0.7 multiply_reduce_fusion.1
  380.8 0.7 div.45
  381.6 1.3 copy.94
  382.8 158.9 %all-to-all-done.6 = bf16[8,512,1,1280]{3,1,2,0:T(8,128)(2,1)} async-done(((bf16[8,512,1,1280]{3,1,2,0:T(8,128)(2,1)}), bf16[8,512,1,1280]{3,1,2,0:T(8,128)(2,1)}, u32[]{:S(2)}, u32[]{:S(2)}) %all-to-all-start.6) | async-done | bytes 10485792 | tf_op jit(solution)/shard_map/all_to_all | solution.py:69
  541.7 5.7 convert_reduce_fusion
  547.4 1.3 slice.46
  548.6 3.0 copy.99
  551.7 1.6 fusion.23
  553.3 1.2 copy.95
  554.4 1.2 slice_bitcast_fusion
  555.6 1.6 convert_element_type.97
  557.4 1.2 copy.96
  558.8 1.0 fusion.21
  (77 shorter events, 3.6 us)
Async XLA Ops:
  7.2 18.0 %copy-start = (bf16[4096,16]{0,1:T(8,128)(2,1)S(1)}, bf16[4096,16]{0,1:T(8,128)(2,1)}, u32[]{:S(2)}) copy-start(bf16[4096,16]{0,1:T(8,128)(2,1)} %param.10) | copy-start | bytes 393220
  17.3 7.6 %copy-start.9 = (s32[128,2]{0,1:T(2,128)S(1)}, s32[128,2]{0,1:T(2,128)}, u32[]{:S(2)}) copy-start(s32[128,2]{0,1:T(2,128)} %param.9) | copy-start | bytes 3076
  17.3 7.9 %copy-start.1 = (bf16[128,4096]{1,0:T(8,128)(2,1)S(1)}, bf16[128,4096]{1,0:T(8,128)(2,1)}, u32[]{:S(2)}) copy-start(bf16[128,4096]{1,0:T(8,128)(2,1)} %param.7) | copy-start | bytes 3145732
  17.3 61.9 %all-to-all-start = ((bf16[16,32,4096]{2,1,0:T(8,128)(2,1)}), bf16[16,32,4096]{2,1,0:T(8,128)(2,1)}, u32[]{:S(2)}, u32[]{:S(2)}) async-start(bf16[16,32,4096]{2,1,0:T(8,128)(2,1)} %bitcast.108), calls=%async_computation | async-start | bytes 8388608 | tf_op jit(solution)/shard_map/all_to_all | solution.py:90
  25.5 2.5 copy-start.6
  27.9 10.3 %copy-start.7 = (f32[128,2]{1,0:T(8,128)}, f32[128,2]{1,0:T(8,128)S(1)}, u32[]{:S(2)}) copy-start(f32[128,2]{1,0:T(8,128)S(1)} %copy.80) | copy-start | bytes 3076
  79.2 19.9 %slice-start.2 = ((s8[6291456]{0:T(1024)(128)(4,1)}), s8[2097152]{0:T(1024)(128)(4,1)S(1)}, s32[]{:S(2)}) async-start(s8[6291456]{0:T(1024)(128)(4,1)} %bitcast.118), calls=%async_computation.11 | async-start | bytes 4194304
  79.2 66.8 %all-to-all-start.1 = ((bf16[16,32,4096]{2,1,0:T(8,128)(2,1)}), bf16[16,32,4096]{2,1,0:T(8,128)(2,1)}, u32[]{:S(2)}, u32[]{:S(2)}) async-start(bf16[16,32,4096]{2,1,0:T(8,128)(2,1)} %bitcast.109), calls=%async_computation.1 | async-start | bytes 8388608 | tf_op jit(solution)/shard_map/all_to_all | solution.py:96
  91.8 7.3 %slice-start.3 = ((s8[6291456]{0:T(1024)(128)(4,1)}), s8[4194304]{0:T(1024)(128)(4,1)S(1)}, s32[]{:S(2)}) async-start(s8[6291456]{0:T(1024)(128)(4,1)} %bitcast.118), calls=%async_computation.12 | async-start | bytes 8388608
  91.8 15.6 %slice-start = ((s8[6291456]{0:T(1024)(128)(4,1)}), s8[4194304]{0:T(1024)(128)(4,1)S(1)}, s32[]{:S(2)}) async-start(s8[6291456]{0:T(1024)(128)(4,1)} %bitcast.116), calls=%async_computation.9 | async-start | bytes 8388608
  99.1 7.5 %copy-start.14 = (f32[16,32,768]{2,1,0:T(8,128)}, f32[16,32,768]{2,1,0:T(8,128)S(1)}, u32[]{:S(2)}) copy-start(f32[16,32,768]{2,1,0:T(8,128)S(1)} %fusion.10) | copy-start | bytes 4718596
  99.1 8.3 %slice-start.1 = ((s8[6291456]{0:T(1024)(128)(4,1)}), s8[2097152]{0:T(1024)(128)(4,1)S(1)}, s32[]{:S(2)}) async-start(s8[6291456]{0:T(1024)(128)(4,1)} %bitcast.116), calls=%async_computation.10 | async-start | bytes 4194304
  106.6 0.9 copy-start.13
  112.4 45.7 %copy-start.15 = (f32[16,32,768]{2,1,0:T(8,128)S(1)}, f32[16,32,768]{2,1,0:T(8,128)}, u32[]{:S(2)}) copy-start(f32[16,32,768]{2,1,0:T(8,128)} %copy-done.14) | copy-start | bytes 4718596
  146.0 66.1 %all-to-all-start.2 = ((bf16[16,32,4096]{2,1,0:T(8,128)(2,1)}), bf16[16,32,4096]{2,1,0:T(8,128)(2,1)}, u32[]{:S(2)}, u32[]{:S(2)}) async-start(bf16[16,32,4096]{2,1,0:T(8,128)(2,1)} %fusion.12), calls=%async_computation.2 | async-start | bytes 8388608 | tf_op jit(solution)/shard_map/all_to_all | solution.py:99
  157.8 397.8 %reduce-scatter.2.cloned.1.call-start = ((), (), s32[]{:S(2)}) async-start(), calls=%async_computation.8 | async-start | bytes 9437184 | tf_op jit(solution)/shard_map/reduce_scatter | solution.py:130
  167.1 6.0 %copy-start.11 = (bf16[16,32,768]{2,1,0:T(8,128)(2,1)}, bf16[16,32,768]{2,1,0:T(8,128)(2,1)S(1)}, u32[]{:S(2)}) copy-start(bf16[16,32,768]{2,1,0:T(8,128)(2,1)S(1)} %get-tuple-element.43) | copy-start | bytes 2359300
  173.1 2.7 copy-start.4
  179.4 8.6 %copy-start.3 = (bf16[4096,256]{0,1:T(8,128)(2,1)S(1)}, bf16[4096,256]{0,1:T(8,128)(2,1)}, u32[]{:S(2)}) copy-start(bf16[4096,256]{0,1:T(8,128)(2,1)} %copy.92) | copy-start | bytes 6291460
  195.1 1.1 copy-start.12
  233.0 26.1 %all-to-all-start.4 = ((f32[128,1,512]{2,1,0:T(1,128)}), f32[128,1,512]{2,1,0:T(1,128)S(1)}, u32[]{:S(2)}, u32[]{:S(2)}) async-start(f32[128,1,512]{2,1,0:T(1,128)} %all_to_all.33), calls=%async_computation.4 | async-start | bytes 524288 | tf_op jit(solution)/shard_map/all_to_all | solution.py:58
  259.1 67.6 %all-to-all-start.3 = ((bf16[16,32,4096]{2,1,0:T(8,128)(2,1)}), bf16[16,32,4096]{2,1,0:T(8,128)(2,1)}, u32[]{:S(2)}, u32[]{:S(2)}) async-start(bf16[16,32,4096]{2,1,0:T(8,128)(2,1)} %add_convert_fusion), calls=%async_computation.3 | async-start | bytes 8388608 | tf_op jit(solution)/shard_map/all_to_all | solution.py:115
  266.4 4.5 copy-start.10
  327.6 18.5 %all-to-all-start.5 = ((f32[128,1,512]{2,1,0:T(1,128)}), f32[128,1,512]{2,1,0:T(1,128)S(1)}, u32[]{:S(2)}, u32[]{:S(2)}) async-start(f32[128,1,512]{2,1,0:T(1,128)} %broadcast_in_dim.20), calls=%async_computation.5 | async-start | bytes 524288 | tf_op jit(solution)/shard_map/all_to_all | solution.py:60
  346.2 195.5 %all-to-all-start.6 = ((bf16[8,512,1,1280]{3,1,2,0:T(8,128)(2,1)}), bf16[8,512,1,1280]{3,1,2,0:T(8,128)(2,1)}, u32[]{:S(2)}, u32[]{:S(2)}) async-start(bf16[8,512,1,1280]{3,1,2,0:T(8,128)(2,1)} %pad_maximum_fusion), calls=%async_computation.6 | async-start | bytes 20971520 | tf_op jit(solution)/shard_map/all_to_all | solution.py:69
  362.6 9.0 %copy-start.8 = (f32[128,2]{1,0:T(8,128)S(1)}, f32[128,2]{1,0:T(8,128)}, u32[]{:S(2)}) copy-start(f32[128,2]{1,0:T(8,128)} %copy-done.7) | copy-start | bytes 3076
  370.1 2.0 copy-start.2
  555.6 3.2 copy-start.5
Sparse Core Ops, SparseCore 0:
  195.2 303.0 reduce-scatter.1

commit v8 on v5

--- a/solution.py
+++ b/solution.py
@@ -62,13 +62,12 @@
 
 def reduce_scatter_by_exchange(parts, axis):
     replica_count = lax.axis_size(axis)
-    rows = parts[0].shape[0] // replica_count
-    blocks = jnp.stack([p.astype(jnp.bfloat16) for p in parts], axis=1)
-    blocks = blocks.reshape((replica_count, rows) + blocks.shape[1:])
-    blocks = blocks.reshape(replica_count, rows, len(parts), parts[0].shape[1])
-    arrived = lax.all_to_all(blocks, axis, 0, 0, tiled=True)
-    total = jnp.sum(arrived.astype(jnp.float32), axis=0)
-    return tuple(total[:, i] for i in range(len(parts)))
+    pieces, row_count, width = parts.shape
+    blocks = parts.astype(jnp.bfloat16).reshape(
+        pieces, replica_count, row_count // replica_count, width
+    )
+    arrived = lax.all_to_all(blocks, axis, 1, 1, tiled=True)
+    return jnp.sum(arrived.astype(jnp.float32), axis=1)
 
 
 def on_device(tokens, cotangent, expert_ids, router_w, w_gate, w_up, w_down):
@@ -121,13 +120,16 @@
     )
     grad_tokens = grad_tokens + jnp.dot(grad_logits, router_w.T, preferred_element_type=jnp.float32)
     d_tokens = grad_tokens.astype(jnp.bfloat16)
-    gate_part = jnp.einsum("nkd,nkh->dh", received, grad_gate, preferred_element_type=jnp.float32)
-    up_part = jnp.einsum("nkd,nkh->dh", received, grad_up, preferred_element_type=jnp.float32)
+    grad_pair = jnp.stack([grad_gate, grad_up], axis=0)
+    pair_part = jnp.einsum(
+        "nkd,pnkh->pdh", received, grad_pair, preferred_element_type=jnp.float32
+    )
     down_part = jnp.einsum("nkd,nkh->dh", grad_recv, hidden, preferred_element_type=jnp.float32)
     down_total = lax.psum_scatter(
         down_part.astype(jnp.bfloat16), "dp", scatter_dimension=0, tiled=True
     ).astype(jnp.float32)
-    gate_total, up_total = reduce_scatter_by_exchange((gate_part, up_part), "dp")
+    pair_total = reduce_scatter_by_exchange(pair_part, "dp")
+    gate_total, up_total = pair_total[0], pair_total[1]
     gate_grad = (gate_total / replica_count).astype(jnp.bfloat16)[None]
     up_grad = (up_total / replica_count).astype(jnp.bfloat16)[None]
     down_grad = (down_total / replica_count).astype(jnp.bfloat16)[None]

time: 539 us -> 604 us (1.12)
  waiting for transfers between devices: 269 us -> 337 us
  other arithmetic: 41.6 us -> 31.1 us
  local copies, waits for them, and re-layouts: 54.5 us -> 64.4 us
  matrix products: 81.4 us -> 73.5 us
    all_to_all x1, waiting for transfers between devices: 129 us -> 186 us  [reduce_scatter_by_exchange(): arrived = lax.all_to_all(blocks, axis, 1, 1, tiled=True)]
    another operation x3 -> x2, other arithmetic: 11.4 us -> 0.63 us  [the longest x1 10.8 us: reduce_scatter_by_exchange(): blocks = jnp.stack([p.astype(jnp.bfloat16) for p in parts], axis=1)]
    all_to_all x1, waiting for transfers between devices: 29.3 us -> 38 us  [on_device(): lax.all_to_all(expert_out, 'expert', split_axis=0, concat_axis=0, tiled=T...]
    dot_general x2 -> x1, matrix products: 16.7 us -> 9.2 us  [on_device(): jnp.einsum('nkd,pnkh->pdh', received, grad_pair, preferred_element_type=j...]
  transfers between devices with their start and end apart: 8 -> 8, of which waited for: 5 -> 5; matrix products, arithmetic and copies ran while one was open for 30% -> 22% of each run, Pallas kernels for 0% -> 0%
where the time goes in v8:
time: 604 us; the launch traced here: 595 us
  waiting for transfers between devices  337 us (56%)
  starting transfers between devices  74.8 us (12%)
  matrix products  73.5 us (12%)
  local copies, waits for them, and re-layouts  64.4 us (11%)
  other arithmetic  31.1 us (5%)
  between operations  14.7 us (2%)
    all_to_all x1, waiting for transfers between devices, reduce_scatter_by_exchange(): arrived = lax.all_to_all(blocks, axis, 1, 1, tiled=True)  186 us
    all_to_all x1, waiting for transfers between devices, on_device(): lax.all_to_all(grad_in, 'expert', split_axis=0, concat_axis=0, tiled=True)  46 us
    all_to_all x1, waiting for transfers between devices, on_device(): lax.all_to_all(expert_out, 'expert', split_axis=0, concat_axis=0, tiled=T...  38 us
    all_to_all x1, waiting for transfers between devices, on_device(): lax.all_to_all(outbound, 'expert', split_axis=0, concat_axis=0, tiled=True)  33.7 us
    all_to_all x1, waiting for transfers between devices, on_device(): lax.all_to_all(grad_out, 'expert', split_axis=0, concat_axis=0, tiled=True)  33.6 us
    all_to_all x1, starting transfers between devices, all_reduce_by_exchange(): lax.all_to_all(chunks, axes, 0, 0, tiled=True)  14.8 us
    all_to_all x1, starting transfers between devices, all_reduce_by_exchange(): return lax.all_to_all(spread, axes, 0, 0, tiled=True).reshape(part.shape)  14.6 us
    all_to_all x1, starting transfers between devices, on_device(): lax.all_to_all(grad_out, 'expert', split_axis=0, concat_axis=0, tiled=True)  12.5 us
  transfers between devices with their start and end apart: 8, of which 5 were waited for; matrix products, arithmetic and copies ran while one was open for 22% of the time, Pallas kernels for 0%

profile of v8, /device:TPU:4, one launch (start us, length us, event | category | flops | bytes accessed | tf_op | source)
XLA Modules:
  0.0 595.3 jit_solution(8312512762865853593)
XLA Ops:
  7.2 0.7 broadcast_multiply_fusion
  7.9 0.8 copy.66
  8.7 0.1 eq.42
  8.8 0.1 eq.38
  9.1 0.1 mul.95
  9.2 0.6 reduce-window.6
  9.8 0.2 slice_reduce_fusion
  10.2 1.4 scatter_custom_fusion
  11.6 1.3 concatenate.6
  12.9 4.4 gather_fusion
  17.3 7.6 %all-to-all-start = ((bf16[16,32,4096]{2,1,0:T(8,128)(2,1)}), bf16[16,32,4096]{2,1,0:T(8,128)(2,1)}, u32[]{:S(2)}, u32[]{:S(2)}) async-start(bf16[16,32,4096]{2,1,0:T(8,128)(2,1)} %bitcast.99), calls=%async_computation | async-start | bytes 8388608 | tf_op jit(solution)/shard_map/all_to_all | solution.py:89
  25.0 0.1 reshape.169
  25.2 0.4 fusion.42
  25.6 2.0 gather_fusion.4
  27.9 0.1 mul.99
  28.1 4.1 mul.101
  32.2 6.0 %mul.102 = f32[256,4096]{1,0:T(8,128)} reshape(f32[128,2,4096]{2,1,0:T(2,128)} %mul.101) | data formatting | bytes 8388608 | tf_op jit(solution)/shard_map/mul | solution.py:90
  38.2 2.6 multiply_convert_fusion
  40.9 0.3 concatenate.7
  41.1 4.4 gather_fusion.1
  45.6 33.7 %all-to-all-done = bf16[16,32,4096]{2,1,0:T(8,128)(2,1)} async-done(((bf16[16,32,4096]{2,1,0:T(8,128)(2,1)}), bf16[16,32,4096]{2,1,0:T(8,128)(2,1)}, u32[]{:S(2)}, u32[]{:S(2)}) %all-to-all-start) | async-done | bytes 4194336 | tf_op jit(solution)/shard_map/all_to_all | solution.py:89
  79.2 12.5 %all-to-all-start.1 = ((bf16[16,32,4096]{2,1,0:T(8,128)(2,1)}), bf16[16,32,4096]{2,1,0:T(8,128)(2,1)}, u32[]{:S(2)}, u32[]{:S(2)}) async-start(bf16[16,32,4096]{2,1,0:T(8,128)(2,1)} %bitcast.100), calls=%async_computation.1 | async-start | bytes 8388608 | tf_op jit(solution)/shard_map/all_to_all | solution.py:95
  91.8 7.2 %fusion.10 = f32[16,32,768]{2,1,0:T(8,128)S(1)} fusion(bf16[16,32,4096]{2,1,0:T(8,128)(2,1)} %all-to-all-done, bf16[1,4096,768]{2,1,0:T(8,128)(2,1)} %param.11), kind=kOutput, calls=%fused_computation.21 | convolution fusion | flops 3221225472 | bytes 12058624 | tf_op jit(solution)/shard_map/...d,dh->...h/dot_general | solution.py:31
  99.1 7.4 %multiply_convert_fusion.4 = (bf16[16,32,768]{2,1,0:T(8,128)(2,1)S(1)}, f32[16,32,768]{2,1,0:T(8,128)}) fusion(f32[16,32,768]{2,1,0:T(8,128)S(1)} %fusion.10, bf16[16,32,4096]{2,1,0:T(8,128)(2,1)} %all-to-all-done, bf16[1,4096,768]{2,1,0:T(8,128)(2,1)S(1)} %bitcast.109), kind=kOutput, calls=%fused_computation.42 | convolution fusion | flops 3223584768 | bytes 14417920 | tf_op jit(solution)/shard_map/...d,dh->...h/dot_general | solution.py:32
  106.4 0.9 copy-done.11
  107.3 5.0 fusion.12
  112.4 33.6 %all-to-all-done.1 = bf16[16,32,4096]{2,1,0:T(8,128)(2,1)} async-done(((bf16[16,32,4096]{2,1,0:T(8,128)(2,1)}), bf16[16,32,4096]{2,1,0:T(8,128)(2,1)}, u32[]{:S(2)}, u32[]{:S(2)}) %all-to-all-start.1) | async-done | bytes 4194336 | tf_op jit(solution)/shard_map/all_to_all | solution.py:95
  146.0 12.3 %all-to-all-start.2 = ((bf16[16,32,4096]{2,1,0:T(8,128)(2,1)}), bf16[16,32,4096]{2,1,0:T(8,128)(2,1)}, u32[]{:S(2)}, u32[]{:S(2)}) async-start(bf16[16,32,4096]{2,1,0:T(8,128)(2,1)} %fusion.12), calls=%async_computation.2 | async-start | bytes 8388608 | tf_op jit(solution)/shard_map/all_to_all | solution.py:98
  158.3 9.6 %multiply_convert_fusion.3 = (bf16[16,32,768]{2,1,0:T(8,128)(2,1)}, bf16[16,32,768]{2,1,0:T(8,128)(2,1)S(1)}) fusion(f32[16,32,768]{2,1,0:T(8,128)} %copy-done.10, f32[16,32,768]{2,1,0:T(8,128)} %get-tuple-element.43, bf16[16,32,4096]{2,1,0:T(8,128)(2,1)} %all-to-all-done.1, bf16[1,4096,768]{2,1,0:T(8,128)(2,1)} %param.13), kind=kOutput, calls=%fused_computation.41 | convolution fusion | flops 3226337280 | bytes 15204352 | tf_op jit(solution)/shard_map/...d,dh->...h/dot_general | solution.py:42
  167.9 0.9 copy-done.8
  168.8 5.7 fusion.4
  174.5 38.0 %all-to-all-done.2 = bf16[16,32,4096]{2,1,0:T(8,128)(2,1)} async-done(((bf16[16,32,4096]{2,1,0:T(8,128)(2,1)}), bf16[16,32,4096]{2,1,0:T(8,128)(2,1)}, u32[]{:S(2)}, u32[]{:S(2)}) %all-to-all-start.2) | async-done | bytes 4194336 | tf_op jit(solution)/shard_map/all_to_all | solution.py:98
  212.5 6.6 %gather_fusion.2 = bf16[256,4096]{1,0:T(8,128)(2,1)S(1)} fusion(bf16[512,4096]{1,0:T(8,128)(2,1)} %bitcast.12, s32[1024]{0:T(1024)S(1)} %pad_clamp_fusion), kind=kCustom, calls=%fused_computation.2 | custom fusion | bytes 4195328 | tf_op jit(solution)/shard_map/gather | solution.py:101
  219.1 2.9 reshape.133
  222.0 7.3 %fusion.19 = f32[128,1,2]{2,1,0:T(1,128)S(1)} fusion(bf16[128,2,4096]{2,1,0:T(2,128)(2,1)} %reshape.133, bf16[128,4096,1]{1,0,2:T(8,128)(2,1)} %bitcast.102), kind=kOutput, calls=%fused_computation.30 | convolution fusion | flops 2097152 | bytes 3146752 | tf_op jit(solution)/shard_map/td,tkd->tk/dot_general | solution.py:105
  229.5 1.0 convolution_bitcast_fusion
  230.4 1.5 copy.70
  232.0 1.5 all_to_all.33
  233.4 14.8 %all-to-all-start.4 = ((f32[128,1,512]{2,1,0:T(1,128)}), f32[128,1,512]{2,1,0:T(1,128)S(1)}, u32[]{:S(2)}, u32[]{:S(2)}) async-start(f32[128,1,512]{2,1,0:T(1,128)} %all_to_all.33), calls=%async_computation.4 | async-start | bytes 524288 | tf_op jit(solution)/shard_map/all_to_all | solution.py:58
  248.3 10.8 %add_convert_fusion = bf16[16,32,4096]{2,1,0:T(8,128)(2,1)} fusion(f32[16,32,4096]{2,1,0:T(8,128)} %fusion.4, bf16[16,32,768]{2,1,0:T(8,128)(2,1)} %get-tuple-element.38, bf16[1,4096,768]{2,1,0:T(8,128)(2,1)} %param.11), kind=kOutput, calls=%fused_computation.10 | convolution fusion | flops 3225419776 | bytes 19660800 | tf_op jit(solution)/shard_map/...h,dh->...d/dot_general | solution.py:48
  259.1 7.4 %all-to-all-start.3 = ((bf16[16,32,4096]{2,1,0:T(8,128)(2,1)}), bf16[16,32,4096]{2,1,0:T(8,128)(2,1)}, u32[]{:S(2)}, u32[]{:S(2)}) async-start(bf16[16,32,4096]{2,1,0:T(8,128)(2,1)} %add_convert_fusion), calls=%async_computation.3 | async-start | bytes 8388608 | tf_op jit(solution)/shard_map/all_to_all | solution.py:114
  266.5 8.4 %bitcast_convert_fusion.1 = bf16[4096,768]{1,0:T(8,128)(2,1)} fusion(bf16[16,32,4096]{2,1,0:T(8,128)(2,1)} %all-to-all-done.1, bf16[16,32,768]{2,1,0:T(8,128)(2,1)S(1)} %copy-done.12), kind=kOutput, calls=%fused_computation.9 | convolution fusion | flops 3224371200 | bytes 11272192 | tf_op jit(solution)/shard_map/nkd,nkh->dh/dot_general | solution.py:127
  274.9 0.2 reduce_sum.81
  275.2 46.0 %all-to-all-done.3 = bf16[16,32,4096]{2,1,0:T(8,128)(2,1)} async-done(((bf16[16,32,4096]{2,1,0:T(8,128)(2,1)}), bf16[16,32,4096]{2,1,0:T(8,128)(2,1)}, u32[]{:S(2)}, u32[]{:S(2)}) %all-to-all-start.3) | async-done | bytes 4194336 | tf_op jit(solution)/shard_map/all_to_all | solution.py:114
  321.1 0.8 broadcast_in_dim.18
  322.0 14.6 %all-to-all-start.5 = ((f32[128,1,512]{2,1,0:T(1,128)}), f32[128,1,512]{2,1,0:T(1,128)S(1)}, u32[]{:S(2)}, u32[]{:S(2)}) async-start(f32[128,1,512]{2,1,0:T(1,128)} %broadcast_in_dim.18), calls=%async_computation.5 | async-start | bytes 524288 | tf_op jit(solution)/shard_map/all_to_all | solution.py:60
  336.6 9.2 %bitcast_convert_fusion = bf16[2,768,4096]{2,1,0:T(8,128)(2,1)S(1)} fusion(bf16[16,32,4096]{2,1,0:T(8,128)(2,1)} %all-to-all-done, bf16[1,16,32,768]{3,2,1,0:T(8,128)(2,1)S(1)} %bitcast.113, bf16[1,16,32,768]{3,2,1,0:T(8,128)(2,1)S(1)} %bitcast.112), kind=kOutput, calls=%fused_computation.6 | convolution fusion | flops 6449528832 | bytes 18350080 | tf_op jit(solution)/shard_map/nkd,pnkh->pdh/dot_general | solution.py:124
  345.8 5.2 copy.89
  351.0 5.6 all-to-all-start.6
  356.7 6.6 %gather_fusion.3 = bf16[256,4096]{1,0:T(8,128)(2,1)S(1)} fusion(bf16[512,4096]{1,0:T(8,128)(2,1)} %bitcast.13, s32[1024]{0:T(1024)S(1)} %pad_clamp_fusion), kind=kCustom, calls=%fused_computation.3 | custom fusion | bytes 4195328 | tf_op jit(solution)/shard_map/gather | solution.py:118
  363.3 4.1 reshape.136
  367.5 7.5 %reduce_sum.78 = f32[128,4096]{1,0:T(8,128)S(1)} reduce(f32[128,2,4096]{2,1,0:T(2,128)} %reshape.136, f32[]{:T(128)} %constant.56.clone.1), dimensions={1}, to_apply=%region_6.7 | reduce | flops 524288 | bytes 6291460 | tf_op jit(solution)/shard_map/reduce_sum | solution.py:117
  375.0 1.4 fusion.17
  376.4 0.5 copy-done.2
  377.0 8.0 %multiply_reduce_fusion = bf16[128,4096]{1,0:T(8,128)(2,1)} fusion(bf16[128,2,4096]{2,1,0:T(2,128)(2,1)S(1)} %copy-done.2, f32[128,2]{1,0:T(8,128)S(1)} %copy-done.5), kind=kLoop, calls=%fused_computation.28 | loop fusion | flops 2621440 | bytes 3146752 | tf_op jit(solution)/shard_map/reduce_sum | solution.py:102
  385.0 0.7 multiply_reduce_fusion.1
  385.7 0.7 div.45
  386.4 1.3 copy.74
  387.7 185.6 %all-to-all-done.6 = bf16[2,8,512,768]{2,3,0,1:T(8,128)(2,1)} async-done(((bf16[2,8,512,768]{2,3,0,1:T(8,128)(2,1)}), bf16[2,8,512,768]{2,3,0,1:T(8,128)(2,1)}, u32[]{:S(2)}, u32[]{:S(2)}) %all-to-all-start.6) | async-done | bytes 12582944 | tf_op jit(solution)/shard_map/all_to_all | solution.py:69
  573.3 6.7 %convert_reduce_fusion = f32[2,512,768]{1,2,0:T(8,128)S(1)} fusion(bf16[2,8,512,768]{2,3,0,1:T(8,128)(2,1)} %all-to-all-done.6), kind=kLoop, calls=%fused_computation.7 | loop fusion | flops 11796480 | bytes 15728640 | tf_op jit(solution)/shard_map/reduce_sum | solution.py:70
  580.0 1.6 fusion.21
  581.6 2.3 copy.76
  583.8 2.3 copy.75
  586.1 2.1 fusion.27
  (64 shorter events, 1.0 us)
Async XLA Ops:
  7.2 18.0 %copy-start = (bf16[4096,16]{0,1:T(8,128)(2,1)S(1)}, bf16[4096,16]{0,1:T(8,128)(2,1)}, u32[]{:S(2)}) copy-start(bf16[4096,16]{0,1:T(8,128)(2,1)} %param.10) | copy-start | bytes 393220
  17.3 7.6 %copy-start.6 = (s32[128,2]{0,1:T(2,128)S(1)}, s32[128,2]{0,1:T(2,128)}, u32[]{:S(2)}) copy-start(s32[128,2]{0,1:T(2,128)} %param.9) | copy-start | bytes 3076
  17.3 7.9 %copy-start.1 = (bf16[128,4096]{1,0:T(8,128)(2,1)S(1)}, bf16[128,4096]{1,0:T(8,128)(2,1)}, u32[]{:S(2)}) copy-start(bf16[128,4096]{1,0:T(8,128)(2,1)} %param.7) | copy-start | bytes 3145732
  17.3 61.9 %all-to-all-start = ((bf16[16,32,4096]{2,1,0:T(8,128)(2,1)}), bf16[16,32,4096]{2,1,0:T(8,128)(2,1)}, u32[]{:S(2)}, u32[]{:S(2)}) async-start(bf16[16,32,4096]{2,1,0:T(8,128)(2,1)} %bitcast.99), calls=%async_computation | async-start | bytes 8388608 | tf_op jit(solution)/shard_map/all_to_all | solution.py:89
  25.6 2.5 copy-start.3
  27.9 10.3 %copy-start.4 = (f32[128,2]{1,0:T(8,128)}, f32[128,2]{1,0:T(8,128)S(1)}, u32[]{:S(2)}) copy-start(f32[128,2]{1,0:T(8,128)S(1)} %copy.64) | copy-start | bytes 3076
  79.2 19.8 %slice-start.2 = ((s8[6291456]{0:T(1024)(128)(4,1)}), s8[2097152]{0:T(1024)(128)(4,1)S(1)}, s32[]{:S(2)}) async-start(s8[6291456]{0:T(1024)(128)(4,1)} %bitcast.108), calls=%async_computation.11 | async-start | bytes 4194304
  79.2 66.7 %all-to-all-start.1 = ((bf16[16,32,4096]{2,1,0:T(8,128)(2,1)}), bf16[16,32,4096]{2,1,0:T(8,128)(2,1)}, u32[]{:S(2)}, u32[]{:S(2)}) async-start(bf16[16,32,4096]{2,1,0:T(8,128)(2,1)} %bitcast.100), calls=%async_computation.1 | async-start | bytes 8388608 | tf_op jit(solution)/shard_map/all_to_all | solution.py:95
  91.8 7.3 %slice-start.3 = ((s8[6291456]{0:T(1024)(128)(4,1)}), s8[4194304]{0:T(1024)(128)(4,1)S(1)}, s32[]{:S(2)}) async-start(s8[6291456]{0:T(1024)(128)(4,1)} %bitcast.108), calls=%async_computation.12 | async-start | bytes 8388608
  91.8 15.5 %slice-start = ((s8[6291456]{0:T(1024)(128)(4,1)}), s8[4194304]{0:T(1024)(128)(4,1)S(1)}, s32[]{:S(2)}) async-start(s8[6291456]{0:T(1024)(128)(4,1)} %bitcast.106), calls=%async_computation.9 | async-start | bytes 8388608
  99.0 7.4 %copy-start.10 = (f32[16,32,768]{2,1,0:T(8,128)}, f32[16,32,768]{2,1,0:T(8,128)S(1)}, u32[]{:S(2)}) copy-start(f32[16,32,768]{2,1,0:T(8,128)S(1)} %fusion.10) | copy-start | bytes 4718596
  99.1 8.3 %slice-start.1 = ((s8[6291456]{0:T(1024)(128)(4,1)}), s8[2097152]{0:T(1024)(128)(4,1)S(1)}, s32[]{:S(2)}) async-start(s8[6291456]{0:T(1024)(128)(4,1)} %bitcast.106), calls=%async_computation.10 | async-start | bytes 4194304
  106.4 0.9 copy-start.11
  146.0 22.8 %slice-start.4 = ((s8[6291456]{0:T(1024)(128)(4,1)}), s8[2097152]{0:T(1024)(128)(4,1)S(1)}, s32[]{:S(2)}) async-start(s8[6291456]{0:T(1024)(128)(4,1)} %bitcast.110), calls=%async_computation.13 | async-start | bytes 4194304
  146.0 66.5 %all-to-all-start.2 = ((bf16[16,32,4096]{2,1,0:T(8,128)(2,1)}), bf16[16,32,4096]{2,1,0:T(8,128)(2,1)}, u32[]{:S(2)}, u32[]{:S(2)}) async-start(bf16[16,32,4096]{2,1,0:T(8,128)(2,1)} %fusion.12), calls=%async_computation.2 | async-start | bytes 8388608 | tf_op jit(solution)/shard_map/all_to_all | solution.py:98
  158.3 10.5 %slice-start.5 = ((s8[6291456]{0:T(1024)(128)(4,1)}), s8[4194304]{0:T(1024)(128)(4,1)S(1)}, s32[]{:S(2)}) async-start(s8[6291456]{0:T(1024)(128)(4,1)} %bitcast.110), calls=%async_computation.14 | async-start | bytes 8388608
  167.9 0.9 copy-start.8
  233.4 25.7 %all-to-all-start.4 = ((f32[128,1,512]{2,1,0:T(1,128)}), f32[128,1,512]{2,1,0:T(1,128)S(1)}, u32[]{:S(2)}, u32[]{:S(2)}) async-start(f32[128,1,512]{2,1,0:T(1,128)} %all_to_all.33), calls=%async_computation.4 | async-start | bytes 524288 | tf_op jit(solution)/shard_map/all_to_all | solution.py:58
  259.1 7.4 %copy-start.12 = (bf16[16,32,768]{2,1,0:T(8,128)(2,1)S(1)}, bf16[16,32,768]{2,1,0:T(8,128)(2,1)}, u32[]{:S(2)}) copy-start(bf16[16,32,768]{2,1,0:T(8,128)(2,1)} %copy-done.11) | copy-start | bytes 2359300
  259.1 62.0 %all-to-all-start.3 = ((bf16[16,32,4096]{2,1,0:T(8,128)(2,1)}), bf16[16,32,4096]{2,1,0:T(8,128)(2,1)}, u32[]{:S(2)}, u32[]{:S(2)}) async-start(bf16[16,32,4096]{2,1,0:T(8,128)(2,1)} %add_convert_fusion), calls=%async_computation.3 | async-start | bytes 8388608 | tf_op jit(solution)/shard_map/all_to_all | solution.py:114
  266.5 319.6 %reduce-scatter.2.cloned.1.call-start = ((), (), s32[]{:S(2)}) async-start(), calls=%async_computation.8 | async-start | bytes 7077888 | tf_op jit(solution)/shard_map/reduce_scatter | solution.py:128
  274.9 61.7 %copy-start.7 = (bf16[16,32,768]{2,1,0:T(8,128)(2,1)S(1)}, bf16[16,32,768]{2,1,0:T(8,128)(2,1)}, u32[]{:S(2)}) copy-start(bf16[16,32,768]{2,1,0:T(8,128)(2,1)} %get-tuple-element.38) | copy-start | bytes 2359300
  274.9 61.7 %copy-start.9 = (bf16[16,32,768]{2,1,0:T(8,128)(2,1)S(1)}, bf16[16,32,768]{2,1,0:T(8,128)(2,1)}, u32[]{:S(2)}) copy-start(bf16[16,32,768]{2,1,0:T(8,128)(2,1)} %copy-done.8) | copy-start | bytes 2359300
  322.0 29.1 %all-to-all-start.5 = ((f32[128,1,512]{2,1,0:T(1,128)}), f32[128,1,512]{2,1,0:T(1,128)S(1)}, u32[]{:S(2)}, u32[]{:S(2)}) async-start(f32[128,1,512]{2,1,0:T(1,128)} %broadcast_in_dim.18), calls=%async_computation.5 | async-start | bytes 524288 | tf_op jit(solution)/shard_map/all_to_all | solution.py:60
  351.0 222.3 %all-to-all-start.6 = ((bf16[2,8,512,768]{2,3,0,1:T(8,128)(2,1)}), bf16[2,8,512,768]{2,3,0,1:T(8,128)(2,1)}, u32[]{:S(2)}, u32[]{:S(2)}) async-start(bf16[2,8,512,768]{2,3,0,1:T(8,128)(2,1)} %bitcast.98), calls=%async_computation.6 | async-start | bytes 25165824 | tf_op jit(solution)/shard_map/all_to_all | solution.py:69
  367.4 9.0 %copy-start.5 = (f32[128,2]{1,0:T(8,128)S(1)}, f32[128,2]{1,0:T(8,128)}, u32[]{:S(2)}) copy-start(f32[128,2]{1,0:T(8,128)} %copy-done.4) | copy-start | bytes 3076
  375.0 2.0 copy-start.2
Sparse Core Ops, SparseCore 0:
  275.1 238.7 reduce-scatter.1

commit v9 on v5

--- a/solution.py
+++ b/solution.py
@@ -67,7 +67,7 @@
     blocks = blocks.reshape((replica_count, rows) + blocks.shape[1:])
     blocks = blocks.reshape(replica_count, rows, len(parts), parts[0].shape[1])
     arrived = lax.all_to_all(blocks, axis, 0, 0, tiled=True)
-    total = jnp.sum(arrived.astype(jnp.float32), axis=0)
+    total = (jnp.sum(arrived.astype(jnp.float32), axis=0) / replica_count).astype(jnp.bfloat16)
     return tuple(total[:, i] for i in range(len(parts)))
 
 
@@ -128,8 +128,8 @@
         down_part.astype(jnp.bfloat16), "dp", scatter_dimension=0, tiled=True
     ).astype(jnp.float32)
     gate_total, up_total = reduce_scatter_by_exchange((gate_part, up_part), "dp")
-    gate_grad = (gate_total / replica_count).astype(jnp.bfloat16)[None]
-    up_grad = (up_total / replica_count).astype(jnp.bfloat16)[None]
+    gate_grad = gate_total[None]
+    up_grad = up_total[None]
     down_grad = (down_total / replica_count).astype(jnp.bfloat16)[None]
     return (output, d_tokens, router_grad, gate_grad, up_grad, down_grad)
 

time: 539 us -> 539 us (level)
  no operation moved by 1% of the time
where the time goes in v9:
time: 539 us; the launch traced here: 531 us
  waiting for transfers between devices  269 us (50%)
  matrix products  81.4 us (15%)
  starting transfers between devices  69.5 us (13%)
  local copies, waits for them, and re-layouts  55.7 us (10%)
  other arithmetic  40.5 us (8%)
  between operations  14.9 us (3%)
    all_to_all x1, waiting for transfers between devices, reduce_scatter_by_exchange(): arrived = lax.all_to_all(blocks, axis, 0, 0, tiled=True)  129 us
    all_to_all x1, waiting for transfers between devices, on_device(): lax.all_to_all(grad_in, 'expert', split_axis=0, concat_axis=0, tiled=True)  43.5 us
    all_to_all x1, waiting for transfers between devices, on_device(): lax.all_to_all(outbound, 'expert', split_axis=0, concat_axis=0, tiled=True)  33.7 us
    all_to_all x1, waiting for transfers between devices, on_device(): lax.all_to_all(grad_out, 'expert', split_axis=0, concat_axis=0, tiled=True)  33.6 us
    all_to_all x1, waiting for transfers between devices, on_device(): lax.all_to_all(expert_out, 'expert', split_axis=0, concat_axis=0, tiled=T...  29.3 us
    all_to_all x1, starting transfers between devices, all_reduce_by_exchange(): lax.all_to_all(chunks, axes, 0, 0, tiled=True)  15.4 us
    all_to_all x1, starting transfers between devices, on_device(): lax.all_to_all(grad_out, 'expert', split_axis=0, concat_axis=0, tiled=True)  12.6 us
    all_to_all x1, starting transfers between devices, on_device(): lax.all_to_all(expert_out, 'expert', split_axis=0, concat_axis=0, tiled=T...  11.8 us
  transfers between devices with their start and end apart: 8, of which 5 were waited for; matrix products, arithmetic and copies ran while one was open for 30% of the time, Pallas kernels for 0%

profile of v9, /device:TPU:4, one launch (start us, length us, event | category | flops | bytes accessed | tf_op | source)
XLA Modules:
  0.0 530.8 jit_solution(12566835490496696481)
XLA Ops:
  7.2 0.7 broadcast_multiply_fusion
  7.9 0.8 copy.62
  8.7 0.1 eq.42
  8.8 0.1 eq.38
  9.1 0.1 mul.95
  9.2 0.6 reduce-window.6
  9.8 0.2 slice_reduce_fusion
  10.2 1.4 scatter_custom_fusion
  11.6 1.3 concatenate.7
  12.9 4.4 gather_fusion
  17.3 7.6 %all-to-all-start = ((bf16[16,32,4096]{2,1,0:T(8,128)(2,1)}), bf16[16,32,4096]{2,1,0:T(8,128)(2,1)}, u32[]{:S(2)}, u32[]{:S(2)}) async-start(bf16[16,32,4096]{2,1,0:T(8,128)(2,1)} %bitcast.103), calls=%async_computation | async-start | bytes 8388608 | tf_op jit(solution)/shard_map/all_to_all | solution.py:90
  25.0 0.1 reshape.170
  25.2 0.4 fusion.35
  25.6 2.0 gather_fusion.4
  28.1 4.1 mul.101
  32.2 6.0 %mul.102 = f32[256,4096]{1,0:T(8,128)} reshape(f32[128,2,4096]{2,1,0:T(2,128)} %mul.101) | data formatting | bytes 8388608 | tf_op jit(solution)/shard_map/mul | solution.py:91
  38.2 2.6 multiply_convert_fusion
  40.9 0.3 concatenate.8
  41.1 4.4 gather_fusion.1
  45.6 33.7 %all-to-all-done = bf16[16,32,4096]{2,1,0:T(8,128)(2,1)} async-done(((bf16[16,32,4096]{2,1,0:T(8,128)(2,1)}), bf16[16,32,4096]{2,1,0:T(8,128)(2,1)}, u32[]{:S(2)}, u32[]{:S(2)}) %all-to-all-start) | async-done | bytes 4194336 | tf_op jit(solution)/shard_map/all_to_all | solution.py:90
  79.2 12.6 %all-to-all-start.1 = ((bf16[16,32,4096]{2,1,0:T(8,128)(2,1)}), bf16[16,32,4096]{2,1,0:T(8,128)(2,1)}, u32[]{:S(2)}, u32[]{:S(2)}) async-start(bf16[16,32,4096]{2,1,0:T(8,128)(2,1)} %bitcast.104), calls=%async_computation.1 | async-start | bytes 8388608 | tf_op jit(solution)/shard_map/all_to_all | solution.py:96
  91.8 7.2 %fusion.10 = f32[16,32,768]{2,1,0:T(8,128)S(1)} fusion(bf16[16,32,4096]{2,1,0:T(8,128)(2,1)} %all-to-all-done, bf16[1,4096,768]{2,1,0:T(8,128)(2,1)} %param.11), kind=kOutput, calls=%fused_computation.22 | convolution fusion | flops 3221225472 | bytes 12058624 | tf_op jit(solution)/shard_map/...d,dh->...h/dot_general | solution.py:31
  99.1 7.4 %multiply_convert_fusion.5 = (bf16[16,32,768]{2,1,0:T(8,128)(2,1)S(1)}, f32[16,32,768]{2,1,0:T(8,128)}) fusion(f32[16,32,768]{2,1,0:T(8,128)S(1)} %fusion.10, bf16[16,32,4096]{2,1,0:T(8,128)(2,1)} %all-to-all-done, bf16[1,4096,768]{2,1,0:T(8,128)(2,1)S(1)} %bitcast.114), kind=kOutput, calls=%fused_computation.36 | convolution fusion | flops 3223584768 | bytes 14417920 | tf_op jit(solution)/shard_map/...d,dh->...h/dot_general | solution.py:32
  106.5 0.9 copy-done.11
  107.4 5.0 fusion.12
  112.4 33.6 %all-to-all-done.1 = bf16[16,32,4096]{2,1,0:T(8,128)(2,1)} async-done(((bf16[16,32,4096]{2,1,0:T(8,128)(2,1)}), bf16[16,32,4096]{2,1,0:T(8,128)(2,1)}, u32[]{:S(2)}, u32[]{:S(2)}) %all-to-all-start.1) | async-done | bytes 4194336 | tf_op jit(solution)/shard_map/all_to_all | solution.py:96
  146.0 11.8 %all-to-all-start.2 = ((bf16[16,32,4096]{2,1,0:T(8,128)(2,1)}), bf16[16,32,4096]{2,1,0:T(8,128)(2,1)}, u32[]{:S(2)}, u32[]{:S(2)}) async-start(bf16[16,32,4096]{2,1,0:T(8,128)(2,1)} %fusion.12), calls=%async_computation.2 | async-start | bytes 8388608 | tf_op jit(solution)/shard_map/all_to_all | solution.py:99
  157.8 0.3 reduce-scatter.2.cloned.1.call-start
  158.1 8.4 %bitcast_convert_fusion = bf16[4096,768]{1,0:T(8,128)(2,1)} fusion(bf16[16,32,4096]{2,1,0:T(8,128)(2,1)} %all-to-all-done.1, bf16[16,32,768]{2,1,0:T(8,128)(2,1)S(1)} %copy-done.12), kind=kOutput, calls=%fused_computation.8 | convolution fusion | flops 3224371200 | bytes 11272192 | tf_op jit(solution)/shard_map/nkd,nkh->dh/dot_general | solution.py:126
  166.5 9.6 %multiply_convert_fusion.4 = (bf16[16,32,768]{2,1,0:T(8,128)(2,1)}, bf16[16,32,768]{2,1,0:T(8,128)(2,1)S(1)}) fusion(f32[16,32,768]{2,1,0:T(8,128)} %copy-done.10, f32[16,32,768]{2,1,0:T(8,128)} %get-tuple-element.43, bf16[16,32,4096]{2,1,0:T(8,128)(2,1)} %all-to-all-done.1, bf16[1,4096,768]{2,1,0:T(8,128)(2,1)} %param.13), kind=kOutput, calls=%fused_computation.35 | convolution fusion | flops 3226337280 | bytes 15204352 | tf_op jit(solution)/shard_map/...d,dh->...h/dot_general | solution.py:42
  176.2 0.9 copy-done.8
  177.0 6.2 %fusion.4 = f32[16,32,4096]{2,1,0:T(8,128)} fusion(bf16[16,32,768]{2,1,0:T(8,128)(2,1)S(1)} %get-tuple-element.37, bf16[1,4096,768]{2,1,0:T(8,128)(2,1)S(1)} %bitcast.116), kind=kOutput, calls=%fused_computation.16 | convolution fusion | flops 3221225472 | bytes 15466496 | tf_op jit(solution)/shard_map/...h,dh->...d/dot_general | solution.py:49
  183.2 29.3 %all-to-all-done.2 = bf16[16,32,4096]{2,1,0:T(8,128)(2,1)} async-done(((bf16[16,32,4096]{2,1,0:T(8,128)(2,1)}), bf16[16,32,4096]{2,1,0:T(8,128)(2,1)}, u32[]{:S(2)}, u32[]{:S(2)}) %all-to-all-start.2) | async-done | bytes 4194336 | tf_op jit(solution)/shard_map/all_to_all | solution.py:99
  212.5 6.6 %gather_fusion.2 = bf16[256,4096]{1,0:T(8,128)(2,1)S(1)} fusion(bf16[512,4096]{1,0:T(8,128)(2,1)} %bitcast.12, s32[1024]{0:T(1024)S(1)} %pad_clamp_fusion), kind=kCustom, calls=%fused_computation.2 | custom fusion | bytes 4195328 | tf_op jit(solution)/shard_map/gather | solution.py:102
  219.1 2.7 reshape.135
  221.8 7.3 %fusion.18 = f32[128,1,2]{2,1,0:T(1,128)S(1)} fusion(bf16[128,2,4096]{2,1,0:T(2,128)(2,1)} %reshape.135, bf16[128,4096,1]{1,0,2:T(8,128)(2,1)} %bitcast.107), kind=kOutput, calls=%fused_computation.31 | convolution fusion | flops 2097152 | bytes 3146752 | tf_op jit(solution)/shard_map/td,tkd->tk/dot_general | solution.py:106
  229.2 1.0 convolution_bitcast_fusion
  230.2 1.5 copy.66
  231.8 1.5 all_to_all.33
  233.2 15.4 %all-to-all-start.4 = ((f32[128,1,512]{2,1,0:T(1,128)}), f32[128,1,512]{2,1,0:T(1,128)S(1)}, u32[]{:S(2)}, u32[]{:S(2)}) async-start(f32[128,1,512]{2,1,0:T(1,128)} %all_to_all.33), calls=%async_computation.4 | async-start | bytes 524288 | tf_op jit(solution)/shard_map/all_to_all | solution.py:58
  248.7 10.8 %add_convert_fusion = bf16[16,32,4096]{2,1,0:T(8,128)(2,1)} fusion(f32[16,32,4096]{2,1,0:T(8,128)} %fusion.4, bf16[16,32,768]{2,1,0:T(8,128)(2,1)} %get-tuple-element.36, bf16[1,4096,768]{2,1,0:T(8,128)(2,1)} %param.11), kind=kOutput, calls=%fused_computation.11 | convolution fusion | flops 3225419776 | bytes 19660800 | tf_op jit(solution)/shard_map/...h,dh->...d/dot_general | solution.py:48
  259.5 7.4 %all-to-all-start.3 = ((bf16[16,32,4096]{2,1,0:T(8,128)(2,1)}), bf16[16,32,4096]{2,1,0:T(8,128)(2,1)}, u32[]{:S(2)}, u32[]{:S(2)}) async-start(bf16[16,32,4096]{2,1,0:T(8,128)(2,1)} %add_convert_fusion), calls=%async_computation.3 | async-start | bytes 8388608 | tf_op jit(solution)/shard_map/all_to_all | solution.py:115
  266.9 8.4 %bitcast_convert_fusion.2 = bf16[4096,768]{1,0:T(8,128)(2,1)} fusion(bf16[16,32,4096]{2,1,0:T(8,128)(2,1)} %all-to-all-done, bf16[16,32,768]{2,1,0:T(8,128)(2,1)S(1)} %copy-done.7), kind=kOutput, calls=%fused_computation.10 | convolution fusion | flops 3224371200 | bytes 11272192 | tf_op jit(solution)/shard_map/nkd,nkh->dh/dot_general | solution.py:124
  275.4 8.3 %bitcast_convert_fusion.1 = bf16[4096,768]{1,0:T(8,128)(2,1)} fusion(bf16[16,32,4096]{2,1,0:T(8,128)(2,1)} %all-to-all-done, bf16[16,32,768]{2,1,0:T(8,128)(2,1)S(1)} %copy-done.9), kind=kOutput, calls=%fused_computation.9 | convolution fusion | flops 3224371200 | bytes 11272192 | tf_op jit(solution)/shard_map/nkd,nkh->dh/dot_general | solution.py:125
  283.7 0.2 reduce_sum.81
  283.9 43.5 %all-to-all-done.3 = bf16[16,32,4096]{2,1,0:T(8,128)(2,1)} async-done(((bf16[16,32,4096]{2,1,0:T(8,128)(2,1)}), bf16[16,32,4096]{2,1,0:T(8,128)(2,1)}, u32[]{:S(2)}, u32[]{:S(2)}) %all-to-all-start.3) | async-done | bytes 4194336 | tf_op jit(solution)/shard_map/all_to_all | solution.py:115
  327.3 0.8 broadcast_in_dim.18
  328.2 8.8 %all-to-all-start.5 = ((f32[128,1,512]{2,1,0:T(1,128)}), f32[128,1,512]{2,1,0:T(1,128)S(1)}, u32[]{:S(2)}, u32[]{:S(2)}) async-start(f32[128,1,512]{2,1,0:T(1,128)} %broadcast_in_dim.18), calls=%async_computation.5 | async-start | bytes 524288 | tf_op jit(solution)/shard_map/all_to_all | solution.py:60
  336.9 10.8 %pad_maximum_fusion = bf16[8,512,2,768]{3,1,2,0:T(8,128)(2,1)} fusion(bf16[8,512,1,768]{3,1,2,0:T(8,128)(2,1)} %bitcast.106, bf16[8,512,1,768]{3,1,2,0:T(8,128)(2,1)} %bitcast.105), kind=kLoop, calls=%fused_computation.7 | loop fusion | flops 6291456 | bytes 25165824 | tf_op jit(solution)/shard_map/stack | solution.py:66
  347.7 5.7 %all-to-all-start.6 = ((bf16[8,512,2,768]{3,1,2,0:T(8,128)(2,1)}), bf16[8,512,2,768]{3,1,2,0:T(8,128)(2,1)}, u32[]{:S(2)}, u32[]{:S(2)}) async-start(bf16[8,512,2,768]{3,1,2,0:T(8,128)(2,1)} %pad_maximum_fusion), calls=%async_computation.6 | async-start | bytes 25165824 | tf_op jit(solution)/shard_map/all_to_all | solution.py:69
  353.4 6.7 %gather_fusion.3 = bf16[256,4096]{1,0:T(8,128)(2,1)S(1)} fusion(bf16[512,4096]{1,0:T(8,128)(2,1)} %bitcast.13, s32[1024]{0:T(1024)S(1)} %pad_clamp_fusion), kind=kCustom, calls=%fused_computation.3 | custom fusion | bytes 4195328 | tf_op jit(solution)/shard_map/gather | solution.py:119
  360.1 4.2 reshape.137
  364.3 7.5 %reduce_sum.78 = f32[128,4096]{1,0:T(8,128)S(1)} reduce(f32[128,2,4096]{2,1,0:T(2,128)} %reshape.137, f32[]{:T(128)} %constant.56.clone.1), dimensions={1}, to_apply=%region_6.7 | reduce | flops 524288 | bytes 6291460 | tf_op jit(solution)/shard_map/reduce_sum | solution.py:118
  371.8 1.4 fusion.17
  373.2 0.5 copy-done.2
  373.8 8.0 %multiply_reduce_fusion = bf16[128,4096]{1,0:T(8,128)(2,1)} fusion(bf16[128,2,4096]{2,1,0:T(2,128)(2,1)S(1)} %copy-done.2, f32[128,2]{1,0:T(8,128)S(1)} %copy-done.5), kind=kLoop, calls=%fused_computation.28 | loop fusion | flops 2621440 | bytes 3146752 | tf_op jit(solution)/shard_map/reduce_sum | solution.py:103
  381.8 0.7 multiply_reduce_fusion.1
  382.5 0.7 div.48
  383.2 1.3 copy.70
  384.5 128.7 %all-to-all-done.6 = bf16[8,512,2,768]{3,1,2,0:T(8,128)(2,1)} async-done(((bf16[8,512,2,768]{3,1,2,0:T(8,128)(2,1)}), bf16[8,512,2,768]{3,1,2,0:T(8,128)(2,1)}, u32[]{:S(2)}, u32[]{:S(2)}) %all-to-all-start.6) | async-done | bytes 12582944 | tf_op jit(solution)/shard_map/all_to_all | solution.py:69
  513.2 6.6 %convert_reduce_fusion = f32[512,2,768]{2,0,1:T(8,128)S(1)} fusion(bf16[8,512,2,768]{3,1,2,0:T(8,128)(2,1)} %all-to-all-done.6), kind=kLoop, calls=%fused_computation.6 | loop fusion | flops 11796480 | bytes 15728640 | tf_op jit(solution)/shard_map/reduce_sum | solution.py:70
  519.8 0.2 multiply_convert_fusion.1
  520.1 1.2 slice_bitcast_fusion
  521.3 2.1 fusion.21
  (64 shorter events, 1.1 us)
Async XLA Ops:
  7.2 18.0 %copy-start = (bf16[4096,16]{0,1:T(8,128)(2,1)S(1)}, bf16[4096,16]{0,1:T(8,128)(2,1)}, u32[]{:S(2)}) copy-start(bf16[4096,16]{0,1:T(8,128)(2,1)} %param.10) | copy-start | bytes 393220
  17.3 7.6 %copy-start.6 = (s32[128,2]{0,1:T(2,128)S(1)}, s32[128,2]{0,1:T(2,128)}, u32[]{:S(2)}) copy-start(s32[128,2]{0,1:T(2,128)} %param.9) | copy-start | bytes 3076
  17.3 7.9 %copy-start.1 = (bf16[128,4096]{1,0:T(8,128)(2,1)S(1)}, bf16[128,4096]{1,0:T(8,128)(2,1)}, u32[]{:S(2)}) copy-start(bf16[128,4096]{1,0:T(8,128)(2,1)} %param.7) | copy-start | bytes 3145732
  17.3 61.9 %all-to-all-start = ((bf16[16,32,4096]{2,1,0:T(8,128)(2,1)}), bf16[16,32,4096]{2,1,0:T(8,128)(2,1)}, u32[]{:S(2)}, u32[]{:S(2)}) async-start(bf16[16,32,4096]{2,1,0:T(8,128)(2,1)} %bitcast.103), calls=%async_computation | async-start | bytes 8388608 | tf_op jit(solution)/shard_map/all_to_all | solution.py:90
  25.6 2.5 copy-start.3
  27.9 10.3 %copy-start.4 = (f32[128,2]{1,0:T(8,128)}, f32[128,2]{1,0:T(8,128)S(1)}, u32[]{:S(2)}) copy-start(f32[128,2]{1,0:T(8,128)S(1)} %copy.60) | copy-start | bytes 3076
  79.2 19.9 %slice-start.2 = ((s8[6291456]{0:T(1024)(128)(4,1)}), s8[2097152]{0:T(1024)(128)(4,1)S(1)}, s32[]{:S(2)}) async-start(s8[6291456]{0:T(1024)(128)(4,1)} %bitcast.113), calls=%async_computation.11 | async-start | bytes 4194304
  79.2 66.8 %all-to-all-start.1 = ((bf16[16,32,4096]{2,1,0:T(8,128)(2,1)}), bf16[16,32,4096]{2,1,0:T(8,128)(2,1)}, u32[]{:S(2)}, u32[]{:S(2)}) async-start(bf16[16,32,4096]{2,1,0:T(8,128)(2,1)} %bitcast.104), calls=%async_computation.1 | async-start | bytes 8388608 | tf_op jit(solution)/shard_map/all_to_all | solution.py:96
  91.8 7.3 %slice-start.3 = ((s8[6291456]{0:T(1024)(128)(4,1)}), s8[4194304]{0:T(1024)(128)(4,1)S(1)}, s32[]{:S(2)}) async-start(s8[6291456]{0:T(1024)(128)(4,1)} %bitcast.113), calls=%async_computation.12 | async-start | bytes 8388608
  91.8 15.6 %slice-start = ((s8[6291456]{0:T(1024)(128)(4,1)}), s8[4194304]{0:T(1024)(128)(4,1)S(1)}, s32[]{:S(2)}) async-start(s8[6291456]{0:T(1024)(128)(4,1)} %bitcast.111), calls=%async_computation.9 | async-start | bytes 8388608
  99.1 7.4 %copy-start.10 = (f32[16,32,768]{2,1,0:T(8,128)}, f32[16,32,768]{2,1,0:T(8,128)S(1)}, u32[]{:S(2)}) copy-start(f32[16,32,768]{2,1,0:T(8,128)S(1)} %fusion.10) | copy-start | bytes 4718596
  99.1 8.3 %slice-start.1 = ((s8[6291456]{0:T(1024)(128)(4,1)}), s8[2097152]{0:T(1024)(128)(4,1)S(1)}, s32[]{:S(2)}) async-start(s8[6291456]{0:T(1024)(128)(4,1)} %bitcast.111), calls=%async_computation.10 | async-start | bytes 4194304
  106.5 0.9 copy-start.11
  112.4 45.7 %copy-start.12 = (bf16[16,32,768]{2,1,0:T(8,128)(2,1)S(1)}, bf16[16,32,768]{2,1,0:T(8,128)(2,1)}, u32[]{:S(2)}) copy-start(bf16[16,32,768]{2,1,0:T(8,128)(2,1)} %copy-done.11) | copy-start | bytes 2359300
  146.0 66.4 %all-to-all-start.2 = ((bf16[16,32,4096]{2,1,0:T(8,128)(2,1)}), bf16[16,32,4096]{2,1,0:T(8,128)(2,1)}, u32[]{:S(2)}, u32[]{:S(2)}) async-start(bf16[16,32,4096]{2,1,0:T(8,128)(2,1)} %fusion.12), calls=%async_computation.2 | async-start | bytes 8388608 | tf_op jit(solution)/shard_map/all_to_all | solution.py:99
  157.8 363.5 %reduce-scatter.2.cloned.1.call-start = ((), (), s32[]{:S(2)}) async-start(), calls=%async_computation.8 | async-start | bytes 7077888 | tf_op jit(solution)/shard_map/reduce_scatter | solution.py:127
  166.5 10.6 %slice-start.4 = ((s8[6291456]{0:T(1024)(128)(4,1)}), s8[2097152]{0:T(1024)(128)(4,1)S(1)}, s32[]{:S(2)}) async-start(s8[6291456]{0:T(1024)(128)(4,1)} %bitcast.115), calls=%async_computation.13 | async-start | bytes 4194304
  166.5 10.5 %slice-start.5 = ((s8[6291456]{0:T(1024)(128)(4,1)}), s8[4194304]{0:T(1024)(128)(4,1)S(1)}, s32[]{:S(2)}) async-start(s8[6291456]{0:T(1024)(128)(4,1)} %bitcast.115), calls=%async_computation.14 | async-start | bytes 8388608
  176.2 0.9 copy-start.8
  233.2 26.3 %all-to-all-start.4 = ((f32[128,1,512]{2,1,0:T(1,128)}), f32[128,1,512]{2,1,0:T(1,128)S(1)}, u32[]{:S(2)}, u32[]{:S(2)}) async-start(f32[128,1,512]{2,1,0:T(1,128)} %all_to_all.33), calls=%async_computation.4 | async-start | bytes 524288 | tf_op jit(solution)/shard_map/all_to_all | solution.py:58
  259.5 7.4 %copy-start.7 = (bf16[16,32,768]{2,1,0:T(8,128)(2,1)S(1)}, bf16[16,32,768]{2,1,0:T(8,128)(2,1)}, u32[]{:S(2)}) copy-start(bf16[16,32,768]{2,1,0:T(8,128)(2,1)} %get-tuple-element.36) | copy-start | bytes 2359300
  259.5 67.8 %all-to-all-start.3 = ((bf16[16,32,4096]{2,1,0:T(8,128)(2,1)}), bf16[16,32,4096]{2,1,0:T(8,128)(2,1)}, u32[]{:S(2)}, u32[]{:S(2)}) async-start(bf16[16,32,4096]{2,1,0:T(8,128)(2,1)} %add_convert_fusion), calls=%async_computation.3 | async-start | bytes 8388608 | tf_op jit(solution)/shard_map/all_to_all | solution.py:115
  266.9 8.4 %copy-start.9 = (bf16[16,32,768]{2,1,0:T(8,128)(2,1)S(1)}, bf16[16,32,768]{2,1,0:T(8,128)(2,1)}, u32[]{:S(2)}) copy-start(bf16[16,32,768]{2,1,0:T(8,128)(2,1)} %copy-done.8) | copy-start | bytes 2359300
  328.2 19.6 %all-to-all-start.5 = ((f32[128,1,512]{2,1,0:T(1,128)}), f32[128,1,512]{2,1,0:T(1,128)S(1)}, u32[]{:S(2)}, u32[]{:S(2)}) async-start(f32[128,1,512]{2,1,0:T(1,128)} %broadcast_in_dim.18), calls=%async_computation.5 | async-start | bytes 524288 | tf_op jit(solution)/shard_map/all_to_all | solution.py:60
  347.7 165.5 %all-to-all-start.6 = ((bf16[8,512,2,768]{3,1,2,0:T(8,128)(2,1)}), bf16[8,512,2,768]{3,1,2,0:T(8,128)(2,1)}, u32[]{:S(2)}, u32[]{:S(2)}) async-start(bf16[8,512,2,768]{3,1,2,0:T(8,128)(2,1)} %pad_maximum_fusion), calls=%async_computation.6 | async-start | bytes 25165824 | tf_op jit(solution)/shard_map/all_to_all | solution.py:69
  364.3 9.0 %copy-start.5 = (f32[128,2]{1,0:T(8,128)S(1)}, f32[128,2]{1,0:T(8,128)}, u32[]{:S(2)}) copy-start(f32[128,2]{1,0:T(8,128)} %copy-done.4) | copy-start | bytes 3076
  371.8 2.0 copy-start.2
Sparse Core Ops, SparseCore 0:
  166.6 230.1 reduce-scatter.1
